TPU v7x, 32 devices: a whole 2x2x4 slice. The times are simulated.
32 devices in a mesh: row: 8 (over y, x, core), col: 4 (over z).
Axes of the slice: x: 2, y: 2, z: 4, core: 2. Of those that a mesh axis runs over, the one named last changes fastest.
Arguments:
- a_panels: bfloat16 [16384, 1024], P('row', 'col'), may hold values from -6 to 6
- a_mask: int32 [128, 8], P('row', 'col'), may hold values 0 or 1
- b_panels: bfloat16 [1024, 4096], P('row', 'col'), may hold values from -0.1875 to 0.1875
- b_mask: int32 [8, 32], P('row', 'col'), may hold values 0 or 1
- owner_map: int32 [128, 1], P('row'), may hold values from 0 to 7; in each aligned block of 16 rows (0 to 15, 16 to 31, ...) at most 2 rows name the same one
Outputs:
- owned: bfloat16 [16384, 4096], P('row', 'col')
Inputs may be any that keep to these rules, and one draw needn't show every extreme that they name: `owner_map`: within each aligned block of 16 tile rows (the tile rows of one grid row) no owner is named more than 2 times, a bound that some block reaches.
All inputs are finite; a program needn't handle non-finite values. No bound on the sum of `a_mask` or of `b_mask` on one device may be relied on, other than what follows from the above.
Results may differ from a plain program's by a relative error of at most 0.001.
Values may be sent and summed in bfloat16 or wider, within the bound.
No kernel may reach another device: no remote copies, remote signals or barrier semaphores. Data moves between devices by JAX's collectives and lax.ppermute only.
A program may use at most 128 MiB of HBM per device.

v0:
```python
import jax
import jax.numpy as jnp
from jax import lax
from jax.sharding import PartitionSpec as P

SLOTS = 2


def from_behind(value, axis, steps):
    count = lax.axis_size(axis)
    pairs = [(source, (source + steps) % count) for source in range(count)]
    return lax.ppermute(value, axis, pairs)


def masked_a(panel, mask):
    tile_rows = mask.shape[0]
    inner = mask.shape[1]
    tiles = panel.reshape(tile_rows, panel.shape[0] // tile_rows, inner, panel.shape[1] // inner)
    return (tiles * mask.astype(jnp.bfloat16)[:, None, :, None]).reshape(panel.shape)


def masked_b(panel, mask):
    inner = mask.shape[0]
    tile_cols = mask.shape[1]
    tiles = panel.reshape(inner, panel.shape[0] // inner, tile_cols, panel.shape[1] // tile_cols)
    return (tiles * mask.astype(jnp.bfloat16)[:, None, :, None]).reshape(panel.shape)


def product(panel_a, mask_a, panel_b, mask_b):
    return jnp.dot(
        masked_a(panel_a, mask_a), masked_b(panel_b, mask_b), preferred_element_type=jnp.float32
    )


def on_device(a_panels, a_mask, b_panels, b_mask, owner_map):
    tile = b_panels.shape[0]
    depth = lax.axis_size("col")
    grid_rows = lax.axis_size("row")
    fold = grid_rows // depth
    row_id = lax.axis_index("row")
    col_id = lax.axis_index("col")
    panel_b, mask_b = (b_panels, b_mask)
    target = fold * col_id
    for bit in range((grid_rows - 1).bit_length()):
        moved_b, moved_bm = from_behind((panel_b, mask_b), "row", -(1 << bit))
        take = target >> bit & 1 == 1
        panel_b = jnp.where(take, moved_b, panel_b)
        mask_b = jnp.where(take, moved_bm, mask_b)
    total = jnp.zeros((a_panels.shape[0], b_panels.shape[1]), jnp.float32)
    panel_a, mask_a = (a_panels, a_mask)
    whole_shift = row_id // fold
    remain = row_id % fold
    for bit in range((depth - 1).bit_length()):
        moved_a, moved_am = from_behind((panel_a, mask_a), "col", -(1 << bit))
        take = whole_shift >> bit & 1 == 1
        panel_a = jnp.where(take, moved_a, panel_a)
        mask_a = jnp.where(take, moved_am, mask_a)
    after_a, after_am = from_behind((panel_a, mask_a), "col", -1)
    joined = jnp.concatenate([panel_a, after_a], axis=1)
    joined_m = jnp.concatenate([mask_a, after_am], axis=1)
    panel_a = lax.dynamic_slice_in_dim(joined, remain * tile, fold * tile, 1)
    mask_a = lax.dynamic_slice_in_dim(joined_m, remain, fold, 1)

    def advance(step, carry):
        acc, cur_a, cur_am, cur_b, cur_bm = carry
        acc = acc + product(cur_a[:, :tile], cur_am[:, :1], cur_b, cur_bm)
        head_a, head_m = from_behind((cur_a[:, :tile], cur_am[:, :1]), "col", -1)
        cur_a = jnp.concatenate([cur_a[:, tile:], head_a], axis=1)
        cur_am = jnp.concatenate([cur_am[:, 1:], head_m], axis=1)
        cur_b, cur_bm = from_behind((cur_b, cur_bm), "row", -1)
        return (acc, cur_a, cur_am, cur_b, cur_bm)

    total, panel_a, mask_a, panel_b, mask_b = lax.fori_loop(
        0, grid_rows - 1, advance, (total, panel_a, mask_a, panel_b, mask_b)
    )
    total = total + product(panel_a[:, :tile], mask_a[:, :1], panel_b, mask_b)
    result = total.astype(jnp.bfloat16)
    owners = owner_map[:, 0]
    tile_rows = owners.shape[0]
    same = owners[:, None] == owners[None, :]
    earlier = (
        jnp.arange(tile_rows, dtype=jnp.int32)[None, :]
        < jnp.arange(tile_rows, dtype=jnp.int32)[:, None]
    )
    rank = jnp.sum(jnp.where(same & earlier, 1, 0).astype(jnp.int32), axis=1)
    slot_id = owners * SLOTS + rank
    select = (jnp.arange(grid_rows * SLOTS, dtype=jnp.int32)[:, None] == slot_id[None, :]).astype(
        jnp.bfloat16
    )
    packed = jnp.dot(
        select, result.reshape(tile_rows, -1), preferred_element_type=jnp.float32
    ).astype(jnp.bfloat16)
    packed = packed.reshape(grid_rows, SLOTS * tile, result.shape[1])
    arrived = lax.all_to_all(packed, "row", split_axis=0, concat_axis=0, tiled=True)
    return arrived.reshape(-1, result.shape[1])


def solution(mesh):
    placed = (P("row", "col"), P("row", "col"), P("row", "col"), P("row", "col"), P("row", None))
    return jax.shard_map(
        on_device, mesh=mesh, in_specs=placed, out_specs=P("row", "col"), check_vma=False
    )
```

profile of v0, /device:TPU:0, one launch (start us, length us, event | category | flops | bytes accessed | tf_op | source)
XLA Modules:
  0.0 282.8 jit_solution(3299915901711081954)
XLA Ops:
  0.0 5.0 %collective-permute-start.4 = (bf16[2048,256]{1,0:T(8,128)(2,1)}, bf16[2048,256]{1,0:T(8,128)(2,1)S(1)}, u32[]{:S(2)}, u32[]{:S(2)}) collective-permute-start(bf16[2048,256]{1,0:T(8,128)(2,1)} %param.7), channel_id=1, source_target_pairs={{0,3},{1,0},{2,1},{3,2},{4,7},{5,4},{6,5},{7,6},{8,11},{9,8},{10,9... | collective-permute-start | bytes 3145736 | tf_op jit(solution)/shard_map/ppermute | solution.py:12
  5.0 0.4 collective-permute-start.7
  5.5 1.3 collective-permute-start.10
  6.8 1.2 collective-permute-start.13
  8.1 0.9 select_reduce_fusion
  9.0 18.8 %collective-permute-done.4 = bf16[2048,256]{1,0:T(8,128)(2,1)S(1)} collective-permute-done((bf16[2048,256]{1,0:T(8,128)(2,1)}, bf16[2048,256]{1,0:T(8,128)(2,1)S(1)}, u32[]{:S(2)}, u32[]{:S(2)}) %collective-permute-start.4) | collective-permute-done | bytes 1048608 | tf_op jit(solution)/shard_map/ppermute | solution.py:12
  27.8 1.3 broadcast_select_fusion
  29.1 1.4 collective-permute-start.5
  30.6 0.7 multiply_add_fusion
  31.2 0.7 broadcast_select_fusion.5
  31.9 1.2 collective-permute-start.14
  33.1 2.3 collective-permute-done.14
  35.4 1.5 collective-permute-start.15
  37.0 0.7 broadcast_select_fusion.8
  37.6 1.6 collective-permute-start.8
  39.2 1.0 broadcast_select_fusion.2
  40.2 0.6 collective-permute-start.11
  40.7 35.9 %collective-permute-done.5 = bf16[2048,256]{1,0:T(8,128)(2,1)S(1)} collective-permute-done((bf16[2048,256]{1,0:T(8,128)(2,1)S(1)}, bf16[2048,256]{1,0:T(8,128)(2,1)S(1)}, u32[]{:S(2)}, u32[]{:S(2)}) %collective-permute-start.5) | collective-permute-done | bytes 1048608 | tf_op jit(solution)/shard_map/ppermute | solution.py:12
  76.6 0.1 broadcast_select_fusion.1
  76.7 2.3 collective-permute-start.6
  79.1 0.1 collective-permute-start.9
  79.2 1.6 collective-permute-start.12
  80.8 20.9 %collective-permute-done.9 = s32[16,2]{0,1:T(2,128)S(1)} collective-permute-done((s32[16,2]{0,1:T(2,128)S(1)}, s32[16,2]{0,1:T(2,128)S(1)}, u32[]{:S(2)}, u32[]{:S(2)}) %collective-permute-start.9) | collective-permute-done | bytes 160 | tf_op jit(solution)/shard_map/ppermute | solution.py:12
  101.8 0.4 fusion.5
  102.2 96.9 %while.19 = (s32[]{:T(128)}, f32[2048,1024]{1,0:T(8,128)}, bf16[2048,256]{1,0:T(8,128)(2,1)S(1)}, s32[16,2]{0,1:T(2,128)S(1)}, bf16[128,1024]{1,0:T(8,128)(2,1)S...) while((s32[]{:T(128)}, f32[2048,1024]{1,0:T(8,128)}, bf16[2048,256]{1,0:T(8,128)(2,1)S(1)}, ...), condition=%wide.region_2.3_spmd.clone, body=%wide.region_1.2_spmd.clone.sunk | while | flops 543555584 | bytes 25441596 | solution.py:73
  102.2 4.4 %collective-permute-start = (bf16[2048,128]{1,0:T(8,128)(2,1)S(1)}, bf16[2048,128]{1,0:T(8,128)(2,1)S(1)}, u32[]{:S(2)}, u32[]{:S(2)}) collective-permute-start(bf16[2048,128]{1,0:T(8,128)(2,1)S(1)} %get-tuple-element.127), channel_id=1, source_target_pairs={{0,3},{1,0},{2,1},{3,2},{4,7},{5,4},{6,5},{7,6},{8,11},{9,8},{10,9... | collective-permute-start | bytes 1572872 | tf_op jit(solution)/shard_map/while/body/eval_jaxpr/ppermute | solution.py:12
  106.8 1.3 collective-permute-start.3
  108.2 4.5 %select_add_fusion.2 = f32[2048,1024]{1,0:T(8,128)} fusion(f32[2048,1024]{1,0:T(8,128)} %get-tuple-element.140, pred[]{:T(512)S(6)} %compare.6, bf16[128,1024]{1,0:T(8,128)(2,1)S(1)} %copy.16, bf16[2048]{0:T(1024)(128)(2,1)S(1)} %broadcast_bitcast_fusion.6, bf16[1024]{0:T(1024)(128)(2,1)S(1)} %broadcast_bitcast_fusion.7, ...), kind=kOutput, calls=%fused_computation.clone.1 | convolution fusion | flops 541458432 | bytes 17569792 | tf_op jit(solution)/shard_map/while/body/eval_jaxpr/dot_general | solution.py:30
  112.8 4.3 %collective-permute-done.1 = s32[16,1]{0,1:T(1,128)S(1)} collective-permute-done((s32[16,1]{0,1:T(1,128)S(1)}, s32[16,1]{0,1:T(1,128)S(1)}, u32[]{:S(2)}, u32[]{:S(2)}) %collective-permute-start.1) | collective-permute-done | bytes 96 | tf_op jit(solution)/shard_map/while/body/eval_jaxpr/ppermute | solution.py:12
  117.1 0.1 pad_maximum_fusion.2
  117.4 4.4 %collective-permute-start = (bf16[2048,128]{1,0:T(8,128)(2,1)S(1)}, bf16[2048,128]{1,0:T(8,128)(2,1)S(1)}, u32[]{:S(2)}, u32[]{:S(2)}) collective-permute-start(bf16[2048,128]{1,0:T(8,128)(2,1)S(1)} %get-tuple-element.127), channel_id=1, source_target_pairs={{0,3},{1,0},{2,1},{3,2},{4,7},{5,4},{6,5},{7,6},{8,11},{9,8},{10,9... | collective-permute-start | bytes 1572872 | tf_op jit(solution)/shard_map/while/body/eval_jaxpr/ppermute | solution.py:12
  121.9 1.3 collective-permute-start.3
  123.3 7.9 %select_add_fusion.2 = f32[2048,1024]{1,0:T(8,128)} fusion(f32[2048,1024]{1,0:T(8,128)} %get-tuple-element.140, pred[]{:T(512)S(6)} %compare.6, bf16[128,1024]{1,0:T(8,128)(2,1)S(1)} %copy.16, bf16[2048]{0:T(1024)(128)(2,1)S(1)} %broadcast_bitcast_fusion.6, bf16[1024]{0:T(1024)(128)(2,1)S(1)} %broadcast_bitcast_fusion.7, ...), kind=kOutput, calls=%fused_computation.clone.1 | convolution fusion | flops 541458432 | bytes 17569792 | tf_op jit(solution)/shard_map/while/body/eval_jaxpr/dot_general | solution.py:30
  131.3 0.1 pad_maximum_fusion.2
  131.5 4.3 %collective-permute-start = (bf16[2048,128]{1,0:T(8,128)(2,1)S(1)}, bf16[2048,128]{1,0:T(8,128)(2,1)S(1)}, u32[]{:S(2)}, u32[]{:S(2)}) collective-permute-start(bf16[2048,128]{1,0:T(8,128)(2,1)S(1)} %get-tuple-element.127), channel_id=1, source_target_pairs={{0,3},{1,0},{2,1},{3,2},{4,7},{5,4},{6,5},{7,6},{8,11},{9,8},{10,9... | collective-permute-start | bytes 1572872 | tf_op jit(solution)/shard_map/while/body/eval_jaxpr/ppermute | solution.py:12
  136.0 1.3 collective-permute-start.3
  137.5 7.9 %select_add_fusion.2 = f32[2048,1024]{1,0:T(8,128)} fusion(f32[2048,1024]{1,0:T(8,128)} %get-tuple-element.140, pred[]{:T(512)S(6)} %compare.6, bf16[128,1024]{1,0:T(8,128)(2,1)S(1)} %copy.16, bf16[2048]{0:T(1024)(128)(2,1)S(1)} %broadcast_bitcast_fusion.6, bf16[1024]{0:T(1024)(128)(2,1)S(1)} %broadcast_bitcast_fusion.7, ...), kind=kOutput, calls=%fused_computation.clone.1 | convolution fusion | flops 541458432 | bytes 17569792 | tf_op jit(solution)/shard_map/while/body/eval_jaxpr/dot_general | solution.py:30
  145.4 0.1 pad_maximum_fusion.2
  145.7 3.3 %collective-permute-start = (bf16[2048,128]{1,0:T(8,128)(2,1)S(1)}, bf16[2048,128]{1,0:T(8,128)(2,1)S(1)}, u32[]{:S(2)}, u32[]{:S(2)}) collective-permute-start(bf16[2048,128]{1,0:T(8,128)(2,1)S(1)} %get-tuple-element.127), channel_id=1, source_target_pairs={{0,3},{1,0},{2,1},{3,2},{4,7},{5,4},{6,5},{7,6},{8,11},{9,8},{10,9... | collective-permute-start | bytes 1572872 | tf_op jit(solution)/shard_map/while/body/eval_jaxpr/ppermute | solution.py:12
  149.1 1.3 collective-permute-start.3
  150.6 7.9 %select_add_fusion.2 = f32[2048,1024]{1,0:T(8,128)} fusion(f32[2048,1024]{1,0:T(8,128)} %get-tuple-element.140, pred[]{:T(512)S(6)} %compare.6, bf16[128,1024]{1,0:T(8,128)(2,1)S(1)} %copy.16, bf16[2048]{0:T(1024)(128)(2,1)S(1)} %broadcast_bitcast_fusion.6, bf16[1024]{0:T(1024)(128)(2,1)S(1)} %broadcast_bitcast_fusion.7, ...), kind=kOutput, calls=%fused_computation.clone.1 | convolution fusion | flops 541458432 | bytes 17569792 | tf_op jit(solution)/shard_map/while/body/eval_jaxpr/dot_general | solution.py:30
  158.5 0.5 collective-permute-done.1
  159.1 0.1 pad_maximum_fusion.2
  159.3 2.2 collective-permute-start
  161.7 1.8 collective-permute-start.3
  163.7 7.9 %select_add_fusion.2 = f32[2048,1024]{1,0:T(8,128)} fusion(f32[2048,1024]{1,0:T(8,128)} %get-tuple-element.140, pred[]{:T(512)S(6)} %compare.6, bf16[128,1024]{1,0:T(8,128)(2,1)S(1)} %copy.16, bf16[2048]{0:T(1024)(128)(2,1)S(1)} %broadcast_bitcast_fusion.6, bf16[1024]{0:T(1024)(128)(2,1)S(1)} %broadcast_bitcast_fusion.7, ...), kind=kOutput, calls=%fused_computation.clone.1 | convolution fusion | flops 541458432 | bytes 17569792 | tf_op jit(solution)/shard_map/while/body/eval_jaxpr/dot_general | solution.py:30
  171.6 0.6 collective-permute-done.1
  172.2 0.1 pad_maximum_fusion.2
  172.4 3.2 %collective-permute-start = (bf16[2048,128]{1,0:T(8,128)(2,1)S(1)}, bf16[2048,128]{1,0:T(8,128)(2,1)S(1)}, u32[]{:S(2)}, u32[]{:S(2)}) collective-permute-start(bf16[2048,128]{1,0:T(8,128)(2,1)S(1)} %get-tuple-element.127), channel_id=1, source_target_pairs={{0,3},{1,0},{2,1},{3,2},{4,7},{5,4},{6,5},{7,6},{8,11},{9,8},{10,9... | collective-permute-start | bytes 1572872 | tf_op jit(solution)/shard_map/while/body/eval_jaxpr/ppermute | solution.py:12
  175.8 1.9 collective-permute-start.3
  177.8 7.9 %select_add_fusion.2 = f32[2048,1024]{1,0:T(8,128)} fusion(f32[2048,1024]{1,0:T(8,128)} %get-tuple-element.140, pred[]{:T(512)S(6)} %compare.6, bf16[128,1024]{1,0:T(8,128)(2,1)S(1)} %copy.16, bf16[2048]{0:T(1024)(128)(2,1)S(1)} %broadcast_bitcast_fusion.6, bf16[1024]{0:T(1024)(128)(2,1)S(1)} %broadcast_bitcast_fusion.7, ...), kind=kOutput, calls=%fused_computation.clone.1 | convolution fusion | flops 541458432 | bytes 17569792 | tf_op jit(solution)/shard_map/while/body/eval_jaxpr/dot_general | solution.py:30
  185.8 0.1 pad_maximum_fusion.2
  186.0 3.1 %collective-permute-start = (bf16[2048,128]{1,0:T(8,128)(2,1)S(1)}, bf16[2048,128]{1,0:T(8,128)(2,1)S(1)}, u32[]{:S(2)}, u32[]{:S(2)}) collective-permute-start(bf16[2048,128]{1,0:T(8,128)(2,1)S(1)} %get-tuple-element.127), channel_id=1, source_target_pairs={{0,3},{1,0},{2,1},{3,2},{4,7},{5,4},{6,5},{7,6},{8,11},{9,8},{10,9... | collective-permute-start | bytes 1572872 | tf_op jit(solution)/shard_map/while/body/eval_jaxpr/ppermute | solution.py:12
  189.3 1.5 collective-permute-start.3
  190.9 7.9 %select_add_fusion.2 = f32[2048,1024]{1,0:T(8,128)} fusion(f32[2048,1024]{1,0:T(8,128)} %get-tuple-element.140, pred[]{:T(512)S(6)} %compare.6, bf16[128,1024]{1,0:T(8,128)(2,1)S(1)} %copy.16, bf16[2048]{0:T(1024)(128)(2,1)S(1)} %broadcast_bitcast_fusion.6, bf16[1024]{0:T(1024)(128)(2,1)S(1)} %broadcast_bitcast_fusion.7, ...), kind=kOutput, calls=%fused_computation.clone.1 | convolution fusion | flops 541458432 | bytes 17569792 | tf_op jit(solution)/shard_map/while/body/eval_jaxpr/dot_general | solution.py:30
  198.9 0.1 pad_maximum_fusion.2
  199.1 0.1 broadcast_bitcast_fusion.3
  199.2 4.6 %fusion.6 = f32[2048,1024]{1,0:T(8,128)} fusion(bf16[2048,256]{1,0:T(8,128)(2,1)S(1)} %get-tuple-element.42, bf16[128,1024]{1,0:T(8,128)(2,1)S(1)} %get-tuple-element.44, bf16[2048]{0:T(1024)(128)(2,1)S(1)} %broadcast_bitcast_fusion.2, bf16[1024]{0:T(1024)(128)(2,1)S(1)} %broadcast_bitcast_fusion.3), kind=kOutput, calls=%fused_computation.19 | convolution fusion | flops 537264128 | bytes 9181184 | tf_op jit(solution)/shard_map/dot_general | solution.py:30
  203.8 9.3 %add_convert_fusion = bf16[2048,1024]{1,0:T(8,128)(2,1)} fusion(f32[2048,1024]{1,0:T(8,128)} %get-tuple-element.41, f32[2048,1024]{1,0:T(8,128)} %fusion.6), kind=kLoop, calls=%fused_computation.13 | loop fusion | flops 4194304 | bytes 20971520 | tf_op jit(solution)/shard_map/convert_element_type | solution.py:77
  213.1 4.8 %reshape.54 = bf16[16,131072]{1,0:T(8,128)(2,1)} reshape(bf16[2048,1024]{1,0:T(8,128)(2,1)} %add_convert_fusion) | data formatting | bytes 8388608 | tf_op jit(solution)/shard_map/reshape | solution.py:91
  217.9 5.4 %convolution_convert_fusion = bf16[16,131072]{1,0:T(8,128)(2,1)} fusion(bf16[16,131072]{1,0:T(8,128)(2,1)} %reshape.54, s32[16]{0:T(128)S(1)} %multiply_add_fusion), kind=kOutput, calls=%fused_computation.12 | convolution fusion | flops 69206272 | bytes 8388672 | tf_op jit(solution)/shard_map/dot_general | solution.py:90
  223.3 4.8 %reshape.55 = bf16[8,256,1024]{2,1,0:T(8,128)(2,1)} reshape(bf16[16,131072]{1,0:T(8,128)(2,1)} %convolution_convert_fusion) | data formatting | bytes 8388608 | tf_op jit(solution)/shard_map/reshape | solution.py:93
  228.2 52.7 %all_to_all.5 = bf16[8,256,1024]{2,1,0:T(8,128)(2,1)S(1)} all-to-all(bf16[8,256,1024]{2,1,0:T(8,128)(2,1)} %reshape.55), channel_id=1, replica_groups=mesh['row'=8,'col'=4] {'row'}, dimensions={0} | all-to-all | bytes 8388608 | tf_op jit(solution)/shard_map/all_to_all | solution.py:94
  280.8 2.0 copy.25
  (115 shorter events, 2.9 us)
Async XLA Ops:
  0.0 27.8 %collective-permute-start.4 = (bf16[2048,256]{1,0:T(8,128)(2,1)}, bf16[2048,256]{1,0:T(8,128)(2,1)S(1)}, u32[]{:S(2)}, u32[]{:S(2)}) collective-permute-start(bf16[2048,256]{1,0:T(8,128)(2,1)} %param.7), channel_id=1, source_target_pairs={{0,3},{1,0},{2,1},{3,2},{4,7},{5,4},{6,5},{7,6},{8,11},{9,8},{10,9... | collective-permute-start | bytes 3145736 | tf_op jit(solution)/shard_map/ppermute | solution.py:12
  5.0 31.9 %collective-permute-start.7 = (s32[16,2]{0,1:T(2,128)}, s32[16,2]{0,1:T(2,128)S(1)}, u32[]{:S(2)}, u32[]{:S(2)}) collective-permute-start(s32[16,2]{0,1:T(2,128)} %param.8), channel_id=1, source_target_pairs={{0,3},{1,0},{2,1},{3,2},{4,7},{5,4},{6,5},{7,6},{8,11},{9,8},{10,9... | collective-permute-start | bytes 392 | tf_op jit(solution)/shard_map/ppermute | solution.py:12
  5.5 33.7 %collective-permute-start.10 = (bf16[128,1024]{1,0:T(8,128)(2,1)}, bf16[128,1024]{1,0:T(8,128)(2,1)S(1)}, u32[]{:S(2)}, u32[]{:S(2)}) collective-permute-start(bf16[128,1024]{1,0:T(8,128)(2,1)} %param.9), channel_id=1, source_target_pairs={{0,28},{4,0},{8,4},{12,8},{16,12},{20,16},{24,20},{28,24},{1,29},{... | collective-permute-start | bytes 786440 | tf_op jit(solution)/shard_map/ppermute | solution.py:12
  6.8 24.4 %collective-permute-start.13 = (s32[1,8]{1,0:T(1,128)}, s32[1,8]{1,0:T(1,128)S(1)}, u32[]{:S(2)}, u32[]{:S(2)}) collective-permute-start(s32[1,8]{1,0:T(1,128)} %param.10), channel_id=1, source_target_pairs={{0,28},{4,0},{8,4},{12,8},{16,12},{20,16},{24,20},{28,24},{1,29},{... | collective-permute-start | bytes 104 | tf_op jit(solution)/shard_map/ppermute | solution.py:12
  29.1 47.5 %collective-permute-start.5 = (bf16[2048,256]{1,0:T(8,128)(2,1)S(1)}, bf16[2048,256]{1,0:T(8,128)(2,1)S(1)}, u32[]{:S(2)}, u32[]{:S(2)}) collective-permute-start(bf16[2048,256]{1,0:T(8,128)(2,1)S(1)} %broadcast_select_fusion), channel_id=1, source_target_pairs={{0,2},{1,3},{2,0},{3,1},{4,6},{5,7},{6,4},{7,5},{8,10},{9,11},{10,... | collective-permute-start | bytes 3145736 | tf_op jit(solution)/shard_map/ppermute | solution.py:12
  31.9 3.5 %collective-permute-start.14 = (s32[1,8]{1,0:T(1,128)S(1)}, s32[1,8]{1,0:T(1,128)S(1)}, u32[]{:S(2)}, u32[]{:S(2)}) collective-permute-start(s32[1,8]{1,0:T(1,128)S(1)} %broadcast_select_fusion.5), channel_id=1, source_target_pairs={{0,24},{4,28},{8,0},{12,4},{16,8},{20,12},{24,16},{28,20},{1,25},{... | collective-permute-start | bytes 104 | tf_op jit(solution)/shard_map/ppermute | solution.py:12
  35.4 45.3 %collective-permute-start.15 = (s32[1,8]{1,0:T(1,128)S(1)}, s32[1,8]{1,0:T(1,128)S(1)}, u32[]{:S(2)}, u32[]{:S(2)}) collective-permute-start(s32[1,8]{1,0:T(1,128)S(1)} %broadcast_select_fusion.6), channel_id=1, source_target_pairs={{0,16},{4,20},{8,24},{12,28},{16,0},{20,4},{24,8},{28,12},{1,17},{... | collective-permute-start | bytes 104 | tf_op jit(solution)/shard_map/ppermute | solution.py:12
  37.6 41.4 %collective-permute-start.8 = (s32[16,2]{0,1:T(2,128)S(1)}, s32[16,2]{0,1:T(2,128)S(1)}, u32[]{:S(2)}, u32[]{:S(2)}) collective-permute-start(s32[16,2]{0,1:T(2,128)S(1)} %broadcast_select_fusion.8), channel_id=1, source_target_pairs={{0,2},{1,3},{2,0},{3,1},{4,6},{5,7},{6,4},{7,5},{8,10},{9,11},{10,... | collective-permute-start | bytes 392 | tf_op jit(solution)/shard_map/ppermute | solution.py:12
  40.2 39.0 %collective-permute-start.11 = (bf16[128,1024]{1,0:T(8,128)(2,1)S(1)}, bf16[128,1024]{1,0:T(8,128)(2,1)S(1)}, u32[]{:S(2)}, u32[]{:S(2)}) collective-permute-start(bf16[128,1024]{1,0:T(8,128)(2,1)S(1)} %broadcast_select_fusion.2), channel_id=1, source_target_pairs={{0,24},{4,28},{8,0},{12,4},{16,8},{20,12},{24,16},{28,20},{1,25},{... | collective-permute-start | bytes 786440 | tf_op jit(solution)/shard_map/ppermute | solution.py:12
  76.7 25.0 %collective-permute-start.6 = (bf16[2048,256]{1,0:T(8,128)(2,1)S(1)}, bf16[2048,256]{1,0:T(8,128)(2,1)S(1)}, u32[]{:S(2)}, u32[]{:S(2)}) collective-permute-start(bf16[2048,256]{1,0:T(8,128)(2,1)S(1)} %broadcast_select_fusion.1), channel_id=1, source_target_pairs={{0,3},{1,0},{2,1},{3,2},{4,7},{5,4},{6,5},{7,6},{8,11},{9,8},{10,9... | collective-permute-start | bytes 3145736 | tf_op jit(solution)/shard_map/ppermute | solution.py:12
  79.1 22.6 %collective-permute-start.9 = (s32[16,2]{0,1:T(2,128)S(1)}, s32[16,2]{0,1:T(2,128)S(1)}, u32[]{:S(2)}, u32[]{:S(2)}) collective-permute-start(s32[16,2]{0,1:T(2,128)S(1)} %broadcast_select_fusion.9), channel_id=1, source_target_pairs={{0,3},{1,0},{2,1},{3,2},{4,7},{5,4},{6,5},{7,6},{8,11},{9,8},{10,9... | collective-permute-start | bytes 392 | tf_op jit(solution)/shard_map/ppermute | solution.py:12
  79.2 22.5 %collective-permute-start.12 = (bf16[128,1024]{1,0:T(8,128)(2,1)S(1)}, bf16[128,1024]{1,0:T(8,128)(2,1)S(1)}, u32[]{:S(2)}, u32[]{:S(2)}) collective-permute-start(bf16[128,1024]{1,0:T(8,128)(2,1)S(1)} %broadcast_select_fusion.3), channel_id=1, source_target_pairs={{0,16},{4,20},{8,24},{12,28},{16,0},{20,4},{24,8},{28,12},{1,17},{... | collective-permute-start | bytes 786440 | tf_op jit(solution)/shard_map/ppermute | solution.py:12
  102.2 14.9 %collective-permute-start = (bf16[2048,128]{1,0:T(8,128)(2,1)S(1)}, bf16[2048,128]{1,0:T(8,128)(2,1)S(1)}, u32[]{:S(2)}, u32[]{:S(2)}) collective-permute-start(bf16[2048,128]{1,0:T(8,128)(2,1)S(1)} %get-tuple-element.127), channel_id=1, source_target_pairs={{0,3},{1,0},{2,1},{3,2},{4,7},{5,4},{6,5},{7,6},{8,11},{9,8},{10,9... | collective-permute-start | bytes 1572872 | tf_op jit(solution)/shard_map/while/body/eval_jaxpr/ppermute | solution.py:12
  106.6 10.5 %collective-permute-start.1 = (s32[16,1]{0,1:T(1,128)S(1)}, s32[16,1]{0,1:T(1,128)S(1)}, u32[]{:S(2)}, u32[]{:S(2)}) collective-permute-start(s32[16,1]{0,1:T(1,128)S(1)} %get-tuple-element.129), channel_id=1, source_target_pairs={{0,3},{1,0},{2,1},{3,2},{4,7},{5,4},{6,5},{7,6},{8,11},{9,8},{10,9... | collective-permute-start | bytes 200 | tf_op jit(solution)/shard_map/while/body/eval_jaxpr/ppermute | solution.py:12
  106.7 10.6 %collective-permute-start.2 = (bf16[128,1024]{1,0:T(8,128)(2,1)S(1)}, bf16[128,1024]{1,0:T(8,128)(2,1)S(1)}, u32[]{:S(2)}, u32[]{:S(2)}) collective-permute-start(bf16[128,1024]{1,0:T(8,128)(2,1)S(1)} %copy.16), channel_id=1, source_target_pairs={{0,28},{4,0},{8,4},{12,8},{16,12},{20,16},{24,20},{28,24},{1,29},{... | collective-permute-start | bytes 786440 | tf_op jit(solution)/shard_map/while/body/eval_jaxpr/ppermute | solution.py:12
  106.8 10.5 %collective-permute-start.3 = (s32[1,8]{1,0:T(1,128)S(1)}, s32[1,8]{1,0:T(1,128)S(1)}, u32[]{:S(2)}, u32[]{:S(2)}) collective-permute-start(s32[1,8]{1,0:T(1,128)S(1)} %copy.17), channel_id=1, source_target_pairs={{0,28},{4,0},{8,4},{12,8},{16,12},{20,16},{24,20},{28,24},{1,29},{... | collective-permute-start | bytes 104 | tf_op jit(solution)/shard_map/while/body/eval_jaxpr/ppermute | solution.py:12
  117.4 13.9 %collective-permute-start = (bf16[2048,128]{1,0:T(8,128)(2,1)S(1)}, bf16[2048,128]{1,0:T(8,128)(2,1)S(1)}, u32[]{:S(2)}, u32[]{:S(2)}) collective-permute-start(bf16[2048,128]{1,0:T(8,128)(2,1)S(1)} %get-tuple-element.127), channel_id=1, source_target_pairs={{0,3},{1,0},{2,1},{3,2},{4,7},{5,4},{6,5},{7,6},{8,11},{9,8},{10,9... | collective-permute-start | bytes 1572872 | tf_op jit(solution)/shard_map/while/body/eval_jaxpr/ppermute | solution.py:12
  121.7 9.6 %collective-permute-start.1 = (s32[16,1]{0,1:T(1,128)S(1)}, s32[16,1]{0,1:T(1,128)S(1)}, u32[]{:S(2)}, u32[]{:S(2)}) collective-permute-start(s32[16,1]{0,1:T(1,128)S(1)} %get-tuple-element.129), channel_id=1, source_target_pairs={{0,3},{1,0},{2,1},{3,2},{4,7},{5,4},{6,5},{7,6},{8,11},{9,8},{10,9... | collective-permute-start | bytes 200 | tf_op jit(solution)/shard_map/while/body/eval_jaxpr/ppermute | solution.py:12
  121.8 9.6 %collective-permute-start.2 = (bf16[128,1024]{1,0:T(8,128)(2,1)S(1)}, bf16[128,1024]{1,0:T(8,128)(2,1)S(1)}, u32[]{:S(2)}, u32[]{:S(2)}) collective-permute-start(bf16[128,1024]{1,0:T(8,128)(2,1)S(1)} %copy.16), channel_id=1, source_target_pairs={{0,28},{4,0},{8,4},{12,8},{16,12},{20,16},{24,20},{28,24},{1,29},{... | collective-permute-start | bytes 786440 | tf_op jit(solution)/shard_map/while/body/eval_jaxpr/ppermute | solution.py:12
  121.9 9.5 %collective-permute-start.3 = (s32[1,8]{1,0:T(1,128)S(1)}, s32[1,8]{1,0:T(1,128)S(1)}, u32[]{:S(2)}, u32[]{:S(2)}) collective-permute-start(s32[1,8]{1,0:T(1,128)S(1)} %copy.17), channel_id=1, source_target_pairs={{0,28},{4,0},{8,4},{12,8},{16,12},{20,16},{24,20},{28,24},{1,29},{... | collective-permute-start | bytes 104 | tf_op jit(solution)/shard_map/while/body/eval_jaxpr/ppermute | solution.py:12
  131.5 13.9 %collective-permute-start = (bf16[2048,128]{1,0:T(8,128)(2,1)S(1)}, bf16[2048,128]{1,0:T(8,128)(2,1)S(1)}, u32[]{:S(2)}, u32[]{:S(2)}) collective-permute-start(bf16[2048,128]{1,0:T(8,128)(2,1)S(1)} %get-tuple-element.127), channel_id=1, source_target_pairs={{0,3},{1,0},{2,1},{3,2},{4,7},{5,4},{6,5},{7,6},{8,11},{9,8},{10,9... | collective-permute-start | bytes 1572872 | tf_op jit(solution)/shard_map/while/body/eval_jaxpr/ppermute | solution.py:12
  135.8 9.6 %collective-permute-start.1 = (s32[16,1]{0,1:T(1,128)S(1)}, s32[16,1]{0,1:T(1,128)S(1)}, u32[]{:S(2)}, u32[]{:S(2)}) collective-permute-start(s32[16,1]{0,1:T(1,128)S(1)} %get-tuple-element.129), channel_id=1, source_target_pairs={{0,3},{1,0},{2,1},{3,2},{4,7},{5,4},{6,5},{7,6},{8,11},{9,8},{10,9... | collective-permute-start | bytes 200 | tf_op jit(solution)/shard_map/while/body/eval_jaxpr/ppermute | solution.py:12
  135.9 9.6 %collective-permute-start.2 = (bf16[128,1024]{1,0:T(8,128)(2,1)S(1)}, bf16[128,1024]{1,0:T(8,128)(2,1)S(1)}, u32[]{:S(2)}, u32[]{:S(2)}) collective-permute-start(bf16[128,1024]{1,0:T(8,128)(2,1)S(1)} %copy.16), channel_id=1, source_target_pairs={{0,28},{4,0},{8,4},{12,8},{16,12},{20,16},{24,20},{28,24},{1,29},{... | collective-permute-start | bytes 786440 | tf_op jit(solution)/shard_map/while/body/eval_jaxpr/ppermute | solution.py:12
  136.0 9.5 %collective-permute-start.3 = (s32[1,8]{1,0:T(1,128)S(1)}, s32[1,8]{1,0:T(1,128)S(1)}, u32[]{:S(2)}, u32[]{:S(2)}) collective-permute-start(s32[1,8]{1,0:T(1,128)S(1)} %copy.17), channel_id=1, source_target_pairs={{0,28},{4,0},{8,4},{12,8},{16,12},{20,16},{24,20},{28,24},{1,29},{... | collective-permute-start | bytes 104 | tf_op jit(solution)/shard_map/while/body/eval_jaxpr/ppermute | solution.py:12
  145.7 13.4 %collective-permute-start = (bf16[2048,128]{1,0:T(8,128)(2,1)S(1)}, bf16[2048,128]{1,0:T(8,128)(2,1)S(1)}, u32[]{:S(2)}, u32[]{:S(2)}) collective-permute-start(bf16[2048,128]{1,0:T(8,128)(2,1)S(1)} %get-tuple-element.127), channel_id=1, source_target_pairs={{0,3},{1,0},{2,1},{3,2},{4,7},{5,4},{6,5},{7,6},{8,11},{9,8},{10,9... | collective-permute-start | bytes 1572872 | tf_op jit(solution)/shard_map/while/body/eval_jaxpr/ppermute | solution.py:12
  149.0 10.1 %collective-permute-start.1 = (s32[16,1]{0,1:T(1,128)S(1)}, s32[16,1]{0,1:T(1,128)S(1)}, u32[]{:S(2)}, u32[]{:S(2)}) collective-permute-start(s32[16,1]{0,1:T(1,128)S(1)} %get-tuple-element.129), channel_id=1, source_target_pairs={{0,3},{1,0},{2,1},{3,2},{4,7},{5,4},{6,5},{7,6},{8,11},{9,8},{10,9... | collective-permute-start | bytes 200 | tf_op jit(solution)/shard_map/while/body/eval_jaxpr/ppermute | solution.py:12
  149.1 10.2 %collective-permute-start.2 = (bf16[128,1024]{1,0:T(8,128)(2,1)S(1)}, bf16[128,1024]{1,0:T(8,128)(2,1)S(1)}, u32[]{:S(2)}, u32[]{:S(2)}) collective-permute-start(bf16[128,1024]{1,0:T(8,128)(2,1)S(1)} %copy.16), channel_id=1, source_target_pairs={{0,28},{4,0},{8,4},{12,8},{16,12},{20,16},{24,20},{28,24},{1,29},{... | collective-permute-start | bytes 786440 | tf_op jit(solution)/shard_map/while/body/eval_jaxpr/ppermute | solution.py:12
  149.1 10.1 %collective-permute-start.3 = (s32[1,8]{1,0:T(1,128)S(1)}, s32[1,8]{1,0:T(1,128)S(1)}, u32[]{:S(2)}, u32[]{:S(2)}) collective-permute-start(s32[1,8]{1,0:T(1,128)S(1)} %copy.17), channel_id=1, source_target_pairs={{0,28},{4,0},{8,4},{12,8},{16,12},{20,16},{24,20},{28,24},{1,29},{... | collective-permute-start | bytes 104 | tf_op jit(solution)/shard_map/while/body/eval_jaxpr/ppermute | solution.py:12
  159.3 12.9 %collective-permute-start = (bf16[2048,128]{1,0:T(8,128)(2,1)S(1)}, bf16[2048,128]{1,0:T(8,128)(2,1)S(1)}, u32[]{:S(2)}, u32[]{:S(2)}) collective-permute-start(bf16[2048,128]{1,0:T(8,128)(2,1)S(1)} %get-tuple-element.127), channel_id=1, source_target_pairs={{0,3},{1,0},{2,1},{3,2},{4,7},{5,4},{6,5},{7,6},{8,11},{9,8},{10,9... | collective-permute-start | bytes 1572872 | tf_op jit(solution)/shard_map/while/body/eval_jaxpr/ppermute | solution.py:12
  161.5 10.7 %collective-permute-start.1 = (s32[16,1]{0,1:T(1,128)S(1)}, s32[16,1]{0,1:T(1,128)S(1)}, u32[]{:S(2)}, u32[]{:S(2)}) collective-permute-start(s32[16,1]{0,1:T(1,128)S(1)} %get-tuple-element.129), channel_id=1, source_target_pairs={{0,3},{1,0},{2,1},{3,2},{4,7},{5,4},{6,5},{7,6},{8,11},{9,8},{10,9... | collective-permute-start | bytes 200 | tf_op jit(solution)/shard_map/while/body/eval_jaxpr/ppermute | solution.py:12
  161.6 10.7 %collective-permute-start.2 = (bf16[128,1024]{1,0:T(8,128)(2,1)S(1)}, bf16[128,1024]{1,0:T(8,128)(2,1)S(1)}, u32[]{:S(2)}, u32[]{:S(2)}) collective-permute-start(bf16[128,1024]{1,0:T(8,128)(2,1)S(1)} %copy.16), channel_id=1, source_target_pairs={{0,28},{4,0},{8,4},{12,8},{16,12},{20,16},{24,20},{28,24},{1,29},{... | collective-permute-start | bytes 786440 | tf_op jit(solution)/shard_map/while/body/eval_jaxpr/ppermute | solution.py:12
  161.7 10.6 %collective-permute-start.3 = (s32[1,8]{1,0:T(1,128)S(1)}, s32[1,8]{1,0:T(1,128)S(1)}, u32[]{:S(2)}, u32[]{:S(2)}) collective-permute-start(s32[1,8]{1,0:T(1,128)S(1)} %copy.17), channel_id=1, source_target_pairs={{0,28},{4,0},{8,4},{12,8},{16,12},{20,16},{24,20},{28,24},{1,29},{... | collective-permute-start | bytes 104 | tf_op jit(solution)/shard_map/while/body/eval_jaxpr/ppermute | solution.py:12
  172.4 13.3 %collective-permute-start = (bf16[2048,128]{1,0:T(8,128)(2,1)S(1)}, bf16[2048,128]{1,0:T(8,128)(2,1)S(1)}, u32[]{:S(2)}, u32[]{:S(2)}) collective-permute-start(bf16[2048,128]{1,0:T(8,128)(2,1)S(1)} %get-tuple-element.127), channel_id=1, source_target_pairs={{0,3},{1,0},{2,1},{3,2},{4,7},{5,4},{6,5},{7,6},{8,11},{9,8},{10,9... | collective-permute-start | bytes 1572872 | tf_op jit(solution)/shard_map/while/body/eval_jaxpr/ppermute | solution.py:12
  175.6 10.1 %collective-permute-start.1 = (s32[16,1]{0,1:T(1,128)S(1)}, s32[16,1]{0,1:T(1,128)S(1)}, u32[]{:S(2)}, u32[]{:S(2)}) collective-permute-start(s32[16,1]{0,1:T(1,128)S(1)} %get-tuple-element.129), channel_id=1, source_target_pairs={{0,3},{1,0},{2,1},{3,2},{4,7},{5,4},{6,5},{7,6},{8,11},{9,8},{10,9... | collective-permute-start | bytes 200 | tf_op jit(solution)/shard_map/while/body/eval_jaxpr/ppermute | solution.py:12
  175.7 10.2 %collective-permute-start.2 = (bf16[128,1024]{1,0:T(8,128)(2,1)S(1)}, bf16[128,1024]{1,0:T(8,128)(2,1)S(1)}, u32[]{:S(2)}, u32[]{:S(2)}) collective-permute-start(bf16[128,1024]{1,0:T(8,128)(2,1)S(1)} %copy.16), channel_id=1, source_target_pairs={{0,28},{4,0},{8,4},{12,8},{16,12},{20,16},{24,20},{28,24},{1,29},{... | collective-permute-start | bytes 786440 | tf_op jit(solution)/shard_map/while/body/eval_jaxpr/ppermute | solution.py:12
  175.8 10.1 %collective-permute-start.3 = (s32[1,8]{1,0:T(1,128)S(1)}, s32[1,8]{1,0:T(1,128)S(1)}, u32[]{:S(2)}, u32[]{:S(2)}) collective-permute-start(s32[1,8]{1,0:T(1,128)S(1)} %copy.17), channel_id=1, source_target_pairs={{0,28},{4,0},{8,4},{12,8},{16,12},{20,16},{24,20},{28,24},{1,29},{... | collective-permute-start | bytes 104 | tf_op jit(solution)/shard_map/while/body/eval_jaxpr/ppermute | solution.py:12
  186.0 12.9 %collective-permute-start = (bf16[2048,128]{1,0:T(8,128)(2,1)S(1)}, bf16[2048,128]{1,0:T(8,128)(2,1)S(1)}, u32[]{:S(2)}, u32[]{:S(2)}) collective-permute-start(bf16[2048,128]{1,0:T(8,128)(2,1)S(1)} %get-tuple-element.127), channel_id=1, source_target_pairs={{0,3},{1,0},{2,1},{3,2},{4,7},{5,4},{6,5},{7,6},{8,11},{9,8},{10,9... | collective-permute-start | bytes 1572872 | tf_op jit(solution)/shard_map/while/body/eval_jaxpr/ppermute | solution.py:12
  189.1 9.8 %collective-permute-start.1 = (s32[16,1]{0,1:T(1,128)S(1)}, s32[16,1]{0,1:T(1,128)S(1)}, u32[]{:S(2)}, u32[]{:S(2)}) collective-permute-start(s32[16,1]{0,1:T(1,128)S(1)} %get-tuple-element.129), channel_id=1, source_target_pairs={{0,3},{1,0},{2,1},{3,2},{4,7},{5,4},{6,5},{7,6},{8,11},{9,8},{10,9... | collective-permute-start | bytes 200 | tf_op jit(solution)/shard_map/while/body/eval_jaxpr/ppermute | solution.py:12
  189.2 9.8 %collective-permute-start.2 = (bf16[128,1024]{1,0:T(8,128)(2,1)S(1)}, bf16[128,1024]{1,0:T(8,128)(2,1)S(1)}, u32[]{:S(2)}, u32[]{:S(2)}) collective-permute-start(bf16[128,1024]{1,0:T(8,128)(2,1)S(1)} %copy.16), channel_id=1, source_target_pairs={{0,28},{4,0},{8,4},{12,8},{16,12},{20,16},{24,20},{28,24},{1,29},{... | collective-permute-start | bytes 786440 | tf_op jit(solution)/shard_map/while/body/eval_jaxpr/ppermute | solution.py:12
  189.3 9.8 %collective-permute-start.3 = (s32[1,8]{1,0:T(1,128)S(1)}, s32[1,8]{1,0:T(1,128)S(1)}, u32[]{:S(2)}, u32[]{:S(2)}) collective-permute-start(s32[1,8]{1,0:T(1,128)S(1)} %copy.17), channel_id=1, source_target_pairs={{0,28},{4,0},{8,4},{12,8},{16,12},{20,16},{24,20},{28,24},{1,29},{... | collective-permute-start | bytes 104 | tf_op jit(solution)/shard_map/while/body/eval_jaxpr/ppermute | solution.py:12
where the time goes:
time: 283 us
  waiting for transfers between devices  83.4 us (29%)
  matrix products  62.1 us (22%)
  starting transfers between devices  54.5 us (19%)
  blocking collectives  52.7 us (19%)
  other arithmetic  16 us (6%)
  local copies, waits for them, and re-layouts  13.5 us (5%)
    ppermute x40, waiting for transfers between devices, from_behind(): return lax.ppermute(value, axis, pairs)  83.4 us
    dot_general x8, matrix products, product(): jnp.dot(masked_a(panel_a, mask_a), masked_b(panel_b, mask_b), preferred_e...  56.6 us
    ppermute x40, starting transfers between devices, from_behind(): return lax.ppermute(value, axis, pairs)  54.5 us
    all_to_all x1, blocking collectives, on_device(): lax.all_to_all(packed, 'row', split_axis=0, concat_axis=0, tiled=True)  52.7 us
    convert_element_type x1, other arithmetic, on_device(): result = total.astype(jnp.bfloat16)  9.3 us
  transfers between devices with their start and end apart: 40, of which 7 were waited for; matrix products, arithmetic and copies ran while one was open for 21% of the time, Pallas kernels for 0%

commit v1 on v0

v1 whole, which is shorter than its diff:
```python
import functools
import jax
import jax.numpy as jnp
from jax import lax
from jax.experimental import pallas as pl
from jax.experimental.pallas import tpu as pltpu
from jax.sharding import PartitionSpec as P

SLOTS = 2
SMEM_SPEC = pl.BlockSpec(memory_space=pltpu.SMEM)


def pack_kernel(grid_rows, by_distance, owner_ref, am_ref, bm_ref, a_ref, b_ref, *rest):
    outs, b_out, inv, used = rest[:grid_rows], rest[grid_rows], rest[-2], rest[-1]
    tile_rows, inner = am_ref.shape
    tile = a_ref.shape[0] // tile_rows
    wide = a_ref.shape[1] // inner
    me = lax.axis_index("row")

    def clear(i, carry):
        inv[i] = -1
        return carry

    def clear_used(i, carry):
        used[i] = 0
        return carry

    def place(t, carry):
        owner = owner_ref[t, 0]
        slot = used[owner]
        inv[owner * SLOTS + slot] = t
        used[owner] = slot + 1
        return carry

    lax.fori_loop(0, grid_rows * SLOTS, clear, 0)
    lax.fori_loop(0, grid_rows, clear_used, 0)
    lax.fori_loop(0, tile_rows, place, 0)
    for d in range(grid_rows):
        owner = me ^ d if by_distance else d
        for s in range(SLOTS):
            t = inv[owner * SLOTS + s]
            row = jnp.maximum(t, 0)
            start = pl.multiple_of(row * tile, tile)
            for j in range(inner):
                keep = jnp.logical_and(t >= 0, am_ref[row, j] != 0)
                block = a_ref[pl.ds(start, tile), j * wide : (j + 1) * wide]
                outs[d][s * tile : (s + 1) * tile, j * wide : (j + 1) * wide] = jnp.where(
                    keep, block, jnp.zeros_like(block)
                )
    cols = bm_ref.shape[1]
    width = b_ref.shape[1] // cols
    for j in range(cols):
        block = b_ref[:, j * width : (j + 1) * width]
        b_out[:, j * width : (j + 1) * width] = jnp.where(
            bm_ref[0, j] != 0, block, jnp.zeros_like(block)
        )


def pack(a_panels, a_mask, b_panels, b_mask, owner_map, grid_rows, by_distance):
    tile = a_panels.shape[0] // a_mask.shape[0]
    slots = jax.ShapeDtypeStruct((SLOTS * tile, a_panels.shape[1]), a_panels.dtype)
    vmem = pl.BlockSpec(memory_space=pltpu.VMEM)
    outs = pl.pallas_call(
        functools.partial(pack_kernel, grid_rows, by_distance),
        out_shape=[slots] * grid_rows + [jax.ShapeDtypeStruct(b_panels.shape, b_panels.dtype)],
        in_specs=[SMEM_SPEC] * 3 + [vmem] * 2,
        out_specs=[vmem] * (grid_rows + 1),
        scratch_shapes=[
            pltpu.SMEM((grid_rows * SLOTS,), jnp.int32),
            pltpu.SMEM((grid_rows,), jnp.int32),
        ],
        name="pack",
    )(owner_map, a_mask, b_mask, a_panels, b_panels)
    return outs[:-1], outs[-1]


def dot_kernel(at_ref, own_ref, prv_ref, nxt_ref, opp_ref, far_ref, b_ref, *rest):
    out_ref, wide = rest[-2], rest[-1]
    depth = own_ref.shape[2]
    me = at_ref[at_ref.shape[0] - 1]
    far = far_ref[0]
    put = lambda panel, value: wide.__setitem__(
        (slice(None), pl.ds(pl.multiple_of(panel * depth, depth), depth)), value
    )
    put(me, own_ref[0])
    put((me + 3) % 4, jnp.where(me == 0, far, prv_ref[0]))
    put((me + 1) % 4, jnp.where(me == 3, far, nxt_ref[0]))
    put((me + 2) % 4, opp_ref[0])
    out_ref[...] = jnp.dot(
        wide[...], b_ref[...], preferred_element_type=jnp.float32
    ).astype(out_ref.dtype)


def chunk_product(at, parts, b_full, out, rows):
    blocks, height, depth = parts[0].shape
    cols = b_full.shape[1]
    spec = pl.BlockSpec((1, height, depth), lambda i, at: (i, 0, 0))
    operands = [at, *parts, b_full]
    in_specs = [spec] * 5 + [pl.BlockSpec(b_full.shape, lambda i, at: (0, 0))]
    aliases = {}
    if out is not None:
        aliases = {len(operands): 0}
        operands.append(out)
        in_specs.append(pl.BlockSpec(memory_space=pl.ANY))
    flops = 2 * blocks * height * b_full.shape[0] * cols
    return pl.pallas_call(
        dot_kernel,
        out_shape=jax.ShapeDtypeStruct((rows, cols), jnp.bfloat16),
        grid_spec=pltpu.PrefetchScalarGridSpec(
            num_scalar_prefetch=1,
            grid=(blocks,),
            in_specs=in_specs,
            out_specs=pl.BlockSpec((height, cols), lambda i, at: (at[i], 0)),
            scratch_shapes=[pltpu.VMEM((height, b_full.shape[0]), jnp.bfloat16)],
        ),
        input_output_aliases=aliases,
        cost_estimate=pl.CostEstimate(
            flops=flops, bytes_accessed=4 << 20, transcendentals=0
        ),
        name="chunk_product",
    )(*operands)


def by_row(value, distance):
    count = lax.axis_size("row")
    return lax.ppermute(value, "row", [(i, i ^ distance) for i in range(count)])


def gather_b(panel):
    mine = panel[None]
    for bit in (2, 4, 1):
        mine = jnp.concatenate([mine, by_row(mine, bit)])
    me = lax.axis_index("row")
    order = []
    for row in range(8):
        far = me ^ row
        order.append((far & 1) * 4 + (far >> 2 & 1) * 2 + (far >> 1 & 1))
    return jnp.take(mine, jnp.stack(order), axis=0, mode="clip").reshape(-1, panel.shape[1])


def along_col(own):
    me = lax.axis_index("col")
    prv = lax.ppermute(own, "col", [(0, 1), (1, 2), (2, 3)])
    nxt = lax.ppermute(own, "col", [(3, 2), (2, 1), (1, 0)])
    passed = jnp.where(me == 2, prv, jnp.where(me == 1, nxt, own))
    opp = lax.ppermute(passed, "col", [(2, 3), (1, 0), (0, 2), (3, 1)])
    far = lax.ppermute(own, "col", [(0, 3), (3, 0)])
    return [own, prv, nxt, opp, far]


def on_8_by_4(a_panels, a_mask, b_panels, b_mask, owner_map):
    packed, panel_b = pack(a_panels, a_mask, b_panels, b_mask, owner_map, 8, True)
    me = lax.axis_index("row")
    moved = [packed[0]] + [by_row(packed[d], d) for d in range(1, 8)]
    rows = 8 * packed[0].shape[0]
    chunks = [(0, 1), (2, 3, 4, 5), (6, 7)]
    gathered = [along_col(jnp.stack([moved[d] for d in chunk])) for chunk in chunks]
    b_full = gather_b(panel_b)
    out = None
    for chunk, parts in zip(chunks, gathered):
        at = jnp.stack([me ^ d for d in chunk] + [lax.axis_index("col")])
        out = chunk_product(at, parts, b_full, out, rows)
    return out


def on_any(a_panels, a_mask, b_panels, b_mask, owner_map):
    grid_rows = lax.axis_size("row")
    packed, panel_b = pack(a_panels, a_mask, b_panels, b_mask, owner_map, grid_rows, False)
    moved = lax.all_to_all(jnp.stack(packed), "row", split_axis=0, concat_axis=0, tiled=True)
    whole_a = lax.all_gather(moved, "col", axis=2, tiled=True)
    whole_b = lax.all_gather(panel_b, "row", axis=0, tiled=True)
    whole_a = whole_a.reshape(-1, whole_b.shape[0])
    return jnp.dot(whole_a, whole_b, preferred_element_type=jnp.float32).astype(jnp.bfloat16)


def solution(mesh):
    placed = (P("row", "col"), P("row", "col"), P("row", "col"), P("row", "col"), P("row", None))
    sizes = (mesh.shape["row"], mesh.shape["col"])
    return jax.shard_map(
        on_8_by_4 if sizes == (8, 4) else on_any,
        mesh=mesh,
        in_specs=placed,
        out_specs=P("row", "col"),
        check_vma=False,
    )
```

time: 283 us -> 123 us (0.43)
  matrix products: 62.1 us -> 0 us
  blocking collectives: 52.7 us -> 0 us
  waiting for transfers between devices: 83.4 us -> 42.6 us
  Pallas kernels: 0 us -> 20.2 us
  starting transfers between devices: 54.5 us -> 41 us
  local copies, waits for them, and re-layouts: 13.5 us -> 6.19 us
  other arithmetic: 16 us -> 11.6 us
    dot_general x9 -> x0, matrix products: 62.1 us -> none  [the longest x8 56.6 us: product(): jnp.dot(masked_a(panel_a, mask_a), masked_b(panel_b, mask_b), preferred_e...]
    all_to_all x1 -> x0, blocking collectives: 52.7 us -> none  [on_device(): lax.all_to_all(packed, 'row', split_axis=0, concat_axis=0, tiled=True)]
    ppermute x40 -> x22, waiting for transfers between devices: 83.4 us -> 42.6 us  [the longest x10 19 us: by_row(): return lax.ppermute(value, 'row', [(i, i ^ distance) for i in range(count)])]
    pallas_call x0 -> x4, Pallas kernels: none -> 20.2 us  [the longest x3 17.2 us: chunk_product(): pl.pallas_call(dot_kernel, out_shape=jax.ShapeDtypeStruct((rows, cols), j...]
    ppermute x40 -> x22, starting transfers between devices: 54.5 us -> 41 us  [the longest x3 12.6 us: along_col(): far = lax.ppermute(own, 'col', [(0, 3), (3, 0)])]
    reshape x2 -> x0, local copies, waits for them, and re-layouts: 9.66 us -> none  [the longest x1 4.83 us: on_device(): result.reshape(tile_rows, -1)]
    convert_element_type x1 -> x0, other arithmetic: 9.3 us -> none  [on_device(): result = total.astype(jnp.bfloat16)]
    another operation x1 -> x5, other arithmetic: 0.01 us -> 4.65 us  [the longest x3 3.39 us: on_8_by_4(): jnp.stack([moved[d] for d in chunk])]
  transfers between devices with their start and end apart: 40 -> 22, of which waited for: 7 -> 10; matrix products, arithmetic and copies ran while one was open for 21% -> 11% of each run, Pallas kernels for 0% -> 10%
where the time goes in v1:
time: 123 us; the launch traced here: 122 us
  waiting for transfers between devices  42.6 us (35%)
  starting transfers between devices  41 us (33%)
  Pallas kernels  20.2 us (16%)
  other arithmetic  11.6 us (9%)
  local copies, waits for them, and re-layouts  6.19 us (5%)
    ppermute x10, waiting for transfers between devices, by_row(): return lax.ppermute(value, 'row', [(i, i ^ distance) for i in range(count)])  19 us
    pallas_call x3, Pallas kernels, chunk_product(): pl.pallas_call(dot_kernel, out_shape=jax.ShapeDtypeStruct((rows, cols), j...  17.2 us
    ppermute x3, waiting for transfers between devices, along_col(): prv = lax.ppermute(own, 'col', [(0, 1), (1, 2), (2, 3)])  16 us
    ppermute x3, starting transfers between devices, along_col(): far = lax.ppermute(own, 'col', [(0, 3), (3, 0)])  12.6 us
    ppermute x10, starting transfers between devices, by_row(): return lax.ppermute(value, 'row', [(i, i ^ distance) for i in range(count)])  11.3 us
    ppermute x3, starting transfers between devices, along_col(): prv = lax.ppermute(own, 'col', [(0, 1), (1, 2), (2, 3)])  9.23 us
    ppermute x3, waiting for transfers between devices, along_col(): opp = lax.ppermute(passed, 'col', [(2, 3), (1, 0), (0, 2), (3, 1)])  6.19 us
    ppermute x3, starting transfers between devices, along_col(): opp = lax.ppermute(passed, 'col', [(2, 3), (1, 0), (0, 2), (3, 1)])  4.01 us
  transfers between devices with their start and end apart: 22, of which 10 were waited for; matrix products, arithmetic and copies ran while one was open for 11% of the time, Pallas kernels for 10%

profile of v1, /device:TPU:0, one launch (start us, length us, event | category | flops | bytes accessed | tf_op | source)
XLA Modules:
  0.0 121.9 jit_solution(2232323878927669528)
XLA Ops:
  0.0 1.3 %copy.8.owner_ref = s32[16,1]{1,0:T(8,128)} copy(s32[16,1]{0,1:T(1,128)} %param.9) | data formatting | bytes 128 | tf_op args[4]
  1.3 1.3 %copy.9.am_ref = s32[16,2]{1,0:T(8,128)} copy(s32[16,2]{0,1:T(2,128)} %param.6) | data formatting | bytes 256 | tf_op args[1]
  2.7 3.0 %pack.1 = (bf16[256,256]{1,0:T(8,128)(2,1)}, bf16[256,256]{1,0:T(8,128)(2,1)}, bf16[256,256]{1,0:T(8,128)(2,1)}, bf16[256,256]{1,0:T(8,128)(2,1)}, bf16[256,256]...) custom-call(s32[16,1]{1,0:T(8,128)} %copy.8.owner_ref, ...), custom_call_target="tpu_custom_call" | custom-call | tf_op jit(solution)/shard_map/pack/pallas_call | solution.py:63
  5.7 3.0 %collective-permute-start.6 = (bf16[1,128,1024]{2,1,0:T(8,128)(2,1)}, bf16[1,128,1024]{2,1,0:T(8,128)(2,1)S(1)}, u32[]{:S(2)}, u32[]{:S(2)}) collective-permute-start(bf16[1,128,1024]{2,1,0:T(8,128)(2,1)} %bitcast.30), channel_id=1, source_target_pairs={{0,8},{4,12},{8,0},{12,4},{16,24},{20,28},{24,16},{28,20},{1,9},{5... | collective-permute-start | bytes 786440 | tf_op jit(solution)/shard_map/ppermute | solution.py:126
  8.6 6.6 %collective-permute-done.6 = bf16[1,128,1024]{2,1,0:T(8,128)(2,1)S(1)} collective-permute-done((bf16[1,128,1024]{2,1,0:T(8,128)(2,1)}, bf16[1,128,1024]{2,1,0:T(8,128)(2,1)S(1)}, u32[]{:S(2)}, u32[]{:S(2)}) %collective-permute-start.6) | collective-permute-done | bytes 262176 | tf_op jit(solution)/shard_map/ppermute | solution.py:126
  15.2 1.0 pad_maximum_fusion.2
  16.2 1.8 %collective-permute-start.7 = (bf16[2,128,1024]{2,1,0:T(8,128)(2,1)S(1)}, bf16[2,128,1024]{2,1,0:T(8,128)(2,1)S(1)}, u32[]{:S(2)}, u32[]{:S(2)}) collective-permute-start(bf16[2,128,1024]{2,1,0:T(8,128)(2,1)S(1)} %pad_maximum_fusion.2), channel_id=1, source_target_pairs={{0,16},{4,20},{8,24},{12,28},{16,0},{20,4},{24,8},{28,12},{1,17},{... | collective-permute-start | bytes 1572872 | tf_op jit(solution)/shard_map/ppermute | solution.py:126
  18.0 0.0 collective-permute-start.17
  18.0 1.5 %collective-permute-start.9 = (bf16[256,256]{1,0:T(8,128)(2,1)}, bf16[256,256]{1,0:T(8,128)(2,1)S(1)}, u32[]{:S(2)}, u32[]{:S(2)}) collective-permute-start(bf16[256,256]{1,0:T(8,128)(2,1)} %get-tuple-element.17), channel_id=1, source_target_pairs={{0,8},{4,12},{8,0},{12,4},{16,24},{20,28},{24,16},{28,20},{1,9},{5... | collective-permute-start | bytes 393224 | tf_op jit(solution)/shard_map/ppermute | solution.py:126
  19.5 0.4 collective-permute-start.10
  19.9 0.3 collective-permute-start.11
  20.2 0.0 collective-permute-done.17
  20.2 1.3 %collective-permute-start.12 = (bf16[256,256]{1,0:T(8,128)(2,1)}, bf16[256,256]{1,0:T(8,128)(2,1)}, u32[]{:S(2)}, u32[]{:S(2)}) collective-permute-start(bf16[256,256]{1,0:T(8,128)(2,1)} %get-tuple-element.20), channel_id=1, source_target_pairs={{0,20},{4,16},{8,28},{12,24},{16,4},{20,0},{24,12},{28,8},{1,21},{... | collective-permute-start | bytes 393224 | tf_op jit(solution)/shard_map/ppermute | solution.py:126
  21.5 0.6 add_add_fusion.1.at_ref
  22.2 1.7 %pad_maximum_fusion.5.own_ref = bf16[2,256,256]{2,1,0:T(8,128)(2,1)} fusion(bf16[1,256,256]{2,1,0:T(8,128)(2,1)S(1)} %bitcast.36, bf16[1,256,256]{2,1,0:T(8,128)(2,1)} %bitcast.34), kind=kLoop, calls=%fused_computation.7 | loop fusion | flops 131072 | bytes 524288 | tf_op jit(solution)/shard_map/stack | solution.py:157
  23.9 0.7 collective-permute-done.9
  24.5 1.4 %collective-permute-start = (bf16[256,256]{1,0:T(8,128)(2,1)}, bf16[256,256]{1,0:T(8,128)(2,1)S(1)}, u32[]{:S(2)}, u32[]{:S(2)}) collective-permute-start(bf16[256,256]{1,0:T(8,128)(2,1)} %get-tuple-element.14), channel_id=1, source_target_pairs={{0,24},{4,28},{8,16},{12,20},{16,8},{20,12},{24,0},{28,4},{1,25},{... | collective-permute-start | bytes 393224 | tf_op jit(solution)/shard_map/ppermute | solution.py:126
  25.9 0.6 collective-permute-done.10
  26.5 1.5 %collective-permute-start.1 = (bf16[256,256]{1,0:T(8,128)(2,1)}, bf16[256,256]{1,0:T(8,128)(2,1)S(1)}, u32[]{:S(2)}, u32[]{:S(2)}) collective-permute-start(bf16[256,256]{1,0:T(8,128)(2,1)} %get-tuple-element.15), channel_id=1, source_target_pairs={{0,28},{4,24},{8,20},{12,16},{16,12},{20,8},{24,4},{28,0},{1,29},{... | collective-permute-start | bytes 393224 | tf_op jit(solution)/shard_map/ppermute | solution.py:126
  28.1 11.1 %collective-permute-done.11 = bf16[256,256]{1,0:T(8,128)(2,1)S(1)} collective-permute-done((bf16[256,256]{1,0:T(8,128)(2,1)}, bf16[256,256]{1,0:T(8,128)(2,1)S(1)}, u32[]{:S(2)}, u32[]{:S(2)}) %collective-permute-start.11) | collective-permute-done | bytes 131104 | tf_op jit(solution)/shard_map/ppermute | solution.py:126
  39.2 3.4 %collective-permute-start.18 = (bf16[2,256,256]{2,1,0:T(8,128)(2,1)}, bf16[2,256,256]{2,1,0:T(8,128)(2,1)S(1)}, u32[]{:S(2)}, u32[]{:S(2)}) collective-permute-start(bf16[2,256,256]{2,1,0:T(8,128)(2,1)} %pad_maximum_fusion.5.own_ref), channel_id=1, source_target_pairs={{0,1},{1,2},{2,3},{4,5},{5,6},{6,7},{8,9},{9,10},{10,11},{12,13},{... | collective-permute-start | bytes 786440 | tf_op jit(solution)/shard_map/ppermute | solution.py:143
  42.6 0.0 collective-permute-done.12
  42.6 1.3 %collective-permute-start.19 = (bf16[2,256,256]{2,1,0:T(8,128)(2,1)}, bf16[2,256,256]{2,1,0:T(8,128)(2,1)S(1)}, u32[]{:S(2)}, u32[]{:S(2)}) collective-permute-start(bf16[2,256,256]{2,1,0:T(8,128)(2,1)} %pad_maximum_fusion.5.own_ref), channel_id=1, source_target_pairs={{3,2},{2,1},{1,0},{7,6},{6,5},{5,4},{11,10},{10,9},{9,8},{15,14},{... | collective-permute-start | bytes 786440 | tf_op jit(solution)/shard_map/ppermute | solution.py:144
  43.9 1.0 pad_maximum_fusion.3.own_ref
  44.9 0.0 collective-permute-done.7
  44.9 4.6 %collective-permute-start.13 = (bf16[4,256,256]{2,1,0:T(8,128)(2,1)S(1)}, bf16[4,256,256]{2,1,0:T(8,128)(2,1)S(1)}, u32[]{:S(2)}, u32[]{:S(2)}) collective-permute-start(bf16[4,256,256]{2,1,0:T(8,128)(2,1)S(1)} %pad_maximum_fusion.3.own_ref), channel_id=1, source_target_pairs={{0,1},{1,2},{2,3},{4,5},{5,6},{6,7},{8,9},{9,10},{10,11},{12,13},{... | collective-permute-start | bytes 1572872 | tf_op jit(solution)/shard_map/ppermute | solution.py:143
  49.5 1.1 pad_maximum_fusion.1
  50.6 0.0 collective-permute-done
  50.6 1.3 %collective-permute-start.14 = (bf16[4,256,256]{2,1,0:T(8,128)(2,1)S(1)}, bf16[4,256,256]{2,1,0:T(8,128)(2,1)S(1)}, u32[]{:S(2)}, u32[]{:S(2)}) collective-permute-start(bf16[4,256,256]{2,1,0:T(8,128)(2,1)S(1)} %pad_maximum_fusion.3.own_ref), channel_id=1, source_target_pairs={{3,2},{2,1},{1,0},{7,6},{6,5},{5,4},{11,10},{10,9},{9,8},{15,14},{... | collective-permute-start | bytes 1572872 | tf_op jit(solution)/shard_map/ppermute | solution.py:144
  51.9 0.0 collective-permute-done.1
  51.9 0.1 collective-permute-start.8
  52.0 0.6 add_add_fusion.at_ref
  52.6 0.6 stack.118.at_ref
  53.2 0.1 stack.113
  53.3 0.7 pad_maximum_fusion.4.own_ref
  54.0 0.0 collective-permute-done.18.prv_ref
  54.0 6.7 %collective-permute-start.21 = (bf16[2,256,256]{2,1,0:T(8,128)(2,1)}, bf16[2,256,256]{2,1,0:T(8,128)(2,1)}, u32[]{:S(2)}, u32[]{:S(2)}) collective-permute-start(bf16[2,256,256]{2,1,0:T(8,128)(2,1)} %pad_maximum_fusion.5.own_ref), channel_id=1, source_target_pairs={{0,3},{3,0},{4,7},{7,4},{8,11},{11,8},{12,15},{15,12},{16,19},{19,... | collective-permute-start | bytes 786440 | tf_op jit(solution)/shard_map/ppermute | solution.py:147
  60.7 0.0 collective-permute-done.19.nxt_ref
  60.8 1.9 %collective-permute-start.16 = (bf16[4,256,256]{2,1,0:T(8,128)(2,1)S(1)}, bf16[4,256,256]{2,1,0:T(8,128)(2,1)}, u32[]{:S(2)}, u32[]{:S(2)}) collective-permute-start(bf16[4,256,256]{2,1,0:T(8,128)(2,1)S(1)} %pad_maximum_fusion.3.own_ref), channel_id=1, source_target_pairs={{0,3},{3,0},{4,7},{7,4},{8,11},{11,8},{12,15},{15,12},{16,19},{19,... | collective-permute-start | bytes 1572872 | tf_op jit(solution)/shard_map/ppermute | solution.py:147
  62.7 0.7 select_select_fusion.1
  63.4 0.0 collective-permute-done.13.prv_ref
  63.4 1.3 %collective-permute-start.2 = (bf16[2,256,256]{2,1,0:T(8,128)(2,1)}, bf16[2,256,256]{2,1,0:T(8,128)(2,1)S(1)}, u32[]{:S(2)}, u32[]{:S(2)}) collective-permute-start(bf16[2,256,256]{2,1,0:T(8,128)(2,1)} %pad_maximum_fusion.4.own_ref), channel_id=1, source_target_pairs={{0,1},{1,2},{2,3},{4,5},{5,6},{6,7},{8,9},{9,10},{10,11},{12,13},{... | collective-permute-start | bytes 786440 | tf_op jit(solution)/shard_map/ppermute | solution.py:143
  64.8 0.2 collective-permute-done.14.nxt_ref
  65.0 1.3 %collective-permute-start.3 = (bf16[2,256,256]{2,1,0:T(8,128)(2,1)}, bf16[2,256,256]{2,1,0:T(8,128)(2,1)S(1)}, u32[]{:S(2)}, u32[]{:S(2)}) collective-permute-start(bf16[2,256,256]{2,1,0:T(8,128)(2,1)} %pad_maximum_fusion.4.own_ref), channel_id=1, source_target_pairs={{3,2},{2,1},{1,0},{7,6},{6,5},{5,4},{11,10},{10,9},{9,8},{15,14},{... | collective-permute-start | bytes 786440 | tf_op jit(solution)/shard_map/ppermute | solution.py:144
  66.3 1.9 %select_select_fusion = bf16[4,256,256]{2,1,0:T(8,128)(2,1)} fusion(bf16[4,256,256]{2,1,0:T(8,128)(2,1)S(1)} %collective-permute-done.13.prv_ref, bf16[4,256,256]{2,1,0:T(8,128)(2,1)S(1)} %collective-permute-done.14.nxt_ref, pred[]{:T(512)S(6)} %eq.5, pred[]{:T(512)S(6)} %eq.4, bf16[1,256,256]{2,1,0:T(8,128)(2,1)} %bitcast.22, ...), kind=kLoop, calls=%fused_computation.5 | loop fusion | flops 1310720 | bytes 2097154 | tf_op jit(solution)/shard_map/jit(_where)/select_n | solution.py:145
  68.2 16.0 %collective-permute-done.2.prv_ref = bf16[2,256,256]{2,1,0:T(8,128)(2,1)S(1)} collective-permute-done((bf16[2,256,256]{2,1,0:T(8,128)(2,1)}, bf16[2,256,256]{2,1,0:T(8,128)(2,1)S(1)}, u32[]{:S(2)}, u32[]{:S(2)}) %collective-permute-start.2) | collective-permute-done | bytes 262176 | tf_op jit(solution)/shard_map/ppermute | solution.py:143
  84.2 3.2 %collective-permute-start.20 = (bf16[2,256,256]{2,1,0:T(8,128)(2,1)}, bf16[2,256,256]{2,1,0:T(8,128)(2,1)}, u32[]{:S(2)}, u32[]{:S(2)}) collective-permute-start(bf16[2,256,256]{2,1,0:T(8,128)(2,1)} %select_select_fusion.1), channel_id=1, source_target_pairs={{2,3},{1,0},{0,2},{3,1},{6,7},{5,4},{4,6},{7,5},{10,11},{9,8},{8,1... | collective-permute-start | bytes 786440 | tf_op jit(solution)/shard_map/ppermute | solution.py:146
  87.4 0.7 collective-permute-done.3.nxt_ref
  88.1 0.8 collective-permute-start.15
  89.0 0.8 select_select_fusion.2
  89.8 0.0 collective-permute-done.8
  89.8 4.0 %collective-permute-start.5 = (bf16[2,256,256]{2,1,0:T(8,128)(2,1)}, bf16[2,256,256]{2,1,0:T(8,128)(2,1)S(1)}, u32[]{:S(2)}, u32[]{:S(2)}) collective-permute-start(bf16[2,256,256]{2,1,0:T(8,128)(2,1)} %pad_maximum_fusion.4.own_ref), channel_id=1, source_target_pairs={{0,3},{3,0},{4,7},{7,4},{8,11},{11,8},{12,15},{15,12},{16,19},{19,... | collective-permute-start | bytes 786440 | tf_op jit(solution)/shard_map/ppermute | solution.py:147
  93.8 1.4 %pad_maximum_fusion = bf16[8,128,1024]{2,1,0:T(8,128)(2,1)S(1)} fusion(bf16[4,128,1024]{2,1,0:T(8,128)(2,1)} %collective-permute-done.8, bf16[2,128,1024]{2,1,0:T(8,128)(2,1)S(1)} %copy-done.5, bf16[1,128,1024]{2,1,0:T(8,128)(2,1)S(1)} %collective-permute-done.6, bf16[1,128,1024]{2,1,0:T(8,128)(2,1)S(1)} %bitcast.33), kind=kLoop, calls=%fused_computation.1 | loop fusion | flops 3145728 | bytes 4194304 | tf_op jit(solution)/shard_map/concatenate | solution.py:132
  95.2 2.0 %gather_fusion = bf16[8,128,1024]{2,1,0:T(8,128)(2,1)} fusion(bf16[8,128,1024]{2,1,0:T(8,128)(2,1)S(1)} %pad_maximum_fusion, s32[1024]{0:T(1024)S(1)} %pad_clamp_fusion), kind=kCustom, calls=%fused_computation | custom fusion | bytes 4194336 | tf_op jit(solution)/shard_map/jit(_take)/gather | solution.py:138
  97.3 0.0 collective-permute-done.21.far_ref
  97.3 0.0 collective-permute-done.20.opp_ref
  97.3 5.0 %chunk_product.3.rest_0_ = bf16[2048,1024]{1,0:T(8,128)(2,1)} custom-call(s32[3]{0:T(128)} %add_add_fusion.1.at_ref, bf16[2,256,256]{2,1,0:T(8,128)(2,1)} %pad_maximum_fusion.5.own_ref, bf16[2,256,256]{2,1,0:T(8,128)(2,1)} %copy-done.6, bf16[2,256,256]{2,1,0:T(8,128)(2,1)} %copy-done.7, bf16[2,256,256]{2,1,0:T(8,128)(2,1)} %collective-permute-done.20.opp_ref, ...), custom_call_target="tpu_custom_call" | custom-call | flops 1073741824 | bytes 4194304 | tf_op jit(solution)/shard_map/chunk_product/pallas_call | solution.py:106
  102.3 0.0 collective-permute-done.16.far_ref
  102.3 3.3 %collective-permute-done.15.opp_ref = bf16[4,256,256]{2,1,0:T(8,128)(2,1)} collective-permute-done((bf16[4,256,256]{2,1,0:T(8,128)(2,1)}, bf16[4,256,256]{2,1,0:T(8,128)(2,1)}, u32[]{:S(2)}, u32[]{:S(2)}) %collective-permute-start.15) | collective-permute-done | bytes 524320 | tf_op jit(solution)/shard_map/ppermute | solution.py:146
  105.6 7.1 %chunk_product.4.rest_0_ = bf16[2048,1024]{1,0:T(8,128)(2,1)} custom-call(s32[5]{0:T(128)} %stack.118.at_ref, bf16[4,256,256]{2,1,0:T(8,128)(2,1)} %copy-done.1, bf16[4,256,256]{2,1,0:T(8,128)(2,1)} %copy-done.2, bf16[4,256,256]{2,1,0:T(8,128)(2,1)} %copy-done.3, ...), custom_call_target="tpu_custom_call", output_to_operand_aliasing={{}: (7, {})} | custom-call | flops 2147483648 | bytes 4194304 | tf_op jit(solution)/shard_map/chunk_product/pallas_call | solution.py:106
  112.8 0.5 collective-permute-done.5.far_ref
  113.2 2.9 %collective-permute-done.4.opp_ref = bf16[2,256,256]{2,1,0:T(8,128)(2,1)S(1)} collective-permute-done((bf16[2,256,256]{2,1,0:T(8,128)(2,1)S(1)}, bf16[2,256,256]{2,1,0:T(8,128)(2,1)S(1)}, u32[]{:S(2)}, u32[]{:S(2)}) %collective-permute-start.4) | collective-permute-done | bytes 262176 | tf_op jit(solution)/shard_map/ppermute | solution.py:146
  116.1 0.7 copy-done.15
  116.8 5.0 %chunk_product.5 = bf16[2048,1024]{1,0:T(8,128)(2,1)} custom-call(s32[3]{0:T(128)} %add_add_fusion.at_ref, bf16[2,256,256]{2,1,0:T(8,128)(2,1)} %pad_maximum_fusion.4.own_ref, bf16[2,256,256]{2,1,0:T(8,128)(2,1)} %copy-done.8, bf16[2,256,256]{2,1,0:T(8,128)(2,1)} %copy-done.9, bf16[2,256,256]{2,1,0:T(8,128)(2,1)} %copy-done.15, ...), custom_call_target="tpu_custom_call", output_to_operand_aliasing={{}: (7, {})} | custom-call | flops 1073741824 | bytes 4194304 | tf_op jit(solution)/shard_map/chunk_product/pallas_call | solution.py:106
  (33 shorter events, 0.1 us)
Async XLA Ops:
  5.7 43.8 %copy-start = (bf16[128,1024]{1,0:T(8,128)(2,1)S(1)}, bf16[128,1024]{1,0:T(8,128)(2,1)}, u32[]{:S(2)}) copy-start(bf16[128,1024]{1,0:T(8,128)(2,1)} %get-tuple-element.16) | copy-start | bytes 786436
  5.7 9.5 %collective-permute-start.6 = (bf16[1,128,1024]{2,1,0:T(8,128)(2,1)}, bf16[1,128,1024]{2,1,0:T(8,128)(2,1)S(1)}, u32[]{:S(2)}, u32[]{:S(2)}) collective-permute-start(bf16[1,128,1024]{2,1,0:T(8,128)(2,1)} %bitcast.30), channel_id=1, source_target_pairs={{0,8},{4,12},{8,0},{12,4},{16,24},{20,28},{24,16},{28,20},{1,9},{5... | collective-permute-start | bytes 786440 | tf_op jit(solution)/shard_map/ppermute | solution.py:126
  16.2 28.7 %collective-permute-start.7 = (bf16[2,128,1024]{2,1,0:T(8,128)(2,1)S(1)}, bf16[2,128,1024]{2,1,0:T(8,128)(2,1)S(1)}, u32[]{:S(2)}, u32[]{:S(2)}) collective-permute-start(bf16[2,128,1024]{2,1,0:T(8,128)(2,1)S(1)} %pad_maximum_fusion.2), channel_id=1, source_target_pairs={{0,16},{4,20},{8,24},{12,28},{16,0},{20,4},{24,8},{28,12},{1,17},{... | collective-permute-start | bytes 1572872 | tf_op jit(solution)/shard_map/ppermute | solution.py:126
  18.0 2.2 %collective-permute-start.17 = (bf16[256,256]{1,0:T(8,128)(2,1)}, bf16[256,256]{1,0:T(8,128)(2,1)S(1)}, u32[]{:S(2)}, u32[]{:S(2)}) collective-permute-start(bf16[256,256]{1,0:T(8,128)(2,1)} %get-tuple-element.22), channel_id=1, source_target_pairs={{0,4},{4,0},{8,12},{12,8},{16,20},{20,16},{24,28},{28,24},{1,5},{5... | collective-permute-start | bytes 393224 | tf_op jit(solution)/shard_map/ppermute | solution.py:126
  18.0 6.5 %collective-permute-start.9 = (bf16[256,256]{1,0:T(8,128)(2,1)}, bf16[256,256]{1,0:T(8,128)(2,1)S(1)}, u32[]{:S(2)}, u32[]{:S(2)}) collective-permute-start(bf16[256,256]{1,0:T(8,128)(2,1)} %get-tuple-element.17), channel_id=1, source_target_pairs={{0,8},{4,12},{8,0},{12,4},{16,24},{20,28},{24,16},{28,20},{1,9},{5... | collective-permute-start | bytes 393224 | tf_op jit(solution)/shard_map/ppermute | solution.py:126
  19.5 7.0 %collective-permute-start.10 = (bf16[256,256]{1,0:T(8,128)(2,1)}, bf16[256,256]{1,0:T(8,128)(2,1)S(1)}, u32[]{:S(2)}, u32[]{:S(2)}) collective-permute-start(bf16[256,256]{1,0:T(8,128)(2,1)} %get-tuple-element.18), channel_id=1, source_target_pairs={{0,12},{4,8},{8,4},{12,0},{16,28},{20,24},{24,20},{28,16},{1,13},{... | collective-permute-start | bytes 393224 | tf_op jit(solution)/shard_map/ppermute | solution.py:126
  19.9 19.4 %collective-permute-start.11 = (bf16[256,256]{1,0:T(8,128)(2,1)}, bf16[256,256]{1,0:T(8,128)(2,1)S(1)}, u32[]{:S(2)}, u32[]{:S(2)}) collective-permute-start(bf16[256,256]{1,0:T(8,128)(2,1)} %get-tuple-element.19), channel_id=1, source_target_pairs={{0,16},{4,20},{8,24},{12,28},{16,0},{20,4},{24,8},{28,12},{1,17},{... | collective-permute-start | bytes 393224 | tf_op jit(solution)/shard_map/ppermute | solution.py:126
  20.2 22.4 %collective-permute-start.12 = (bf16[256,256]{1,0:T(8,128)(2,1)}, bf16[256,256]{1,0:T(8,128)(2,1)}, u32[]{:S(2)}, u32[]{:S(2)}) collective-permute-start(bf16[256,256]{1,0:T(8,128)(2,1)} %get-tuple-element.20), channel_id=1, source_target_pairs={{0,20},{4,16},{8,28},{12,24},{16,4},{20,0},{24,12},{28,8},{1,21},{... | collective-permute-start | bytes 393224 | tf_op jit(solution)/shard_map/ppermute | solution.py:126
  22.2 40.5 %copy-start.10 = (bf16[256,256]{1,0:T(8,128)(2,1)S(1)}, bf16[256,256]{1,0:T(8,128)(2,1)}, u32[]{:S(2)}) copy-start(bf16[256,256]{1,0:T(8,128)(2,1)} %get-tuple-element.21) | copy-start | bytes 393220
  24.5 26.1 %collective-permute-start = (bf16[256,256]{1,0:T(8,128)(2,1)}, bf16[256,256]{1,0:T(8,128)(2,1)S(1)}, u32[]{:S(2)}, u32[]{:S(2)}) collective-permute-start(bf16[256,256]{1,0:T(8,128)(2,1)} %get-tuple-element.14), channel_id=1, source_target_pairs={{0,24},{4,28},{8,16},{12,20},{16,8},{20,12},{24,0},{28,4},{1,25},{... | collective-permute-start | bytes 393224 | tf_op jit(solution)/shard_map/ppermute | solution.py:126
  26.5 38.2 %copy-start.11 = (bf16[256,256]{1,0:T(8,128)(2,1)}, bf16[256,256]{1,0:T(8,128)(2,1)S(1)}, u32[]{:S(2)}) copy-start(bf16[256,256]{1,0:T(8,128)(2,1)S(1)} %collective-permute-done.10) | copy-start | bytes 393220
  26.5 25.3 %collective-permute-start.1 = (bf16[256,256]{1,0:T(8,128)(2,1)}, bf16[256,256]{1,0:T(8,128)(2,1)S(1)}, u32[]{:S(2)}, u32[]{:S(2)}) collective-permute-start(bf16[256,256]{1,0:T(8,128)(2,1)} %get-tuple-element.15), channel_id=1, source_target_pairs={{0,28},{4,24},{8,20},{12,16},{16,12},{20,8},{24,4},{28,0},{1,29},{... | collective-permute-start | bytes 393224 | tf_op jit(solution)/shard_map/ppermute | solution.py:126
  39.2 25.5 %copy-start.12 = (bf16[256,256]{1,0:T(8,128)(2,1)}, bf16[256,256]{1,0:T(8,128)(2,1)S(1)}, u32[]{:S(2)}) copy-start(bf16[256,256]{1,0:T(8,128)(2,1)S(1)} %collective-permute-done.11) | copy-start | bytes 393220
  39.2 14.8 %collective-permute-start.18 = (bf16[2,256,256]{2,1,0:T(8,128)(2,1)}, bf16[2,256,256]{2,1,0:T(8,128)(2,1)S(1)}, u32[]{:S(2)}, u32[]{:S(2)}) collective-permute-start(bf16[2,256,256]{2,1,0:T(8,128)(2,1)} %pad_maximum_fusion.5.own_ref), channel_id=1, source_target_pairs={{0,1},{1,2},{2,3},{4,5},{5,6},{6,7},{8,9},{9,10},{10,11},{12,13},{... | collective-permute-start | bytes 786440 | tf_op jit(solution)/shard_map/ppermute | solution.py:143
  42.6 18.1 %collective-permute-start.19 = (bf16[2,256,256]{2,1,0:T(8,128)(2,1)}, bf16[2,256,256]{2,1,0:T(8,128)(2,1)S(1)}, u32[]{:S(2)}, u32[]{:S(2)}) collective-permute-start(bf16[2,256,256]{2,1,0:T(8,128)(2,1)} %pad_maximum_fusion.5.own_ref), channel_id=1, source_target_pairs={{3,2},{2,1},{1,0},{7,6},{6,5},{5,4},{11,10},{10,9},{9,8},{15,14},{... | collective-permute-start | bytes 786440 | tf_op jit(solution)/shard_map/ppermute | solution.py:144
  44.9 23.4 %copy-start.1 = (bf16[4,256,256]{2,1,0:T(8,128)(2,1)}, bf16[4,256,256]{2,1,0:T(8,128)(2,1)S(1)}, u32[]{:S(2)}) copy-start(bf16[4,256,256]{2,1,0:T(8,128)(2,1)S(1)} %pad_maximum_fusion.3.own_ref) | copy-start | bytes 1572868
  44.9 5.7 %copy-start.4 = (bf16[2,128,1024]{2,1,0:T(8,128)(2,1)}, bf16[2,128,1024]{2,1,0:T(8,128)(2,1)S(1)}, u32[]{:S(2)}) copy-start(bf16[2,128,1024]{2,1,0:T(8,128)(2,1)S(1)} %collective-permute-done.7) | copy-start | bytes 1572868
  44.9 18.5 %collective-permute-start.13 = (bf16[4,256,256]{2,1,0:T(8,128)(2,1)S(1)}, bf16[4,256,256]{2,1,0:T(8,128)(2,1)S(1)}, u32[]{:S(2)}, u32[]{:S(2)}) collective-permute-start(bf16[4,256,256]{2,1,0:T(8,128)(2,1)S(1)} %pad_maximum_fusion.3.own_ref), channel_id=1, source_target_pairs={{0,1},{1,2},{2,3},{4,5},{5,6},{6,7},{8,9},{9,10},{10,11},{12,13},{... | collective-permute-start | bytes 1572872 | tf_op jit(solution)/shard_map/ppermute | solution.py:143
  50.6 14.4 %collective-permute-start.14 = (bf16[4,256,256]{2,1,0:T(8,128)(2,1)S(1)}, bf16[4,256,256]{2,1,0:T(8,128)(2,1)S(1)}, u32[]{:S(2)}, u32[]{:S(2)}) collective-permute-start(bf16[4,256,256]{2,1,0:T(8,128)(2,1)S(1)} %pad_maximum_fusion.3.own_ref), channel_id=1, source_target_pairs={{3,2},{2,1},{1,0},{7,6},{6,5},{5,4},{11,10},{10,9},{9,8},{15,14},{... | collective-permute-start | bytes 1572872 | tf_op jit(solution)/shard_map/ppermute | solution.py:144
  51.9 37.9 %collective-permute-start.8 = (bf16[4,128,1024]{2,1,0:T(8,128)(2,1)}, bf16[4,128,1024]{2,1,0:T(8,128)(2,1)}, u32[]{:S(2)}, u32[]{:S(2)}) collective-permute-start(bf16[4,128,1024]{2,1,0:T(8,128)(2,1)} %pad_maximum_fusion.1), channel_id=1, source_target_pairs={{0,4},{4,0},{8,12},{12,8},{16,20},{20,16},{24,28},{28,24},{1,5},{5... | collective-permute-start | bytes 3145736 | tf_op jit(solution)/shard_map/ppermute | solution.py:126
  54.0 39.7 %copy-start.5 = (bf16[2,128,1024]{2,1,0:T(8,128)(2,1)S(1)}, bf16[2,128,1024]{2,1,0:T(8,128)(2,1)}, u32[]{:S(2)}) copy-start(bf16[2,128,1024]{2,1,0:T(8,128)(2,1)} %copy-done.4) | copy-start | bytes 1572868
  54.0 35.7 %copy-start.6 = (bf16[2,256,256]{2,1,0:T(8,128)(2,1)}, bf16[2,256,256]{2,1,0:T(8,128)(2,1)S(1)}, u32[]{:S(2)}) copy-start(bf16[2,256,256]{2,1,0:T(8,128)(2,1)S(1)} %collective-permute-done.18.prv_ref) | copy-start | bytes 786436
  54.0 43.2 %collective-permute-start.21 = (bf16[2,256,256]{2,1,0:T(8,128)(2,1)}, bf16[2,256,256]{2,1,0:T(8,128)(2,1)}, u32[]{:S(2)}, u32[]{:S(2)}) collective-permute-start(bf16[2,256,256]{2,1,0:T(8,128)(2,1)} %pad_maximum_fusion.5.own_ref), channel_id=1, source_target_pairs={{0,3},{3,0},{4,7},{7,4},{8,11},{11,8},{12,15},{15,12},{16,19},{19,... | collective-permute-start | bytes 786440 | tf_op jit(solution)/shard_map/ppermute | solution.py:147
  60.8 29.0 %copy-start.7 = (bf16[2,256,256]{2,1,0:T(8,128)(2,1)}, bf16[2,256,256]{2,1,0:T(8,128)(2,1)S(1)}, u32[]{:S(2)}) copy-start(bf16[2,256,256]{2,1,0:T(8,128)(2,1)S(1)} %collective-permute-done.19.nxt_ref) | copy-start | bytes 786436
  60.8 41.6 %collective-permute-start.16 = (bf16[4,256,256]{2,1,0:T(8,128)(2,1)S(1)}, bf16[4,256,256]{2,1,0:T(8,128)(2,1)}, u32[]{:S(2)}, u32[]{:S(2)}) collective-permute-start(bf16[4,256,256]{2,1,0:T(8,128)(2,1)S(1)} %pad_maximum_fusion.3.own_ref), channel_id=1, source_target_pairs={{0,3},{3,0},{4,7},{7,4},{8,11},{11,8},{12,15},{15,12},{16,19},{19,... | collective-permute-start | bytes 1572872 | tf_op jit(solution)/shard_map/ppermute | solution.py:147
  63.4 26.3 %copy-start.2 = (bf16[4,256,256]{2,1,0:T(8,128)(2,1)}, bf16[4,256,256]{2,1,0:T(8,128)(2,1)S(1)}, u32[]{:S(2)}) copy-start(bf16[4,256,256]{2,1,0:T(8,128)(2,1)S(1)} %collective-permute-done.13.prv_ref) | copy-start | bytes 1572868
  63.4 20.8 %collective-permute-start.2 = (bf16[2,256,256]{2,1,0:T(8,128)(2,1)}, bf16[2,256,256]{2,1,0:T(8,128)(2,1)S(1)}, u32[]{:S(2)}, u32[]{:S(2)}) collective-permute-start(bf16[2,256,256]{2,1,0:T(8,128)(2,1)} %pad_maximum_fusion.4.own_ref), channel_id=1, source_target_pairs={{0,1},{1,2},{2,3},{4,5},{5,6},{6,7},{8,9},{9,10},{10,11},{12,13},{... | collective-permute-start | bytes 786440 | tf_op jit(solution)/shard_map/ppermute | solution.py:143
  65.0 24.8 %copy-start.3 = (bf16[4,256,256]{2,1,0:T(8,128)(2,1)}, bf16[4,256,256]{2,1,0:T(8,128)(2,1)S(1)}, u32[]{:S(2)}) copy-start(bf16[4,256,256]{2,1,0:T(8,128)(2,1)S(1)} %collective-permute-done.14.nxt_ref) | copy-start | bytes 1572868
  65.0 23.1 %collective-permute-start.3 = (bf16[2,256,256]{2,1,0:T(8,128)(2,1)}, bf16[2,256,256]{2,1,0:T(8,128)(2,1)S(1)}, u32[]{:S(2)}, u32[]{:S(2)}) collective-permute-start(bf16[2,256,256]{2,1,0:T(8,128)(2,1)} %pad_maximum_fusion.4.own_ref), channel_id=1, source_target_pairs={{3,2},{2,1},{1,0},{7,6},{6,5},{5,4},{11,10},{10,9},{9,8},{15,14},{... | collective-permute-start | bytes 786440 | tf_op jit(solution)/shard_map/ppermute | solution.py:144
  84.2 5.6 %copy-start.8 = (bf16[2,256,256]{2,1,0:T(8,128)(2,1)}, bf16[2,256,256]{2,1,0:T(8,128)(2,1)S(1)}, u32[]{:S(2)}) copy-start(bf16[2,256,256]{2,1,0:T(8,128)(2,1)S(1)} %collective-permute-done.2.prv_ref) | copy-start | bytes 786436
  84.2 13.1 %collective-permute-start.20 = (bf16[2,256,256]{2,1,0:T(8,128)(2,1)}, bf16[2,256,256]{2,1,0:T(8,128)(2,1)}, u32[]{:S(2)}, u32[]{:S(2)}) collective-permute-start(bf16[2,256,256]{2,1,0:T(8,128)(2,1)} %select_select_fusion.1), channel_id=1, source_target_pairs={{2,3},{1,0},{0,2},{3,1},{6,7},{5,4},{4,6},{7,5},{10,11},{9,8},{8,1... | collective-permute-start | bytes 786440 | tf_op jit(solution)/shard_map/ppermute | solution.py:146
  88.1 1.7 %copy-start.9 = (bf16[2,256,256]{2,1,0:T(8,128)(2,1)}, bf16[2,256,256]{2,1,0:T(8,128)(2,1)S(1)}, u32[]{:S(2)}) copy-start(bf16[2,256,256]{2,1,0:T(8,128)(2,1)S(1)} %collective-permute-done.3.nxt_ref) | copy-start | bytes 786436
  88.1 17.5 %collective-permute-start.15 = (bf16[4,256,256]{2,1,0:T(8,128)(2,1)}, bf16[4,256,256]{2,1,0:T(8,128)(2,1)}, u32[]{:S(2)}, u32[]{:S(2)}) collective-permute-start(bf16[4,256,256]{2,1,0:T(8,128)(2,1)} %select_select_fusion), channel_id=1, source_target_pairs={{2,3},{1,0},{0,2},{3,1},{6,7},{5,4},{4,6},{7,5},{10,11},{9,8},{8,1... | collective-permute-start | bytes 1572872 | tf_op jit(solution)/shard_map/ppermute | solution.py:146
  89.8 23.4 %collective-permute-start.5 = (bf16[2,256,256]{2,1,0:T(8,128)(2,1)}, bf16[2,256,256]{2,1,0:T(8,128)(2,1)S(1)}, u32[]{:S(2)}, u32[]{:S(2)}) collective-permute-start(bf16[2,256,256]{2,1,0:T(8,128)(2,1)} %pad_maximum_fusion.4.own_ref), channel_id=1, source_target_pairs={{0,3},{3,0},{4,7},{7,4},{8,11},{11,8},{12,15},{15,12},{16,19},{19,... | collective-permute-start | bytes 786440 | tf_op jit(solution)/shard_map/ppermute | solution.py:147
  95.2 2.1 %copy-start.13 = (bf16[2,256,256]{2,1,0:T(8,128)(2,1)S(1)}, bf16[2,256,256]{2,1,0:T(8,128)(2,1)}, u32[]{:S(2)}) copy-start(bf16[2,256,256]{2,1,0:T(8,128)(2,1)} %select_select_fusion.2) | copy-start | bytes 786436
  97.3 18.9 %collective-permute-start.4 = (bf16[2,256,256]{2,1,0:T(8,128)(2,1)S(1)}, bf16[2,256,256]{2,1,0:T(8,128)(2,1)S(1)}, u32[]{:S(2)}, u32[]{:S(2)}) collective-permute-start(bf16[2,256,256]{2,1,0:T(8,128)(2,1)S(1)} %copy-done.13), channel_id=1, source_target_pairs={{2,3},{1,0},{0,2},{3,1},{6,7},{5,4},{4,6},{7,5},{10,11},{9,8},{8,1... | collective-permute-start | bytes 786440 | tf_op jit(solution)/shard_map/ppermute | solution.py:146
  113.2 2.9 %copy-start.14 = (bf16[2,256,256]{2,1,0:T(8,128)(2,1)}, bf16[2,256,256]{2,1,0:T(8,128)(2,1)S(1)}, u32[]{:S(2)}) copy-start(bf16[2,256,256]{2,1,0:T(8,128)(2,1)S(1)} %collective-permute-done.5.far_ref) | copy-start | bytes 786436
  116.1 0.7 copy-start.15

commit v2 on v1

v2 whole, which is shorter than its diff:
```python
import functools
import jax
import jax.numpy as jnp
from jax import lax
from jax.experimental import pallas as pl
from jax.experimental.pallas import tpu as pltpu
from jax.sharding import PartitionSpec as P

SLOTS = 2
SMEM = pl.BlockSpec(memory_space=pltpu.SMEM)
VMEM = pl.BlockSpec(memory_space=pltpu.VMEM)
HBM = pl.BlockSpec(memory_space=pltpu.HBM)
ANY = pl.BlockSpec(memory_space=pl.ANY)


def pack_kernel(owners_of, owner_hbm, am_hbm, bm_hbm, a_hbm, b_hbm, *rest):
    outs, b_out = rest[:-9], rest[-9]
    owner_ref, am_ref, bm_ref, a_ref, b_ref, inv, used, sems = rest[-8:]
    inner, tile_rows = am_ref.shape
    tile = a_ref.shape[0] // tile_rows
    wide = a_ref.shape[1] // inner
    copies = [
        pltpu.make_async_copy(source, target, sems.at[i])
        for i, (source, target) in enumerate(
            (
                (owner_hbm, owner_ref),
                (am_hbm, am_ref),
                (a_hbm, a_ref),
                (bm_hbm, bm_ref),
                (b_hbm, b_ref),
            )
        )
    ]
    for copy in copies:
        copy.start()

    def clear(i, carry):
        inv[i] = -1
        return carry

    def clear_used(i, carry):
        used[i] = 0
        return carry

    def place(t, carry):
        owner = owner_ref[0, t]
        slot = used[owner]
        inv[owner * SLOTS + slot] = t
        used[owner] = slot + 1
        return carry

    lax.fori_loop(0, inv.shape[0], clear, 0)
    lax.fori_loop(0, used.shape[0], clear_used, 0)
    copies[0].wait()
    lax.fori_loop(0, tile_rows, place, 0)
    copies[1].wait()
    copies[2].wait()
    for out, owners in zip(outs, owners_of(lax.axis_index("row"))):
        for d, owner in enumerate(owners):
            for s in range(SLOTS):
                t = inv[owner * SLOTS + s]
                row = jnp.maximum(t, 0)
                start = pl.multiple_of(row * tile, tile)
                for j in range(inner):
                    keep = jnp.logical_and(t >= 0, am_ref[j, row] != 0)
                    block = a_ref[pl.ds(start, tile), j * wide : (j + 1) * wide]
                    out[d, s * tile : (s + 1) * tile, j * wide : (j + 1) * wide] = jnp.where(
                        keep, block, jnp.zeros_like(block)
                    )
    copies[3].wait()
    copies[4].wait()
    cols = bm_ref.shape[1]
    width = b_ref.shape[1] // cols
    height = b_ref.shape[0]
    for j in range(cols):
        block = b_ref[:, j * width : (j + 1) * width]
        block = jnp.where(bm_ref[0, j] != 0, block, jnp.zeros_like(block))
        if len(b_out.shape) == 2:
            b_out[:, j * width : (j + 1) * width] = block
        else:
            piece, at = divmod(j * width, b_out.shape[2])
            piece, up = divmod(piece * height, b_out.shape[1])
            b_out[piece, up : up + height, at : at + width] = block


def pack(a_panels, a_mask, b_panels, b_mask, owner_map, owners_of, grid_rows, b_shape):
    tile = a_panels.shape[0] // a_mask.shape[0]
    groups = [len(owners) for owners in owners_of(0)]
    operands = [owner_map.T, a_mask.T, b_mask, a_panels, b_panels]
    return pl.pallas_call(
        functools.partial(pack_kernel, owners_of),
        out_shape=[
            jax.ShapeDtypeStruct((count, SLOTS * tile, a_panels.shape[1]), a_panels.dtype)
            for count in groups
        ]
        + [jax.ShapeDtypeStruct(b_shape, b_panels.dtype)],
        in_specs=[HBM] * 5,
        out_specs=[VMEM] * (len(groups) + 1),
        scratch_shapes=[pltpu.SMEM(x.shape, x.dtype) for x in operands[:3]]
        + [pltpu.VMEM(x.shape, x.dtype) for x in operands[3:]]
        + [
            pltpu.SMEM((grid_rows * SLOTS,), jnp.int32),
            pltpu.SMEM((grid_rows,), jnp.int32),
            pltpu.SemaphoreType.DMA((5,)),
        ],
        compiler_params=pltpu.CompilerParams(vmem_limit_bytes=60 << 20),
        name="pack",
    )(*operands)


def dot_kernel(first, own_ref, one_ref, two_ref, three_ref, b_ref, *rest):
    out_ref, done, sems = rest[-3:]
    blocks, height, depth = own_ref.shape
    me, col = lax.axis_index("row"), lax.axis_index("col")
    copies = []
    for i in range(blocks):
        total = None
        for far, ref in enumerate((own_ref, one_ref, two_ref, three_ref)):
            rows = pl.ds(pl.multiple_of((col ^ far) * depth, depth), depth)
            term = jnp.dot(ref[i], b_ref[rows, :], preferred_element_type=jnp.float32)
            total = term if total is None else total + term
        done[i] = total.astype(done.dtype)
        start = pl.multiple_of((me ^ (first + i)) * height, height)
        copy = pltpu.make_async_copy(
            done.at[i], out_ref.at[pl.ds(start, height), :], sems.at[i]
        )
        copy.start()
        copies.append(copy)
    for copy in copies:
        copy.wait()


def chunk_product(first, parts, b_full, out, rows):
    blocks, height, depth = parts[0].shape
    cols = b_full.shape[1]
    operands = [*parts, b_full]
    in_specs = [VMEM] * 5
    aliases = {}
    if out is not None:
        aliases = {len(operands): 0}
        operands.append(out)
        in_specs.append(ANY)
    flops = 2 * blocks * height * b_full.shape[0] * cols
    return pl.pallas_call(
        functools.partial(dot_kernel, first),
        out_shape=jax.ShapeDtypeStruct((rows, cols), jnp.bfloat16),
        in_specs=in_specs,
        out_specs=ANY,
        scratch_shapes=[
            pltpu.VMEM((blocks, height, cols), jnp.bfloat16),
            pltpu.SemaphoreType.DMA((blocks,)),
        ],
        input_output_aliases=aliases,
        compiler_params=pltpu.CompilerParams(vmem_limit_bytes=24 << 20),
        cost_estimate=pl.CostEstimate(flops=flops, bytes_accessed=4 << 20, transcendentals=0),
        name="chunk_product",
    )(*operands)


def after(value, *earlier):
    return lax.optimization_barrier((value, *earlier))[0]


def by_row(value, distance):
    return lax.ppermute(value, "row", [(i, i ^ distance) for i in range(8)])


def by_col(value, pairs):
    return lax.ppermute(value, "col", pairs)


def join_kernel(kept_ref, came_ref, b_ref, *outs):
    for chip, out in enumerate(outs, 1):
        out[0] = kept_ref[chip]
        out[1] = came_ref[chip]
        out[2:] = b_ref[...]


def join(kept, came, b_blocks):
    chunk = jax.ShapeDtypeStruct((2 + b_blocks.shape[0], *kept.shape[1:]), kept.dtype)
    return pl.pallas_call(
        join_kernel,
        out_shape=[chunk] * 3,
        in_specs=[VMEM] * 3,
        out_specs=[VMEM] * 3,
        compiler_params=pltpu.CompilerParams(vmem_limit_bytes=16 << 20),
        name="join",
    )(kept, came, b_blocks)


def order_b_kernel(mine_ref, other_ref, out_ref):
    me = lax.axis_index("row")
    height, width = mine_ref.shape[2:]
    cols = out_ref.shape[1]
    tile = mine_ref.shape[1] * height * width // cols
    for core in range(2):
        for chip in range(4):
            far = (me >> 1) ^ chip
            top = (2 * chip + core) * tile
            for ref, same in ((mine_ref, True), (other_ref, False)):

                @pl.when((me & 1 == core) == same)
                def _():
                    for j in range(cols // width):
                        piece, up = divmod(j * tile, height)
                        out_ref[top : top + tile, j * width : (j + 1) * width] = ref[
                            far, piece, up : up + tile, :
                        ]


def order_b(mine, other, shape):
    return pl.pallas_call(
        order_b_kernel,
        out_shape=jax.ShapeDtypeStruct(shape, mine.dtype),
        in_specs=[VMEM] * 2,
        out_specs=VMEM,
        compiler_params=pltpu.CompilerParams(vmem_limit_bytes=16 << 20),
        name="order_b",
    )(mine, other)


PAIRS = {
    1: [(0, 1), (1, 0), (2, 3), (3, 2)],
    2: [(2, 3), (1, 0), (0, 2), (3, 1)],
    3: [(0, 3), (3, 0), (1, 2), (2, 1)],
}


def first_hops(own):
    return by_col(own, PAIRS[3]), by_col(own, PAIRS[1])


def last_hop(own, three):
    col = lax.axis_index("col")
    return by_col(jnp.where((col == 1) | (col == 2), three, own), PAIRS[2])


def on_8_by_4(a_panels, a_mask, b_panels, b_mask, owner_map):
    def owners_of(me):
        return [me ^ (2 * chip) for chip in range(4)], [me ^ (2 * chip + 1) for chip in range(4)]

    height = SLOTS * b_panels.shape[0]
    width = a_panels.shape[1]
    b_shape = (b_panels.shape[0] * b_panels.shape[1] // (height * width), height, width)
    kept, sent, b_blocks = pack(
        a_panels, a_mask, b_panels, b_mask, owner_map, owners_of, 8, b_shape
    )
    came = by_row(sent, 1)
    near = jnp.stack([kept[0], came[0]])
    near_3, near_1 = first_hops(near)
    x, y, diagonal = join(kept, came, b_blocks)
    x, y = by_row(x, 2), by_row(y, 4)
    side = jnp.concatenate([x[:2], y[:2]])
    side_3, side_1 = first_hops(side)
    near_2 = last_hop(after(near, side), near_3)
    both = by_row(after(diagonal, side, near_3, near_1), 6)
    diagonal = both[:2]
    diagonal_3, diagonal_1 = first_hops(after(diagonal, near_1, near_2))
    mine = jnp.stack([b_blocks, x[2:], y[2:], both[2:]])
    mine = after(mine, side_3, side_1)
    b_full = order_b(mine, by_row(mine, 1), (8 * b_panels.shape[0], b_panels.shape[1]))
    side_2 = last_hop(after(side, side_1), side_3)
    rows = 8 * kept.shape[1]
    out = chunk_product(0, [near, near_1, near_2, near_3], b_full, None, rows)
    diagonal, diagonal_1, out = lax.optimization_barrier((diagonal, diagonal_1, out))
    diagonal_2 = last_hop(diagonal, diagonal_3)
    out = chunk_product(2, [side, side_1, side_2, side_3], b_full, out, rows)
    return chunk_product(
        6, [diagonal, diagonal_1, diagonal_2, diagonal_3], b_full, out, rows
    )


def on_any(a_panels, a_mask, b_panels, b_mask, owner_map):
    grid_rows = lax.axis_size("row")
    packed, panel_b = pack(
        a_panels, a_mask, b_panels, b_mask, owner_map, lambda me: [list(range(grid_rows))], grid_rows,
        b_panels.shape,
    )
    moved = lax.all_to_all(packed, "row", split_axis=0, concat_axis=0, tiled=True)
    whole_a = lax.all_gather(moved, "col", axis=2, tiled=True)
    whole_b = lax.all_gather(panel_b, "row", axis=0, tiled=True)
    whole_a = whole_a.reshape(-1, whole_b.shape[0])
    return jnp.dot(whole_a, whole_b, preferred_element_type=jnp.float32).astype(jnp.bfloat16)


def solution(mesh):
    placed = (P("row", "col"), P("row", "col"), P("row", "col"), P("row", "col"), P("row", None))
    sizes = (mesh.shape["row"], mesh.shape["col"])
    return jax.shard_map(
        on_8_by_4 if sizes == (8, 4) else on_any,
        mesh=mesh,
        in_specs=placed,
        out_specs=P("row", "col"),
        check_vma=False,
    )
```

time: 123 us -> 98.7 us (0.80)
  waiting for transfers between devices: 42.6 us -> 54.3 us
  starting transfers between devices: 41 us -> 29.4 us
  other arithmetic: 11.6 us -> 0.33 us
  Pallas kernels: 20.2 us -> 11.5 us
  local copies, waits for them, and re-layouts: 6.19 us -> 2.82 us
    ppermute x22 -> x14, waiting for transfers between devices: 42.6 us -> 54.3 us  [the longest x9 32 us: by_col(): return lax.ppermute(value, 'col', pairs)]
    ppermute x22 -> x14, starting transfers between devices: 41 us -> 29.4 us  [the longest x9 24 us: by_col(): return lax.ppermute(value, 'col', pairs)]
    pallas_call x4 -> x6, Pallas kernels: 20.2 us -> 11.5 us  [the longest x3 7.3 us: chunk_product(): pl.pallas_call(functools.partial(dot_kernel, first), out_shape=jax.ShapeD...]
    another operation x5 -> x2, other arithmetic: 4.65 us -> 0.16 us  [the longest x1 0.13 us: on_8_by_4(): mine = jnp.stack([b_blocks, x[2:], y[2:], both[2:]])]
    concatenate x3 -> x1, other arithmetic: 3.51 us -> 0.05 us  [on_8_by_4(): side = jnp.concatenate([x[:2], y[:2]])]
    select_n x3, other arithmetic: 3.45 us -> 0.12 us  [last_hop(): return by_col(jnp.where((col == 1) | (col == 2), three, own), PAIRS[2])]
    gather x1 -> x0, local copies, waits for them, and re-layouts: 2.05 us -> none  [gather_b(): jnp.take(mine, jnp.stack(order), axis=0, mode='clip')]
    unnamed x34 -> x8, local copies, waits for them, and re-layouts: 3.43 us -> 2.7 us
  transfers between devices with their start and end apart: 22 -> 14, of which waited for: 10 -> 10; matrix products, arithmetic and copies ran while one was open for 11% -> 0% of each run, Pallas kernels for 10% -> 7%
where the time goes in v2:
time: 98.7 us; the launch traced here: 98.5 us
  waiting for transfers between devices  54.3 us (55%)
  starting transfers between devices  29.4 us (30%)
  Pallas kernels  11.5 us (12%)
  local copies, waits for them, and re-layouts  2.82 us (3%)
    ppermute x9, waiting for transfers between devices, by_col(): return lax.ppermute(value, 'col', pairs)  32 us
    ppermute x9, starting transfers between devices, by_col(): return lax.ppermute(value, 'col', pairs)  24 us
    ppermute x5, waiting for transfers between devices, by_row(): return lax.ppermute(value, 'row', [(i, i ^ distance) for i in range(8)])  22.3 us
    pallas_call x3, Pallas kernels, chunk_product(): pl.pallas_call(functools.partial(dot_kernel, first), out_shape=jax.ShapeD...  7.3 us
    ppermute x5, starting transfers between devices, by_row(): return lax.ppermute(value, 'row', [(i, i ^ distance) for i in range(8)])  5.44 us
    unnamed x8, local copies, waits for them, and re-layouts  2.7 us
    pallas_call x1, Pallas kernels, pack(): pl.pallas_call(functools.partial(pack_kernel, owners_of), out_shape=[jax....  2.64 us
  transfers between devices with their start and end apart: 14, of which 10 were waited for; matrix products, arithmetic and copies ran while one was open for 0% of the time, Pallas kernels for 7%

profile of v2, /device:TPU:0, one launch (start us, length us, event | category | flops | bytes accessed | tf_op | source)
XLA Modules:
  0.0 98.5 jit_solution(2806519573472803363)
XLA Ops:
  0.0 2.6 %pack.1 = (bf16[4,256,256]{2,1,0:T(8,128)(2,1)}, bf16[4,256,256]{2,1,0:T(8,128)(2,1)}, bf16[2,256,256]{2,1,0:T(8,128)(2,1)}) custom-call(s32[1,16]{1,0:T(1,128)} %bitcast.11, s32[2,16]{1,0:T(2,128)} %bitcast.10, s32[1,8]{1,0:T(1,128)} %bm_hbm.1, bf16[2048,256]{1,0:T(8,128)(2,1)} %a_hbm.1, bf16[128,1024]{1,0:T(8,128)(2,1)} %b_hbm.1), custom_call_target="tpu_custom_call" | custom-call | tf_op jit(solution)/shard_map/pack/pallas_call | solution.py:90
  2.6 0.5 collective-permute-start
  3.2 1.7 %collective-permute-done.came_ref = bf16[4,256,256]{2,1,0:T(8,128)(2,1)S(1)} collective-permute-done((bf16[4,256,256]{2,1,0:T(8,128)(2,1)}, bf16[4,256,256]{2,1,0:T(8,128)(2,1)S(1)}, u32[]{:S(2)}, u32[]{:S(2)}) %collective-permute-start) | collective-permute-done | bytes 524320 | tf_op jit(solution)/shard_map/ppermute | solution.py:165
  4.9 0.0 copy-start
  4.9 0.9 copy-done
  5.9 0.0 copy-start.1
  5.9 1.0 %copy-done.1 = bf16[4,256,256]{2,1,0:T(8,128)(2,1)S(1)} copy-done((bf16[4,256,256]{2,1,0:T(8,128)(2,1)S(1)}, bf16[4,256,256]{2,1,0:T(8,128)(2,1)}, u32[]{:S(2)}) %copy-start.1) | copy-done | bytes 524312
  6.9 0.1 join.1
  7.0 2.9 %collective-permute-start.1 = (bf16[4,256,256]{2,1,0:T(8,128)(2,1)S(1)}, bf16[4,256,256]{2,1,0:T(8,128)(2,1)S(1)}, u32[]{:S(2)}, u32[]{:S(2)}) collective-permute-start(bf16[4,256,256]{2,1,0:T(8,128)(2,1)S(1)} %get-tuple-element.23), channel_id=1, source_target_pairs={{0,8},{4,12},{8,0},{12,4},{16,24},{20,28},{24,16},{28,20},{1,9},{5... | collective-permute-start | bytes 1572872 | tf_op jit(solution)/shard_map/ppermute | solution.py:165
  9.9 1.5 %collective-permute-start.2 = (bf16[4,256,256]{2,1,0:T(8,128)(2,1)S(1)}, bf16[4,256,256]{2,1,0:T(8,128)(2,1)S(1)}, u32[]{:S(2)}, u32[]{:S(2)}) collective-permute-start(bf16[4,256,256]{2,1,0:T(8,128)(2,1)S(1)} %get-tuple-element.24), channel_id=1, source_target_pairs={{0,16},{4,20},{8,24},{12,28},{16,0},{20,4},{24,8},{28,12},{1,17},{... | collective-permute-start | bytes 1572872 | tf_op jit(solution)/shard_map/ppermute | solution.py:165
  11.5 3.7 %collective-permute-start.3 = (bf16[2,256,256]{2,1,0:T(8,128)(2,1)S(1)}, bf16[2,256,256]{2,1,0:T(8,128)(2,1)S(1)}, u32[]{:S(2)}, u32[]{:S(2)}) collective-permute-start(bf16[2,256,256]{2,1,0:T(8,128)(2,1)S(1)} %pad_maximum_fusion.2.own_ref), channel_id=1, source_target_pairs={{0,3},{3,0},{1,2},{2,1},{4,7},{7,4},{5,6},{6,5},{8,11},{11,8},{9,1... | collective-permute-start | bytes 786440 | tf_op jit(solution)/shard_map/ppermute | solution.py:169
  15.2 0.0 collective-permute-start.4
  15.2 7.0 %collective-permute-done.1 = bf16[4,256,256]{2,1,0:T(8,128)(2,1)S(1)} collective-permute-done((bf16[4,256,256]{2,1,0:T(8,128)(2,1)S(1)}, bf16[4,256,256]{2,1,0:T(8,128)(2,1)S(1)}, u32[]{:S(2)}, u32[]{:S(2)}) %collective-permute-start.1) | collective-permute-done | bytes 524320 | tf_op jit(solution)/shard_map/ppermute | solution.py:165
  22.2 1.4 %collective-permute-done.2 = bf16[4,256,256]{2,1,0:T(8,128)(2,1)S(1)} collective-permute-done((bf16[4,256,256]{2,1,0:T(8,128)(2,1)S(1)}, bf16[4,256,256]{2,1,0:T(8,128)(2,1)S(1)}, u32[]{:S(2)}, u32[]{:S(2)}) %collective-permute-start.2) | collective-permute-done | bytes 524320 | tf_op jit(solution)/shard_map/ppermute | solution.py:165
  23.7 0.0 collective-permute-done.3.three_ref
  23.7 3.2 %collective-permute-done.4.one_ref = bf16[2,256,256]{2,1,0:T(8,128)(2,1)S(1)} collective-permute-done((bf16[2,256,256]{2,1,0:T(8,128)(2,1)S(1)}, bf16[2,256,256]{2,1,0:T(8,128)(2,1)S(1)}, u32[]{:S(2)}, u32[]{:S(2)}) %collective-permute-start.4) | collective-permute-done | bytes 262176 | tf_op jit(solution)/shard_map/ppermute | solution.py:169
  27.0 0.0 copy-start.2
  27.0 0.7 copy-done.2
  27.7 0.5 collective-permute-start.5
  28.1 1.7 %collective-permute-start.9 = (bf16[4,256,256]{2,1,0:T(8,128)(2,1)S(1)}, bf16[4,256,256]{2,1,0:T(8,128)(2,1)S(1)}, u32[]{:S(2)}, u32[]{:S(2)}) collective-permute-start(bf16[4,256,256]{2,1,0:T(8,128)(2,1)S(1)} %pad_maximum_fusion.1.own_ref), channel_id=1, source_target_pairs={{0,1},{1,0},{2,3},{3,2},{4,5},{5,4},{6,7},{7,6},{8,9},{9,8},{10,11... | collective-permute-start | bytes 1572872 | tf_op jit(solution)/shard_map/ppermute | solution.py:169
  29.8 0.4 collective-permute-start.8
  30.2 12.2 %collective-permute-done.5 = bf16[4,256,256]{2,1,0:T(8,128)(2,1)S(1)} collective-permute-done((bf16[4,256,256]{2,1,0:T(8,128)(2,1)S(1)}, bf16[4,256,256]{2,1,0:T(8,128)(2,1)S(1)}, u32[]{:S(2)}, u32[]{:S(2)}) %collective-permute-start.5) | collective-permute-done | bytes 524320 | tf_op jit(solution)/shard_map/ppermute | solution.py:165
  42.4 0.1 pad_maximum_fusion.mine_ref
  42.6 10.4 %collective-permute-done.9.one_ref = bf16[4,256,256]{2,1,0:T(8,128)(2,1)S(1)} collective-permute-done((bf16[4,256,256]{2,1,0:T(8,128)(2,1)S(1)}, bf16[4,256,256]{2,1,0:T(8,128)(2,1)S(1)}, u32[]{:S(2)}, u32[]{:S(2)}) %collective-permute-start.9) | collective-permute-done | bytes 524320 | tf_op jit(solution)/shard_map/ppermute | solution.py:169
  52.9 0.0 collective-permute-done.8.three_ref
  52.9 0.0 collective-permute-start.10
  52.9 0.0 copy-start.3
  53.0 1.5 %collective-permute-start.6 = (bf16[2,256,256]{2,1,0:T(8,128)(2,1)S(1)}, bf16[2,256,256]{2,1,0:T(8,128)(2,1)S(1)}, u32[]{:S(2)}, u32[]{:S(2)}) collective-permute-start(bf16[2,256,256]{2,1,0:T(8,128)(2,1)S(1)} %broadcast_select_fusion.2), channel_id=1, source_target_pairs={{2,3},{1,0},{0,2},{3,1},{6,7},{5,4},{4,6},{7,5},{10,11},{9,8},{8,1... | collective-permute-start | bytes 786440 | tf_op jit(solution)/shard_map/ppermute | solution.py:169
  54.5 7.3 %collective-permute-done.6.two_ref = bf16[2,256,256]{2,1,0:T(8,128)(2,1)S(1)} collective-permute-done((bf16[2,256,256]{2,1,0:T(8,128)(2,1)S(1)}, bf16[2,256,256]{2,1,0:T(8,128)(2,1)S(1)}, u32[]{:S(2)}, u32[]{:S(2)}) %collective-permute-start.6) | collective-permute-done | bytes 262176 | tf_op jit(solution)/shard_map/ppermute | solution.py:169
  61.8 2.6 %collective-permute-start.7 = (bf16[2,256,256]{2,1,0:T(8,128)(2,1)S(1)}, bf16[2,256,256]{2,1,0:T(8,128)(2,1)S(1)}, u32[]{:S(2)}, u32[]{:S(2)}) collective-permute-start(bf16[2,256,256]{2,1,0:T(8,128)(2,1)S(1)} %get-tuple-element.29.own_ref), channel_id=1, source_target_pairs={{0,1},{1,0},{2,3},{3,2},{4,5},{5,4},{6,7},{7,6},{8,9},{9,8},{10,11... | collective-permute-start | bytes 786440 | tf_op jit(solution)/shard_map/ppermute | solution.py:169
  64.4 1.2 %collective-permute-start.11 = (bf16[2,256,256]{2,1,0:T(8,128)(2,1)S(1)}, bf16[2,256,256]{2,1,0:T(8,128)(2,1)S(1)}, u32[]{:S(2)}, u32[]{:S(2)}) collective-permute-start(bf16[2,256,256]{2,1,0:T(8,128)(2,1)S(1)} %get-tuple-element.29.own_ref), channel_id=1, source_target_pairs={{0,3},{3,0},{1,2},{2,1},{4,7},{7,4},{5,6},{6,5},{8,11},{11,8},{9,1... | collective-permute-start | bytes 786440 | tf_op jit(solution)/shard_map/ppermute | solution.py:169
  65.6 0.1 broadcast_select_fusion
  65.6 0.3 collective-permute-start.13
  66.0 0.0 collective-permute-done.10.other_ref
  66.0 1.4 %order_b.1.b_ref = bf16[1024,1024]{1,0:T(8,128)(2,1)S(1)} custom-call(bf16[4,2,256,256]{3,2,1,0:T(8,128)(2,1)S(1)} %pad_maximum_fusion.mine_ref, bf16[4,2,256,256]{3,2,1,0:T(8,128)(2,1)} %collective-permute-done.10.other_ref), custom_call_target="tpu_custom_call" | custom-call | tf_op jit(solution)/shard_map/order_b/pallas_call | solution.py:212
  67.4 0.0 copy-done.3
  67.4 2.1 %chunk_product.3.rest_0_ = bf16[2048,1024]{1,0:T(8,128)(2,1)} custom-call(bf16[2,256,256]{2,1,0:T(8,128)(2,1)S(1)} %pad_maximum_fusion.2.own_ref, bf16[2,256,256]{2,1,0:T(8,128)(2,1)S(1)} %copy-done.3, bf16[2,256,256]{2,1,0:T(8,128)(2,1)S(1)} %collective-permute-done.6.two_ref, bf16[2,256,256]{2,1,0:T(8,128)(2,1)S(1)} %collective-permute-done.3.three_ref, ...), custom_call_target="tpu_custom_call" | custom-call | flops 1073741824 | bytes 4194304 | tf_op jit(solution)/shard_map/chunk_product/pallas_call | solution.py:144
  69.5 3.3 %collective-permute-done.7.one_ref = bf16[2,256,256]{2,1,0:T(8,128)(2,1)S(1)} collective-permute-done((bf16[2,256,256]{2,1,0:T(8,128)(2,1)S(1)}, bf16[2,256,256]{2,1,0:T(8,128)(2,1)S(1)}, u32[]{:S(2)}, u32[]{:S(2)}) %collective-permute-start.7) | collective-permute-done | bytes 262176 | tf_op jit(solution)/shard_map/ppermute | solution.py:169
  72.8 5.7 %collective-permute-done.11.three_ref = bf16[2,256,256]{2,1,0:T(8,128)(2,1)S(1)} collective-permute-done((bf16[2,256,256]{2,1,0:T(8,128)(2,1)S(1)}, bf16[2,256,256]{2,1,0:T(8,128)(2,1)S(1)}, u32[]{:S(2)}, u32[]{:S(2)}) %collective-permute-start.11) | collective-permute-done | bytes 262176 | tf_op jit(solution)/shard_map/ppermute | solution.py:169
  78.5 12.6 %collective-permute-start.12 = (bf16[2,256,256]{2,1,0:T(8,128)(2,1)S(1)}, bf16[2,256,256]{2,1,0:T(8,128)(2,1)S(1)}, u32[]{:S(2)}, u32[]{:S(2)}) collective-permute-start(bf16[2,256,256]{2,1,0:T(8,128)(2,1)S(1)} %broadcast_select_fusion.1), channel_id=1, source_target_pairs={{2,3},{1,0},{0,2},{3,1},{6,7},{5,4},{4,6},{7,5},{10,11},{9,8},{8,1... | collective-permute-start | bytes 786440 | tf_op jit(solution)/shard_map/ppermute | solution.py:169
  91.1 0.0 collective-permute-done.13.two_ref
  91.1 3.2 %chunk_product.4.rest_0_ = bf16[2048,1024]{1,0:T(8,128)(2,1)} custom-call(bf16[4,256,256]{2,1,0:T(8,128)(2,1)S(1)} %pad_maximum_fusion.1.own_ref, bf16[4,256,256]{2,1,0:T(8,128)(2,1)S(1)} %collective-permute-done.9.one_ref, bf16[4,256,256]{2,1,0:T(8,128)(2,1)S(1)} %collective-permute-done.13.two_ref, ...), custom_call_target="tpu_custom_call", output_to_operand_aliasing={{}: (5, {})} | custom-call | flops 2147483648 | bytes 4194304 | tf_op jit(solution)/shard_map/chunk_product/pallas_call | solution.py:144
  94.3 2.2 %collective-permute-done.12.two_ref = bf16[2,256,256]{2,1,0:T(8,128)(2,1)S(1)} collective-permute-done((bf16[2,256,256]{2,1,0:T(8,128)(2,1)S(1)}, bf16[2,256,256]{2,1,0:T(8,128)(2,1)S(1)}, u32[]{:S(2)}, u32[]{:S(2)}) %collective-permute-start.12) | collective-permute-done | bytes 262176 | tf_op jit(solution)/shard_map/ppermute | solution.py:169
  96.4 2.1 %chunk_product.5 = bf16[2048,1024]{1,0:T(8,128)(2,1)} custom-call(bf16[2,256,256]{2,1,0:T(8,128)(2,1)S(1)} %get-tuple-element.29.own_ref, bf16[2,256,256]{2,1,0:T(8,128)(2,1)S(1)} %collective-permute-done.7.one_ref, bf16[2,256,256]{2,1,0:T(8,128)(2,1)S(1)} %collective-permute-done.12.two_ref, ...), custom_call_target="tpu_custom_call", output_to_operand_aliasing={{}: (5, {})} | custom-call | flops 1073741824 | bytes 4194304 | tf_op jit(solution)/shard_map/chunk_product/pallas_call | solution.py:144
  (9 shorter events, 0.3 us)
Async XLA Ops:
  2.6 2.3 %collective-permute-start = (bf16[4,256,256]{2,1,0:T(8,128)(2,1)}, bf16[4,256,256]{2,1,0:T(8,128)(2,1)S(1)}, u32[]{:S(2)}, u32[]{:S(2)}) collective-permute-start(bf16[4,256,256]{2,1,0:T(8,128)(2,1)} %get-tuple-element.20), channel_id=1, source_target_pairs={{0,4},{4,0},{8,12},{12,8},{16,20},{20,16},{24,28},{28,24},{1,5},{5... | collective-permute-start | bytes 1572872 | tf_op jit(solution)/shard_map/ppermute | solution.py:165
  4.9 0.9 copy-start
  5.9 1.0 %copy-start.1 = (bf16[4,256,256]{2,1,0:T(8,128)(2,1)S(1)}, bf16[4,256,256]{2,1,0:T(8,128)(2,1)}, u32[]{:S(2)}) copy-start(bf16[4,256,256]{2,1,0:T(8,128)(2,1)} %get-tuple-element.19.kept_ref) | copy-start | bytes 1572868
  7.0 15.2 %collective-permute-start.1 = (bf16[4,256,256]{2,1,0:T(8,128)(2,1)S(1)}, bf16[4,256,256]{2,1,0:T(8,128)(2,1)S(1)}, u32[]{:S(2)}, u32[]{:S(2)}) collective-permute-start(bf16[4,256,256]{2,1,0:T(8,128)(2,1)S(1)} %get-tuple-element.23), channel_id=1, source_target_pairs={{0,8},{4,12},{8,0},{12,4},{16,24},{20,28},{24,16},{28,20},{1,9},{5... | collective-permute-start | bytes 1572872 | tf_op jit(solution)/shard_map/ppermute | solution.py:165
  9.9 13.7 %collective-permute-start.2 = (bf16[4,256,256]{2,1,0:T(8,128)(2,1)S(1)}, bf16[4,256,256]{2,1,0:T(8,128)(2,1)S(1)}, u32[]{:S(2)}, u32[]{:S(2)}) collective-permute-start(bf16[4,256,256]{2,1,0:T(8,128)(2,1)S(1)} %get-tuple-element.24), channel_id=1, source_target_pairs={{0,16},{4,20},{8,24},{12,28},{16,0},{20,4},{24,8},{28,12},{1,17},{... | collective-permute-start | bytes 1572872 | tf_op jit(solution)/shard_map/ppermute | solution.py:165
  11.5 12.2 %collective-permute-start.3 = (bf16[2,256,256]{2,1,0:T(8,128)(2,1)S(1)}, bf16[2,256,256]{2,1,0:T(8,128)(2,1)S(1)}, u32[]{:S(2)}, u32[]{:S(2)}) collective-permute-start(bf16[2,256,256]{2,1,0:T(8,128)(2,1)S(1)} %pad_maximum_fusion.2.own_ref), channel_id=1, source_target_pairs={{0,3},{3,0},{1,2},{2,1},{4,7},{7,4},{5,6},{6,5},{8,11},{11,8},{9,1... | collective-permute-start | bytes 786440 | tf_op jit(solution)/shard_map/ppermute | solution.py:169
  15.2 11.8 %collective-permute-start.4 = (bf16[2,256,256]{2,1,0:T(8,128)(2,1)S(1)}, bf16[2,256,256]{2,1,0:T(8,128)(2,1)S(1)}, u32[]{:S(2)}, u32[]{:S(2)}) collective-permute-start(bf16[2,256,256]{2,1,0:T(8,128)(2,1)S(1)} %pad_maximum_fusion.2.own_ref), channel_id=1, source_target_pairs={{0,1},{1,0},{2,3},{3,2},{4,5},{5,4},{6,7},{7,6},{8,9},{9,8},{10,11... | collective-permute-start | bytes 786440 | tf_op jit(solution)/shard_map/ppermute | solution.py:169
  27.0 0.7 copy-start.2
  27.7 14.7 %collective-permute-start.5 = (bf16[4,256,256]{2,1,0:T(8,128)(2,1)S(1)}, bf16[4,256,256]{2,1,0:T(8,128)(2,1)S(1)}, u32[]{:S(2)}, u32[]{:S(2)}) collective-permute-start(bf16[4,256,256]{2,1,0:T(8,128)(2,1)S(1)} %get-tuple-element.25), channel_id=1, source_target_pairs={{0,24},{4,28},{8,16},{12,20},{16,8},{20,12},{24,0},{28,4},{1,25},{... | collective-permute-start | bytes 1572872 | tf_op jit(solution)/shard_map/ppermute | solution.py:165
  28.1 24.8 %collective-permute-start.9 = (bf16[4,256,256]{2,1,0:T(8,128)(2,1)S(1)}, bf16[4,256,256]{2,1,0:T(8,128)(2,1)S(1)}, u32[]{:S(2)}, u32[]{:S(2)}) collective-permute-start(bf16[4,256,256]{2,1,0:T(8,128)(2,1)S(1)} %pad_maximum_fusion.1.own_ref), channel_id=1, source_target_pairs={{0,1},{1,0},{2,3},{3,2},{4,5},{5,4},{6,7},{7,6},{8,9},{9,8},{10,11... | collective-permute-start | bytes 1572872 | tf_op jit(solution)/shard_map/ppermute | solution.py:169
  29.8 23.1 %collective-permute-start.8 = (bf16[4,256,256]{2,1,0:T(8,128)(2,1)S(1)}, bf16[4,256,256]{2,1,0:T(8,128)(2,1)S(1)}, u32[]{:S(2)}, u32[]{:S(2)}) collective-permute-start(bf16[4,256,256]{2,1,0:T(8,128)(2,1)S(1)} %pad_maximum_fusion.1.own_ref), channel_id=1, source_target_pairs={{0,3},{3,0},{1,2},{2,1},{4,7},{7,4},{5,6},{6,5},{8,11},{11,8},{9,1... | collective-permute-start | bytes 1572872 | tf_op jit(solution)/shard_map/ppermute | solution.py:169
  52.9 13.0 %collective-permute-start.10 = (bf16[4,2,256,256]{3,2,1,0:T(8,128)(2,1)S(1)}, bf16[4,2,256,256]{3,2,1,0:T(8,128)(2,1)}, u32[]{:S(2)}, u32[]{:S(2)}) collective-permute-start(bf16[4,2,256,256]{3,2,1,0:T(8,128)(2,1)S(1)} %pad_maximum_fusion.mine_ref), channel_id=1, source_target_pairs={{0,4},{4,0},{8,12},{12,8},{16,20},{20,16},{24,28},{28,24},{1,5},{5... | collective-permute-start | bytes 3145736 | tf_op jit(solution)/shard_map/ppermute | solution.py:165
  52.9 14.5 %copy-start.3 = (bf16[2,256,256]{2,1,0:T(8,128)(2,1)S(1)}, bf16[2,256,256]{2,1,0:T(8,128)(2,1)}, u32[]{:S(2)}) copy-start(bf16[2,256,256]{2,1,0:T(8,128)(2,1)} %copy-done.2) | copy-start | bytes 786436
  53.0 8.8 %collective-permute-start.6 = (bf16[2,256,256]{2,1,0:T(8,128)(2,1)S(1)}, bf16[2,256,256]{2,1,0:T(8,128)(2,1)S(1)}, u32[]{:S(2)}, u32[]{:S(2)}) collective-permute-start(bf16[2,256,256]{2,1,0:T(8,128)(2,1)S(1)} %broadcast_select_fusion.2), channel_id=1, source_target_pairs={{2,3},{1,0},{0,2},{3,1},{6,7},{5,4},{4,6},{7,5},{10,11},{9,8},{8,1... | collective-permute-start | bytes 786440 | tf_op jit(solution)/shard_map/ppermute | solution.py:169
  61.8 11.1 %collective-permute-start.7 = (bf16[2,256,256]{2,1,0:T(8,128)(2,1)S(1)}, bf16[2,256,256]{2,1,0:T(8,128)(2,1)S(1)}, u32[]{:S(2)}, u32[]{:S(2)}) collective-permute-start(bf16[2,256,256]{2,1,0:T(8,128)(2,1)S(1)} %get-tuple-element.29.own_ref), channel_id=1, source_target_pairs={{0,1},{1,0},{2,3},{3,2},{4,5},{5,4},{6,7},{7,6},{8,9},{9,8},{10,11... | collective-permute-start | bytes 786440 | tf_op jit(solution)/shard_map/ppermute | solution.py:169
  64.4 14.1 %collective-permute-start.11 = (bf16[2,256,256]{2,1,0:T(8,128)(2,1)S(1)}, bf16[2,256,256]{2,1,0:T(8,128)(2,1)S(1)}, u32[]{:S(2)}, u32[]{:S(2)}) collective-permute-start(bf16[2,256,256]{2,1,0:T(8,128)(2,1)S(1)} %get-tuple-element.29.own_ref), channel_id=1, source_target_pairs={{0,3},{3,0},{1,2},{2,1},{4,7},{7,4},{5,6},{6,5},{8,11},{11,8},{9,1... | collective-permute-start | bytes 786440 | tf_op jit(solution)/shard_map/ppermute | solution.py:169
  65.6 25.5 %collective-permute-start.13 = (bf16[4,256,256]{2,1,0:T(8,128)(2,1)S(1)}, bf16[4,256,256]{2,1,0:T(8,128)(2,1)S(1)}, u32[]{:S(2)}, u32[]{:S(2)}) collective-permute-start(bf16[4,256,256]{2,1,0:T(8,128)(2,1)S(1)} %broadcast_select_fusion), channel_id=1, source_target_pairs={{2,3},{1,0},{0,2},{3,1},{6,7},{5,4},{4,6},{7,5},{10,11},{9,8},{8,1... | collective-permute-start | bytes 1572872 | tf_op jit(solution)/shard_map/ppermute | solution.py:169
  78.5 17.9 %collective-permute-start.12 = (bf16[2,256,256]{2,1,0:T(8,128)(2,1)S(1)}, bf16[2,256,256]{2,1,0:T(8,128)(2,1)S(1)}, u32[]{:S(2)}, u32[]{:S(2)}) collective-permute-start(bf16[2,256,256]{2,1,0:T(8,128)(2,1)S(1)} %broadcast_select_fusion.1), channel_id=1, source_target_pairs={{2,3},{1,0},{0,2},{3,1},{6,7},{5,4},{4,6},{7,5},{10,11},{9,8},{8,1... | collective-permute-start | bytes 786440 | tf_op jit(solution)/shard_map/ppermute | solution.py:169

commit v3 on v2

--- a/solution.py
+++ b/solution.py
@@ -7,6 +7,7 @@
 from jax.sharding import PartitionSpec as P
 
 SLOTS = 2
+B = "b"
 SMEM = pl.BlockSpec(memory_space=pltpu.SMEM)
 VMEM = pl.BlockSpec(memory_space=pltpu.VMEM)
 HBM = pl.BlockSpec(memory_space=pltpu.HBM)
@@ -14,7 +15,7 @@
 
 
 def pack_kernel(owners_of, owner_hbm, am_hbm, bm_hbm, a_hbm, b_hbm, *rest):
-    outs, b_out = rest[:-9], rest[-9]
+    outs = rest[:-8]
     owner_ref, am_ref, bm_ref, a_ref, b_ref, inv, used, sems = rest[-8:]
     inner, tile_rows = am_ref.shape
     tile = a_ref.shape[0] // tile_rows
@@ -55,8 +56,11 @@
     lax.fori_loop(0, tile_rows, place, 0)
     copies[1].wait()
     copies[2].wait()
-    for out, owners in zip(outs, owners_of(lax.axis_index("row"))):
+    layout = owners_of(lax.axis_index("row"))
+    for out, owners in zip(outs, layout):
         for d, owner in enumerate(owners):
+            if owner is None or owner is B:
+                continue
             for s in range(SLOTS):
                 t = inv[owner * SLOTS + s]
                 row = jnp.maximum(t, 0)
@@ -75,27 +79,28 @@
     for j in range(cols):
         block = b_ref[:, j * width : (j + 1) * width]
         block = jnp.where(bm_ref[0, j] != 0, block, jnp.zeros_like(block))
-        if len(b_out.shape) == 2:
-            b_out[:, j * width : (j + 1) * width] = block
-        else:
-            piece, at = divmod(j * width, b_out.shape[2])
-            piece, up = divmod(piece * height, b_out.shape[1])
-            b_out[piece, up : up + height, at : at + width] = block
-
-
-def pack(a_panels, a_mask, b_panels, b_mask, owner_map, owners_of, grid_rows, b_shape):
+        for out, owners in zip(outs, layout):
+            if B in owners:
+                piece, at = divmod(j * width, out.shape[2])
+                piece, up = divmod(piece * height, out.shape[1])
+                out[owners.index(B) + piece, up : up + height, at : at + width] = block
+
+
+def pack(a_panels, a_mask, b_panels, b_mask, owner_map, owners_of, grid_rows):
     tile = a_panels.shape[0] // a_mask.shape[0]
-    groups = [len(owners) for owners in owners_of(0)]
+    height, width = SLOTS * tile, a_panels.shape[1]
+    b_blocks = b_panels.size // (height * width)
+    counts = [
+        sum(b_blocks if owner is B else 1 for owner in owners) for owners in owners_of(0)
+    ]
     operands = [owner_map.T, a_mask.T, b_mask, a_panels, b_panels]
     return pl.pallas_call(
         functools.partial(pack_kernel, owners_of),
         out_shape=[
-            jax.ShapeDtypeStruct((count, SLOTS * tile, a_panels.shape[1]), a_panels.dtype)
-            for count in groups
-        ]
-        + [jax.ShapeDtypeStruct(b_shape, b_panels.dtype)],
+            jax.ShapeDtypeStruct((count, height, width), a_panels.dtype) for count in counts
+        ],
         in_specs=[HBM] * 5,
-        out_specs=[VMEM] * (len(groups) + 1),
+        out_specs=[VMEM] * len(counts),
         scratch_shapes=[pltpu.SMEM(x.shape, x.dtype) for x in operands[:3]]
         + [pltpu.VMEM(x.shape, x.dtype) for x in operands[3:]]
         + [
@@ -108,16 +113,17 @@
     )(*operands)
 
 
-def dot_kernel(first, own_ref, one_ref, two_ref, three_ref, b_ref, *rest):
+def dot_kernel(first, at, own_ref, one_ref, two_ref, three_ref, b_ref, *rest):
     out_ref, done, sems = rest[-3:]
-    blocks, height, depth = own_ref.shape
+    blocks, height, depth = two_ref.shape
     me, col = lax.axis_index("row"), lax.axis_index("col")
     copies = []
     for i in range(blocks):
         total = None
-        for far, ref in enumerate((own_ref, one_ref, two_ref, three_ref)):
+        terms = (own_ref[at + i], one_ref[at + i], two_ref[i], three_ref[at + i])
+        for far, block in enumerate(terms):
             rows = pl.ds(pl.multiple_of((col ^ far) * depth, depth), depth)
-            term = jnp.dot(ref[i], b_ref[rows, :], preferred_element_type=jnp.float32)
+            term = jnp.dot(block, b_ref[rows, :], preferred_element_type=jnp.float32)
             total = term if total is None else total + term
         done[i] = total.astype(done.dtype)
         start = pl.multiple_of((me ^ (first + i)) * height, height)
@@ -130,8 +136,8 @@
         copy.wait()
 
 
-def chunk_product(first, parts, b_full, out, rows):
-    blocks, height, depth = parts[0].shape
+def chunk_product(first, at, parts, b_full, out, rows):
+    blocks, height, depth = parts[2].shape
     cols = b_full.shape[1]
     operands = [*parts, b_full]
     in_specs = [VMEM] * 5
@@ -142,7 +148,7 @@
         in_specs.append(ANY)
     flops = 2 * blocks * height * b_full.shape[0] * cols
     return pl.pallas_call(
-        functools.partial(dot_kernel, first),
+        functools.partial(dot_kernel, first, at),
         out_shape=jax.ShapeDtypeStruct((rows, cols), jnp.bfloat16),
         in_specs=in_specs,
         out_specs=ANY,
@@ -169,25 +175,6 @@
     return lax.ppermute(value, "col", pairs)
 
 
-def join_kernel(kept_ref, came_ref, b_ref, *outs):
-    for chip, out in enumerate(outs, 1):
-        out[0] = kept_ref[chip]
-        out[1] = came_ref[chip]
-        out[2:] = b_ref[...]
-
-
-def join(kept, came, b_blocks):
-    chunk = jax.ShapeDtypeStruct((2 + b_blocks.shape[0], *kept.shape[1:]), kept.dtype)
-    return pl.pallas_call(
-        join_kernel,
-        out_shape=[chunk] * 3,
-        in_specs=[VMEM] * 3,
-        out_specs=[VMEM] * 3,
-        compiler_params=pltpu.CompilerParams(vmem_limit_bytes=16 << 20),
-        name="join",
-    )(kept, came, b_blocks)
-
-
 def order_b_kernel(mine_ref, other_ref, out_ref):
     me = lax.axis_index("row")
     height, width = mine_ref.shape[2:]
@@ -230,52 +217,81 @@
     return by_col(own, PAIRS[3]), by_col(own, PAIRS[1])
 
 
-def last_hop(own, three):
+def pass_kernel(own_ref, three_ref, *outs):
     col = lax.axis_index("col")
-    return by_col(jnp.where((col == 1) | (col == 2), three, own), PAIRS[2])
+    middle = jnp.logical_or(col == 1, col == 2)
+    for ref, cond in ((three_ref, middle), (own_ref, jnp.logical_not(middle))):
+
+        @pl.when(cond)
+        def _():
+            at = 0
+            for out in outs:
+                out[...] = ref[at : at + out.shape[0]]
+                at += out.shape[0]
+
+
+def pass_on(own, three, counts):
+    return pl.pallas_call(
+        pass_kernel,
+        out_shape=[jax.ShapeDtypeStruct((n, *own.shape[1:]), own.dtype) for n in counts],
+        in_specs=[VMEM] * 2,
+        out_specs=[VMEM] * len(counts),
+        compiler_params=pltpu.CompilerParams(vmem_limit_bytes=16 << 20),
+        cost_estimate=pl.CostEstimate(flops=0, bytes_accessed=1 << 20, transcendentals=0),
+        name="passed",
+    )(own, three)
+
+
+def fill(chunk, came, chip):
+    return lax.dynamic_update_slice(chunk, came[chip : chip + 1], (1, 0, 0))
 
 
 def on_8_by_4(a_panels, a_mask, b_panels, b_mask, owner_map):
     def owners_of(me):
-        return [me ^ (2 * chip) for chip in range(4)], [me ^ (2 * chip + 1) for chip in range(4)]
-
-    height = SLOTS * b_panels.shape[0]
-    width = a_panels.shape[1]
-    b_shape = (b_panels.shape[0] * b_panels.shape[1] // (height * width), height, width)
-    kept, sent, b_blocks = pack(
-        a_panels, a_mask, b_panels, b_mask, owner_map, owners_of, 8, b_shape
+        chips = [[me ^ (2 * chip), None] for chip in range(4)]
+        sent = [me ^ (2 * chip + 1) for chip in range(4)]
+        return [*chips, sent, [B]]
+
+    near, x, y, diagonal, sent, own_b = pack(
+        a_panels, a_mask, b_panels, b_mask, owner_map, owners_of, 8
     )
     came = by_row(sent, 1)
-    near = jnp.stack([kept[0], came[0]])
+    near = fill(near, came, 0)
     near_3, near_1 = first_hops(near)
-    x, y, diagonal = join(kept, came, b_blocks)
-    x, y = by_row(x, 2), by_row(y, 4)
-    side = jnp.concatenate([x[:2], y[:2]])
-    side_3, side_1 = first_hops(side)
-    near_2 = last_hop(after(near, side), near_3)
-    both = by_row(after(diagonal, side, near_3, near_1), 6)
-    diagonal = both[:2]
-    diagonal_3, diagonal_1 = first_hops(after(diagonal, near_1, near_2))
-    mine = jnp.stack([b_blocks, x[2:], y[2:], both[2:]])
-    mine = after(mine, side_3, side_1)
+    came = after(came, near)
+    far = [by_row(fill(chunk, came, i), 2 * i) for i, chunk in enumerate((x, y, diagonal), 1)]
+    (passed,) = pass_on(near, near_3, [2])
+    near_2 = by_col(passed, PAIRS[2])
+    far = jnp.concatenate(after(far, near_1, passed))
+    far_3, far_1 = first_hops(far)
+    own_b = after(own_b, far)
+    pair = jnp.concatenate([own_b, by_row(own_b, 2)])
+    came_b = by_row(pair, 4)
+    passed = pass_on(far, far_3, [2, 2, 2])
+    last = [by_col(piece, PAIRS[2]) for piece in passed]
+    mine = jnp.concatenate([pair, after(came_b, far_1, *passed)])
+    mine = mine.reshape(4, -1, *mine.shape[1:])
     b_full = order_b(mine, by_row(mine, 1), (8 * b_panels.shape[0], b_panels.shape[1]))
-    side_2 = last_hop(after(side, side_1), side_3)
-    rows = 8 * kept.shape[1]
-    out = chunk_product(0, [near, near_1, near_2, near_3], b_full, None, rows)
-    diagonal, diagonal_1, out = lax.optimization_barrier((diagonal, diagonal_1, out))
-    diagonal_2 = last_hop(diagonal, diagonal_3)
-    out = chunk_product(2, [side, side_1, side_2, side_3], b_full, out, rows)
-    return chunk_product(
-        6, [diagonal, diagonal_1, diagonal_2, diagonal_3], b_full, out, rows
-    )
+    rows = 8 * near.shape[1]
+    out = chunk_product(0, 0, [near, near_1, near_2, near_3], b_full, None, rows)
+    for i, piece in enumerate(last):
+        out = chunk_product(2 * i + 2, 2 * i, [far, far_1, piece, far_3], b_full, out, rows)
+    return out
 
 
 def on_any(a_panels, a_mask, b_panels, b_mask, owner_map):
     grid_rows = lax.axis_size("row")
     packed, panel_b = pack(
-        a_panels, a_mask, b_panels, b_mask, owner_map, lambda me: [list(range(grid_rows))], grid_rows,
-        b_panels.shape,
+        a_panels,
+        a_mask,
+        b_panels,
+        b_mask,
+        owner_map,
+        lambda me: [list(range(grid_rows)), [B]],
+        grid_rows,
     )
+    height, width = b_panels.shape[0], a_panels.shape[1]
+    panel_b = panel_b.reshape(-1, height, width).transpose(1, 0, 2).reshape(b_panels.shape)
     moved = lax.all_to_all(packed, "row", split_axis=0, concat_axis=0, tiled=True)
     whole_a = lax.all_gather(moved, "col", axis=2, tiled=True)
     whole_b = lax.all_gather(panel_b, "row", axis=0, tiled=True)

time: 98.7 us -> 92.2 us (0.934)
  starting transfers between devices: 29.4 us -> 17.6 us
  waiting for transfers between devices: 54.3 us -> 59.4 us
    ppermute x9 -> x8, starting transfers between devices: 24 us -> 10.4 us  [by_col(): return lax.ppermute(value, 'col', pairs)]
    ppermute x9 -> x8, waiting for transfers between devices: 32 us -> 43.9 us  [by_col(): return lax.ppermute(value, 'col', pairs)]
    ppermute x5 -> x7, waiting for transfers between devices: 22.3 us -> 15.5 us  [by_row(): return lax.ppermute(value, 'row', [(i, i ^ distance) for i in range(8)])]
    ppermute x5 -> x7, starting transfers between devices: 5.44 us -> 7.22 us  [by_row(): return lax.ppermute(value, 'row', [(i, i ^ distance) for i in range(8)])]
    unnamed x8, local copies, waits for them, and re-layouts: 2.7 us -> 1 us
    dynamic_update_slice x0 -> x2, local copies, waits for them, and re-layouts: none -> 1.4 us  [fill(): return lax.dynamic_update_slice(chunk, came[chip:chip + 1], (1, 0, 0))]
    pallas_call x1, Pallas kernels: 1.44 us -> 0.21 us  [order_b(): pl.pallas_call(order_b_kernel, out_shape=jax.ShapeDtypeStruct(shape, mine...]
    concatenate x1 -> x2, other arithmetic: 0.05 us -> 1.1 us  [the longest x1 1 us: on_8_by_4(): pair = jnp.concatenate([own_b, by_row(own_b, 2)])]
  transfers between devices with their start and end apart: 14 -> 15, of which waited for: 10 -> 12; matrix products, arithmetic and copies ran while one was open for 0% -> 2% of each run, Pallas kernels for 7% -> 7%
where the time goes in v3:
time: 92.2 us; the launch traced here: 92 us
  waiting for transfers between devices  59.4 us (64%)
  starting transfers between devices  17.6 us (19%)
  Pallas kernels  11.3 us (12%)
  local copies, waits for them, and re-layouts  2.42 us (3%)
  other arithmetic  1.1 us (1%)
    ppermute x8, waiting for transfers between devices, by_col(): return lax.ppermute(value, 'col', pairs)  43.9 us
    ppermute x7, waiting for transfers between devices, by_row(): return lax.ppermute(value, 'row', [(i, i ^ distance) for i in range(8)])  15.5 us
    ppermute x8, starting transfers between devices, by_col(): return lax.ppermute(value, 'col', pairs)  10.4 us
    pallas_call x4, Pallas kernels, chunk_product(): pl.pallas_call(functools.partial(dot_kernel, first, at), out_shape=jax.Sh...  8.25 us
    ppermute x7, starting transfers between devices, by_row(): return lax.ppermute(value, 'row', [(i, i ^ distance) for i in range(8)])  7.22 us
    pallas_call x1, Pallas kernels, pack(): pl.pallas_call(functools.partial(pack_kernel, owners_of), out_shape=[jax....  2.81 us
  transfers between devices with their start and end apart: 15, of which 12 were waited for; matrix products, arithmetic and copies ran while one was open for 2% of the time, Pallas kernels for 7%

profile of v3, /device:TPU:0, one launch (start us, length us, event | category | flops | bytes accessed | tf_op | source)
XLA Modules:
  0.0 92.0 jit_solution(6909219342382718381)
XLA Ops:
  0.0 2.8 %pack.1 = (bf16[2,256,256]{2,1,0:T(8,128)(2,1)}, bf16[2,256,256]{2,1,0:T(8,128)(2,1)}, bf16[2,256,256]{2,1,0:T(8,128)(2,1)}, bf16[2,256,256]{2,1,0:T(8,128)(2,1)...) custom-call(s32[1,16]{1,0:T(1,128)} %bitcast.6, s32[2,16]{1,0:T(2,128)} %bitcast.5, s32[1,8]{1,0:T(1,128)} %bm_hbm.1, ...), custom_call_target="tpu_custom_call" | custom-call | tf_op jit(solution)/shard_map/pack/pallas_call | solution.py:97
  2.8 0.0 copy-start.2
  2.8 0.5 collective-permute-start
  3.3 1.7 %collective-permute-done = bf16[4,256,256]{2,1,0:T(8,128)(2,1)S(1)} collective-permute-done((bf16[4,256,256]{2,1,0:T(8,128)(2,1)}, bf16[4,256,256]{2,1,0:T(8,128)(2,1)S(1)}, u32[]{:S(2)}, u32[]{:S(2)}) %collective-permute-start) | collective-permute-done | bytes 524320 | tf_op jit(solution)/shard_map/ppermute | solution.py:171
  5.1 0.7 slice_dynamic-update-slice_fusion.own_ref
  5.8 5.0 %collective-permute-start.5 = (bf16[2,256,256]{2,1,0:T(8,128)(2,1)}, bf16[2,256,256]{2,1,0:T(8,128)(2,1)S(1)}, u32[]{:S(2)}, u32[]{:S(2)}) collective-permute-start(bf16[2,256,256]{2,1,0:T(8,128)(2,1)} %slice_dynamic-update-slice_fusion.own_ref), channel_id=1, source_target_pairs={{0,3},{3,0},{1,2},{2,1},{4,7},{7,4},{5,6},{6,5},{8,11},{11,8},{9,1... | collective-permute-start | bytes 786440 | tf_op jit(solution)/shard_map/ppermute | solution.py:175
  10.7 0.7 slice_dynamic-update-slice_fusion.1
  11.5 2.4 %collective-permute-start.3 = (bf16[2,256,256]{2,1,0:T(8,128)(2,1)}, bf16[2,256,256]{2,1,0:T(8,128)(2,1)S(1)}, u32[]{:S(2)}, u32[]{:S(2)}) collective-permute-start(bf16[2,256,256]{2,1,0:T(8,128)(2,1)} %get-tuple-element.35), channel_id=1, source_target_pairs={{0,24},{4,28},{8,16},{12,20},{16,8},{20,12},{24,0},{28,4},{1,25},{... | collective-permute-start | bytes 786440 | tf_op jit(solution)/shard_map/ppermute | solution.py:171
  13.9 0.5 collective-permute-start.2
  14.4 0.5 collective-permute-start.1
  15.0 0.0 collective-permute-start.4
  15.0 3.1 %collective-permute-done.5.three_ref = bf16[2,256,256]{2,1,0:T(8,128)(2,1)S(1)} collective-permute-done((bf16[2,256,256]{2,1,0:T(8,128)(2,1)}, bf16[2,256,256]{2,1,0:T(8,128)(2,1)S(1)}, u32[]{:S(2)}, u32[]{:S(2)}) %collective-permute-start.5) | collective-permute-done | bytes 262176 | tf_op jit(solution)/shard_map/ppermute | solution.py:175
  18.1 0.0 copy-start
  18.1 0.9 %copy-done = bf16[2,256,256]{2,1,0:T(8,128)(2,1)S(1)} copy-done((bf16[2,256,256]{2,1,0:T(8,128)(2,1)S(1)}, bf16[2,256,256]{2,1,0:T(8,128)(2,1)}, u32[]{:S(2)}) %copy-start) | copy-done | bytes 262168
  19.0 2.8 %collective-permute-done.3 = bf16[2,256,256]{2,1,0:T(8,128)(2,1)S(1)} collective-permute-done((bf16[2,256,256]{2,1,0:T(8,128)(2,1)}, bf16[2,256,256]{2,1,0:T(8,128)(2,1)S(1)}, u32[]{:S(2)}, u32[]{:S(2)}) %collective-permute-start.3) | collective-permute-done | bytes 262176 | tf_op jit(solution)/shard_map/ppermute | solution.py:171
  21.8 4.4 %collective-permute-done.2 = bf16[2,256,256]{2,1,0:T(8,128)(2,1)S(1)} collective-permute-done((bf16[2,256,256]{2,1,0:T(8,128)(2,1)}, bf16[2,256,256]{2,1,0:T(8,128)(2,1)S(1)}, u32[]{:S(2)}, u32[]{:S(2)}) %collective-permute-start.2) | collective-permute-done | bytes 262176 | tf_op jit(solution)/shard_map/ppermute | solution.py:171
  26.3 0.1 collective-permute-done.1
  26.4 0.0 collective-permute-done.4.one_ref
  26.4 1.6 %collective-permute-start.9 = (bf16[2,256,256]{2,1,0:T(8,128)(2,1)}, bf16[2,256,256]{2,1,0:T(8,128)(2,1)S(1)}, u32[]{:S(2)}, u32[]{:S(2)}) collective-permute-start(bf16[2,256,256]{2,1,0:T(8,128)(2,1)} %get-tuple-element.31), channel_id=1, source_target_pairs={{0,8},{4,12},{8,0},{12,4},{16,24},{20,28},{24,16},{28,20},{1,9},{5... | collective-permute-start | bytes 786440 | tf_op jit(solution)/shard_map/ppermute | solution.py:171
  28.0 0.4 collective-permute-start.7
  28.4 0.0 collective-permute-start.6
  28.4 6.4 %collective-permute-done.9 = bf16[2,256,256]{2,1,0:T(8,128)(2,1)S(1)} collective-permute-done((bf16[2,256,256]{2,1,0:T(8,128)(2,1)}, bf16[2,256,256]{2,1,0:T(8,128)(2,1)S(1)}, u32[]{:S(2)}, u32[]{:S(2)}) %collective-permute-start.9) | collective-permute-done | bytes 262176 | tf_op jit(solution)/shard_map/ppermute | solution.py:171
  34.9 1.0 %pad_maximum_fusion.1 = bf16[4,256,256]{2,1,0:T(8,128)(2,1)S(1)} fusion(bf16[2,256,256]{2,1,0:T(8,128)(2,1)S(1)} %collective-permute-done.9, bf16[2,256,256]{2,1,0:T(8,128)(2,1)} %get-tuple-element.31), kind=kLoop, calls=%fused_computation.1 | loop fusion | flops 262144 | bytes 1048576 | tf_op jit(solution)/shard_map/concatenate | solution.py:268
  35.9 0.0 copy-start.1
  35.9 1.6 %collective-permute-start.10 = (bf16[4,256,256]{2,1,0:T(8,128)(2,1)S(1)}, bf16[4,256,256]{2,1,0:T(8,128)(2,1)S(1)}, u32[]{:S(2)}, u32[]{:S(2)}) collective-permute-start(bf16[4,256,256]{2,1,0:T(8,128)(2,1)S(1)} %pad_maximum_fusion.1), channel_id=1, source_target_pairs={{0,16},{4,20},{8,24},{12,28},{16,0},{20,4},{24,8},{28,12},{1,17},{... | collective-permute-start | bytes 1572872 | tf_op jit(solution)/shard_map/ppermute | solution.py:171
  37.4 12.8 %collective-permute-done.7.three_ref = bf16[6,256,256]{2,1,0:T(8,128)(2,1)S(1)} collective-permute-done((bf16[6,256,256]{2,1,0:T(8,128)(2,1)S(1)}, bf16[6,256,256]{2,1,0:T(8,128)(2,1)S(1)}, u32[]{:S(2)}, u32[]{:S(2)}) %collective-permute-start.7) | collective-permute-done | bytes 786464 | tf_op jit(solution)/shard_map/ppermute | solution.py:175
  50.3 0.1 passed.3
  50.3 0.0 collective-permute-done.10
  50.3 13.9 %collective-permute-done.6.one_ref = bf16[6,256,256]{2,1,0:T(8,128)(2,1)S(1)} collective-permute-done((bf16[6,256,256]{2,1,0:T(8,128)(2,1)S(1)}, bf16[6,256,256]{2,1,0:T(8,128)(2,1)S(1)}, u32[]{:S(2)}, u32[]{:S(2)}) %collective-permute-start.6) | collective-permute-done | bytes 786464 | tf_op jit(solution)/shard_map/ppermute | solution.py:175
  64.2 0.0 copy-done.2
  64.2 0.1 pad_maximum_fusion
  64.3 0.1 collective-permute-start.11
  64.4 2.2 %collective-permute-start.14 = (bf16[2,256,256]{2,1,0:T(8,128)(2,1)S(1)}, bf16[2,256,256]{2,1,0:T(8,128)(2,1)S(1)}, u32[]{:S(2)}, u32[]{:S(2)}) collective-permute-start(bf16[2,256,256]{2,1,0:T(8,128)(2,1)S(1)} %passed.2), channel_id=1, source_target_pairs={{2,3},{1,0},{0,2},{3,1},{6,7},{5,4},{4,6},{7,5},{10,11},{9,8},{8,1... | collective-permute-start | bytes 786440 | tf_op jit(solution)/shard_map/ppermute | solution.py:175
  66.6 0.6 collective-permute-start.13
  67.2 0.6 collective-permute-start.12
  67.7 1.7 %collective-permute-start.8 = (bf16[2,256,256]{2,1,0:T(8,128)(2,1)S(1)}, bf16[2,256,256]{2,1,0:T(8,128)(2,1)S(1)}, u32[]{:S(2)}, u32[]{:S(2)}) collective-permute-start(bf16[2,256,256]{2,1,0:T(8,128)(2,1)S(1)} %get-tuple-element.29), channel_id=1, source_target_pairs={{2,3},{1,0},{0,2},{3,1},{6,7},{5,4},{4,6},{7,5},{10,11},{9,8},{8,1... | collective-permute-start | bytes 786440 | tf_op jit(solution)/shard_map/ppermute | solution.py:175
  69.4 0.0 collective-permute-done.11.other_ref
  69.4 0.2 order_b.1.b_ref
  69.6 3.9 %collective-permute-done.14.two_ref = bf16[2,256,256]{2,1,0:T(8,128)(2,1)S(1)} collective-permute-done((bf16[2,256,256]{2,1,0:T(8,128)(2,1)S(1)}, bf16[2,256,256]{2,1,0:T(8,128)(2,1)S(1)}, u32[]{:S(2)}, u32[]{:S(2)}) %collective-permute-start.14) | collective-permute-done | bytes 262176 | tf_op jit(solution)/shard_map/ppermute | solution.py:175
  73.5 0.0 copy-done.1
  73.5 2.1 %chunk_product.4.rest_0_ = bf16[2048,1024]{1,0:T(8,128)(2,1)} custom-call(bf16[2,256,256]{2,1,0:T(8,128)(2,1)S(1)} %copy-done.1, bf16[2,256,256]{2,1,0:T(8,128)(2,1)S(1)} %collective-permute-done.4.one_ref, bf16[2,256,256]{2,1,0:T(8,128)(2,1)S(1)} %collective-permute-done.14.two_ref, bf16[2,256,256]{2,1,0:T(8,128)(2,1)S(1)} %collective-permute-done.5.three_ref, ...), custom_call_target="tpu_custom_call" | custom-call | flops 1073741824 | bytes 4194304 | tf_op jit(solution)/shard_map/chunk_product/pallas_call | solution.py:150
  75.6 3.5 %collective-permute-done.13.two_ref = bf16[2,256,256]{2,1,0:T(8,128)(2,1)S(1)} collective-permute-done((bf16[2,256,256]{2,1,0:T(8,128)(2,1)S(1)}, bf16[2,256,256]{2,1,0:T(8,128)(2,1)S(1)}, u32[]{:S(2)}, u32[]{:S(2)}) %collective-permute-start.13) | collective-permute-done | bytes 262176 | tf_op jit(solution)/shard_map/ppermute | solution.py:175
  79.2 2.1 %chunk_product.5.rest_0_ = bf16[2048,1024]{1,0:T(8,128)(2,1)} custom-call(bf16[6,256,256]{2,1,0:T(8,128)(2,1)S(1)} %constant_dynamic-update-slice_fusion.own_ref, bf16[6,256,256]{2,1,0:T(8,128)(2,1)S(1)} %collective-permute-done.6.one_ref, bf16[2,256,256]{2,1,0:T(8,128)(2,1)S(1)} %collective-permute-done.13.two_ref, ...), custom_call_target="tpu_custom_call", output_to_operand_aliasing={{}: (5, {})} | custom-call | flops 1073741824 | bytes 4194304 | tf_op jit(solution)/shard_map/chunk_product/pallas_call | solution.py:150
  81.2 3.5 %collective-permute-done.12.two_ref = bf16[2,256,256]{2,1,0:T(8,128)(2,1)S(1)} collective-permute-done((bf16[2,256,256]{2,1,0:T(8,128)(2,1)S(1)}, bf16[2,256,256]{2,1,0:T(8,128)(2,1)S(1)}, u32[]{:S(2)}, u32[]{:S(2)}) %collective-permute-start.12) | collective-permute-done | bytes 262176 | tf_op jit(solution)/shard_map/ppermute | solution.py:175
  84.8 2.1 %chunk_product.6.rest_0_ = bf16[2048,1024]{1,0:T(8,128)(2,1)} custom-call(bf16[6,256,256]{2,1,0:T(8,128)(2,1)S(1)} %constant_dynamic-update-slice_fusion.own_ref, bf16[6,256,256]{2,1,0:T(8,128)(2,1)S(1)} %collective-permute-done.6.one_ref, bf16[2,256,256]{2,1,0:T(8,128)(2,1)S(1)} %collective-permute-done.12.two_ref, ...), custom_call_target="tpu_custom_call", output_to_operand_aliasing={{}: (5, {})} | custom-call | flops 1073741824 | bytes 4194304 | tf_op jit(solution)/shard_map/chunk_product/pallas_call | solution.py:150
  86.8 3.1 %collective-permute-done.8.two_ref = bf16[2,256,256]{2,1,0:T(8,128)(2,1)S(1)} collective-permute-done((bf16[2,256,256]{2,1,0:T(8,128)(2,1)S(1)}, bf16[2,256,256]{2,1,0:T(8,128)(2,1)S(1)}, u32[]{:S(2)}, u32[]{:S(2)}) %collective-permute-start.8) | collective-permute-done | bytes 262176 | tf_op jit(solution)/shard_map/ppermute | solution.py:175
  89.9 2.1 %chunk_product.7 = bf16[2048,1024]{1,0:T(8,128)(2,1)} custom-call(bf16[6,256,256]{2,1,0:T(8,128)(2,1)S(1)} %constant_dynamic-update-slice_fusion.own_ref, bf16[6,256,256]{2,1,0:T(8,128)(2,1)S(1)} %collective-permute-done.6.one_ref, bf16[2,256,256]{2,1,0:T(8,128)(2,1)S(1)} %collective-permute-done.8.two_ref, ...), custom_call_target="tpu_custom_call", output_to_operand_aliasing={{}: (5, {})} | custom-call | flops 1073741824 | bytes 4194304 | tf_op jit(solution)/shard_map/chunk_product/pallas_call | solution.py:150
  (4 shorter events, 0.1 us)
Async XLA Ops:
  2.8 61.4 %copy-start.2 = (bf16[2,256,256]{2,1,0:T(8,128)(2,1)S(1)}, bf16[2,256,256]{2,1,0:T(8,128)(2,1)}, u32[]{:S(2)}) copy-start(bf16[2,256,256]{2,1,0:T(8,128)(2,1)} %get-tuple-element.31) | copy-start | bytes 786436
  2.8 2.3 %collective-permute-start = (bf16[4,256,256]{2,1,0:T(8,128)(2,1)}, bf16[4,256,256]{2,1,0:T(8,128)(2,1)S(1)}, u32[]{:S(2)}, u32[]{:S(2)}) collective-permute-start(bf16[4,256,256]{2,1,0:T(8,128)(2,1)} %get-tuple-element.21), channel_id=1, source_target_pairs={{0,4},{4,0},{8,12},{12,8},{16,20},{20,16},{24,28},{28,24},{1,5},{5... | collective-permute-start | bytes 1572872 | tf_op jit(solution)/shard_map/ppermute | solution.py:171
  5.8 12.3 %collective-permute-start.5 = (bf16[2,256,256]{2,1,0:T(8,128)(2,1)}, bf16[2,256,256]{2,1,0:T(8,128)(2,1)S(1)}, u32[]{:S(2)}, u32[]{:S(2)}) collective-permute-start(bf16[2,256,256]{2,1,0:T(8,128)(2,1)} %slice_dynamic-update-slice_fusion.own_ref), channel_id=1, source_target_pairs={{0,3},{3,0},{1,2},{2,1},{4,7},{7,4},{5,6},{6,5},{8,11},{11,8},{9,1... | collective-permute-start | bytes 786440 | tf_op jit(solution)/shard_map/ppermute | solution.py:175
  11.5 10.3 %collective-permute-start.3 = (bf16[2,256,256]{2,1,0:T(8,128)(2,1)}, bf16[2,256,256]{2,1,0:T(8,128)(2,1)S(1)}, u32[]{:S(2)}, u32[]{:S(2)}) collective-permute-start(bf16[2,256,256]{2,1,0:T(8,128)(2,1)} %get-tuple-element.35), channel_id=1, source_target_pairs={{0,24},{4,28},{8,16},{12,20},{16,8},{20,12},{24,0},{28,4},{1,25},{... | collective-permute-start | bytes 786440 | tf_op jit(solution)/shard_map/ppermute | solution.py:171
  13.9 12.3 %collective-permute-start.2 = (bf16[2,256,256]{2,1,0:T(8,128)(2,1)}, bf16[2,256,256]{2,1,0:T(8,128)(2,1)S(1)}, u32[]{:S(2)}, u32[]{:S(2)}) collective-permute-start(bf16[2,256,256]{2,1,0:T(8,128)(2,1)} %get-tuple-element.36), channel_id=1, source_target_pairs={{0,16},{4,20},{8,24},{12,28},{16,0},{20,4},{24,8},{28,12},{1,17},{... | collective-permute-start | bytes 786440 | tf_op jit(solution)/shard_map/ppermute | solution.py:171
  14.4 11.9 %collective-permute-start.1 = (bf16[2,256,256]{2,1,0:T(8,128)(2,1)}, bf16[2,256,256]{2,1,0:T(8,128)(2,1)S(1)}, u32[]{:S(2)}, u32[]{:S(2)}) collective-permute-start(bf16[2,256,256]{2,1,0:T(8,128)(2,1)} %get-tuple-element.37), channel_id=1, source_target_pairs={{0,8},{4,12},{8,0},{12,4},{16,24},{20,28},{24,16},{28,20},{1,9},{5... | collective-permute-start | bytes 786440 | tf_op jit(solution)/shard_map/ppermute | solution.py:171
  15.0 11.4 %collective-permute-start.4 = (bf16[2,256,256]{2,1,0:T(8,128)(2,1)}, bf16[2,256,256]{2,1,0:T(8,128)(2,1)S(1)}, u32[]{:S(2)}, u32[]{:S(2)}) collective-permute-start(bf16[2,256,256]{2,1,0:T(8,128)(2,1)} %slice_dynamic-update-slice_fusion.own_ref), channel_id=1, source_target_pairs={{0,1},{1,0},{2,3},{3,2},{4,5},{5,4},{6,7},{7,6},{8,9},{9,8},{10,11... | collective-permute-start | bytes 786440 | tf_op jit(solution)/shard_map/ppermute | solution.py:175
  18.1 1.0 %copy-start = (bf16[2,256,256]{2,1,0:T(8,128)(2,1)S(1)}, bf16[2,256,256]{2,1,0:T(8,128)(2,1)}, u32[]{:S(2)}) copy-start(bf16[2,256,256]{2,1,0:T(8,128)(2,1)} %slice_dynamic-update-slice_fusion.own_ref) | copy-start | bytes 786436
  26.4 8.4 %collective-permute-start.9 = (bf16[2,256,256]{2,1,0:T(8,128)(2,1)}, bf16[2,256,256]{2,1,0:T(8,128)(2,1)S(1)}, u32[]{:S(2)}, u32[]{:S(2)}) collective-permute-start(bf16[2,256,256]{2,1,0:T(8,128)(2,1)} %get-tuple-element.31), channel_id=1, source_target_pairs={{0,8},{4,12},{8,0},{12,4},{16,24},{20,28},{24,16},{28,20},{1,9},{5... | collective-permute-start | bytes 786440 | tf_op jit(solution)/shard_map/ppermute | solution.py:171
  28.0 22.3 %collective-permute-start.7 = (bf16[6,256,256]{2,1,0:T(8,128)(2,1)S(1)}, bf16[6,256,256]{2,1,0:T(8,128)(2,1)S(1)}, u32[]{:S(2)}, u32[]{:S(2)}) collective-permute-start(bf16[6,256,256]{2,1,0:T(8,128)(2,1)S(1)} %constant_dynamic-update-slice_fusion.own_ref), channel_id=1, source_target_pairs={{0,3},{3,0},{1,2},{2,1},{4,7},{7,4},{5,6},{6,5},{8,11},{11,8},{9,1... | collective-permute-start | bytes 2359304 | tf_op jit(solution)/shard_map/ppermute | solution.py:175
  28.4 35.8 %collective-permute-start.6 = (bf16[6,256,256]{2,1,0:T(8,128)(2,1)S(1)}, bf16[6,256,256]{2,1,0:T(8,128)(2,1)S(1)}, u32[]{:S(2)}, u32[]{:S(2)}) collective-permute-start(bf16[6,256,256]{2,1,0:T(8,128)(2,1)S(1)} %constant_dynamic-update-slice_fusion.own_ref), channel_id=1, source_target_pairs={{0,1},{1,0},{2,3},{3,2},{4,5},{5,4},{6,7},{7,6},{8,9},{9,8},{10,11... | collective-permute-start | bytes 2359304 | tf_op jit(solution)/shard_map/ppermute | solution.py:175
  35.9 37.7 %copy-start.1 = (bf16[2,256,256]{2,1,0:T(8,128)(2,1)S(1)}, bf16[2,256,256]{2,1,0:T(8,128)(2,1)}, u32[]{:S(2)}) copy-start(bf16[2,256,256]{2,1,0:T(8,128)(2,1)} %slice_dynamic-update-slice_fusion.own_ref) | copy-start | bytes 786436
  35.9 14.5 %collective-permute-start.10 = (bf16[4,256,256]{2,1,0:T(8,128)(2,1)S(1)}, bf16[4,256,256]{2,1,0:T(8,128)(2,1)S(1)}, u32[]{:S(2)}, u32[]{:S(2)}) collective-permute-start(bf16[4,256,256]{2,1,0:T(8,128)(2,1)S(1)} %pad_maximum_fusion.1), channel_id=1, source_target_pairs={{0,16},{4,20},{8,24},{12,28},{16,0},{20,4},{24,8},{28,12},{1,17},{... | collective-permute-start | bytes 1572872 | tf_op jit(solution)/shard_map/ppermute | solution.py:171
  64.3 5.1 %collective-permute-start.11 = (bf16[4,2,256,256]{3,2,1,0:T(8,128)(2,1)S(1)}, bf16[4,2,256,256]{3,2,1,0:T(8,128)(2,1)S(1)}, u32[]{:S(2)}, u32[]{:S(2)}) collective-permute-start(bf16[4,2,256,256]{3,2,1,0:T(8,128)(2,1)S(1)} %bitcast.3), channel_id=1, source_target_pairs={{0,4},{4,0},{8,12},{12,8},{16,20},{20,16},{24,28},{28,24},{1,5},{5... | collective-permute-start | bytes 3145736 | tf_op jit(solution)/shard_map/ppermute | solution.py:171
  64.4 9.2 %collective-permute-start.14 = (bf16[2,256,256]{2,1,0:T(8,128)(2,1)S(1)}, bf16[2,256,256]{2,1,0:T(8,128)(2,1)S(1)}, u32[]{:S(2)}, u32[]{:S(2)}) collective-permute-start(bf16[2,256,256]{2,1,0:T(8,128)(2,1)S(1)} %passed.2), channel_id=1, source_target_pairs={{2,3},{1,0},{0,2},{3,1},{6,7},{5,4},{4,6},{7,5},{10,11},{9,8},{8,1... | collective-permute-start | bytes 786440 | tf_op jit(solution)/shard_map/ppermute | solution.py:175
  66.6 12.6 %collective-permute-start.13 = (bf16[2,256,256]{2,1,0:T(8,128)(2,1)S(1)}, bf16[2,256,256]{2,1,0:T(8,128)(2,1)S(1)}, u32[]{:S(2)}, u32[]{:S(2)}) collective-permute-start(bf16[2,256,256]{2,1,0:T(8,128)(2,1)S(1)} %get-tuple-element.32), channel_id=1, source_target_pairs={{2,3},{1,0},{0,2},{3,1},{6,7},{5,4},{4,6},{7,5},{10,11},{9,8},{8,1... | collective-permute-start | bytes 786440 | tf_op jit(solution)/shard_map/ppermute | solution.py:175
  67.2 17.6 %collective-permute-start.12 = (bf16[2,256,256]{2,1,0:T(8,128)(2,1)S(1)}, bf16[2,256,256]{2,1,0:T(8,128)(2,1)S(1)}, u32[]{:S(2)}, u32[]{:S(2)}) collective-permute-start(bf16[2,256,256]{2,1,0:T(8,128)(2,1)S(1)} %get-tuple-element.33), channel_id=1, source_target_pairs={{2,3},{1,0},{0,2},{3,1},{6,7},{5,4},{4,6},{7,5},{10,11},{9,8},{8,1... | collective-permute-start | bytes 786440 | tf_op jit(solution)/shard_map/ppermute | solution.py:175
  67.7 22.2 %collective-permute-start.8 = (bf16[2,256,256]{2,1,0:T(8,128)(2,1)S(1)}, bf16[2,256,256]{2,1,0:T(8,128)(2,1)S(1)}, u32[]{:S(2)}, u32[]{:S(2)}) collective-permute-start(bf16[2,256,256]{2,1,0:T(8,128)(2,1)S(1)} %get-tuple-element.29), channel_id=1, source_target_pairs={{2,3},{1,0},{0,2},{3,1},{6,7},{5,4},{4,6},{7,5},{10,11},{9,8},{8,1... | collective-permute-start | bytes 786440 | tf_op jit(solution)/shard_map/ppermute | solution.py:175

commit v4 on v3

--- a/solution.py
+++ b/solution.py
@@ -7,6 +7,7 @@
 from jax.sharding import PartitionSpec as P
 
 SLOTS = 2
+LAST = [3, 2, 1]
 B = "b"
 SMEM = pl.BlockSpec(memory_space=pltpu.SMEM)
 VMEM = pl.BlockSpec(memory_space=pltpu.VMEM)
@@ -94,6 +95,7 @@
         sum(b_blocks if owner is B else 1 for owner in owners) for owners in owners_of(0)
     ]
     operands = [owner_map.T, a_mask.T, b_mask, a_panels, b_panels]
+    operands = [pltpu.with_memory_space_constraint(x, pltpu.HBM) for x in operands]
     return pl.pallas_call(
         functools.partial(pack_kernel, owners_of),
         out_shape=[
@@ -108,7 +110,7 @@
             pltpu.SMEM((grid_rows,), jnp.int32),
             pltpu.SemaphoreType.DMA((5,)),
         ],
-        compiler_params=pltpu.CompilerParams(vmem_limit_bytes=60 << 20),
+        compiler_params=pltpu.CompilerParams(vmem_limit_bytes=16 << 20),
         name="pack",
     )(*operands)
 
@@ -262,20 +264,22 @@
     far = [by_row(fill(chunk, came, i), 2 * i) for i, chunk in enumerate((x, y, diagonal), 1)]
     (passed,) = pass_on(near, near_3, [2])
     near_2 = by_col(passed, PAIRS[2])
-    far = jnp.concatenate(after(far, near_1, passed))
+    far = jnp.concatenate(after(far, near_1, near_2))
     far_3, far_1 = first_hops(far)
     own_b = after(own_b, far)
     pair = jnp.concatenate([own_b, by_row(own_b, 2)])
     came_b = by_row(pair, 4)
-    passed = pass_on(far, far_3, [2, 2, 2])
+    passed = pass_on(far, far_3, LAST)
     last = [by_col(piece, PAIRS[2]) for piece in passed]
     mine = jnp.concatenate([pair, after(came_b, far_1, *passed)])
     mine = mine.reshape(4, -1, *mine.shape[1:])
     b_full = order_b(mine, by_row(mine, 1), (8 * b_panels.shape[0], b_panels.shape[1]))
     rows = 8 * near.shape[1]
     out = chunk_product(0, 0, [near, near_1, near_2, near_3], b_full, None, rows)
-    for i, piece in enumerate(last):
-        out = chunk_product(2 * i + 2, 2 * i, [far, far_1, piece, far_3], b_full, out, rows)
+    at = 0
+    for piece in last:
+        out = chunk_product(2 + at, at, [far, far_1, piece, far_3], b_full, out, rows)
+        at += piece.shape[0]
     return out
 
 

time: 92.2 us -> 86.8 us (0.941)
  waiting for transfers between devices: 59.4 us -> 50.7 us
  starting transfers between devices: 17.6 us -> 25.4 us
  local copies, waits for them, and re-layouts: 2.42 us -> 0.09 us
  Pallas kernels: 11.3 us -> 10.1 us
  other arithmetic: 1.1 us -> 0.15 us
    ppermute x7, waiting for transfers between devices: 15.5 us -> 4.75 us  [by_row(): return lax.ppermute(value, 'row', [(i, i ^ distance) for i in range(8)])]
    ppermute x8, starting transfers between devices: 10.4 us -> 18.1 us  [by_col(): return lax.ppermute(value, 'col', pairs)]
    ppermute x8, waiting for transfers between devices: 43.9 us -> 46 us  [by_col(): return lax.ppermute(value, 'col', pairs)]
    dynamic_update_slice x2, local copies, waits for them, and re-layouts: 1.4 us -> 0.04 us  [fill(): return lax.dynamic_update_slice(chunk, came[chip:chip + 1], (1, 0, 0))]
    pallas_call x1, Pallas kernels: 2.81 us -> 1.6 us  [pack(): pl.pallas_call(functools.partial(pack_kernel, owners_of), out_shape=[jax....]
    unnamed x8 -> x2, local copies, waits for them, and re-layouts: 1 us -> 0.04 us
    concatenate x1, other arithmetic: 1 us -> 0.05 us  [on_8_by_4(): pair = jnp.concatenate([own_b, by_row(own_b, 2)])]
  transfers between devices with their start and end apart: 15 -> 15, of which waited for: 12 -> 11; matrix products, arithmetic and copies ran while one was open for 2% -> 0% of each run, Pallas kernels for 7% -> 8%
where the time goes in v4:
time: 86.8 us; the launch traced here: 86.7 us
  waiting for transfers between devices  50.7 us (58%)
  starting transfers between devices  25.4 us (29%)
  Pallas kernels  10.1 us (12%)
    ppermute x8, waiting for transfers between devices, by_col(): return lax.ppermute(value, 'col', pairs)  46 us
    ppermute x8, starting transfers between devices, by_col(): return lax.ppermute(value, 'col', pairs)  18.1 us
    pallas_call x4, Pallas kernels, chunk_product(): pl.pallas_call(functools.partial(dot_kernel, first, at), out_shape=jax.Sh...  8.26 us
    ppermute x7, starting transfers between devices, by_row(): return lax.ppermute(value, 'row', [(i, i ^ distance) for i in range(8)])  7.29 us
    ppermute x7, waiting for transfers between devices, by_row(): return lax.ppermute(value, 'row', [(i, i ^ distance) for i in range(8)])  4.75 us
  transfers between devices with their start and end apart: 15, of which 11 were waited for; matrix products, arithmetic and copies ran while one was open for 0% of the time, Pallas kernels for 8%

profile of v4, /device:TPU:0, one launch (start us, length us, event | category | flops | bytes accessed | tf_op | source)
XLA Modules:
  0.0 86.7 jit_solution(14098759595594827549)
XLA Ops:
  0.0 1.6 %pack.1 = (bf16[2,256,256]{2,1,0:T(8,128)(2,1)S(1)}, bf16[2,256,256]{2,1,0:T(8,128)(2,1)S(1)}, bf16[2,256,256]{2,1,0:T(8,128)(2,1)S(1)}, bf16[2,256,256]{2,1,0:T...) custom-call(s32[1,16]{1,0:T(1,128)} %bitcast.6, s32[2,16]{1,0:T(2,128)} %bitcast.5, ...), custom_call_target="tpu_custom_call" | custom-call | tf_op jit(solution)/shard_map/pack/pallas_call | solution.py:99
  1.6 0.5 collective-permute-start
  2.1 1.5 %collective-permute-done = bf16[4,256,256]{2,1,0:T(8,128)(2,1)S(1)} collective-permute-done((bf16[4,256,256]{2,1,0:T(8,128)(2,1)S(1)}, bf16[4,256,256]{2,1,0:T(8,128)(2,1)S(1)}, u32[]{:S(2)}, u32[]{:S(2)}) %collective-permute-start) | collective-permute-done | bytes 524320 | tf_op jit(solution)/shard_map/ppermute | solution.py:173
  3.7 5.0 %collective-permute-start.5 = (bf16[2,256,256]{2,1,0:T(8,128)(2,1)S(1)}, bf16[2,256,256]{2,1,0:T(8,128)(2,1)S(1)}, u32[]{:S(2)}, u32[]{:S(2)}) collective-permute-start(bf16[2,256,256]{2,1,0:T(8,128)(2,1)S(1)} %slice_dynamic-update-slice_fusion.own_ref), channel_id=1, source_target_pairs={{0,3},{3,0},{1,2},{2,1},{4,7},{7,4},{5,6},{6,5},{8,11},{11,8},{9,1... | collective-permute-start | bytes 786440 | tf_op jit(solution)/shard_map/ppermute | solution.py:177
  8.7 0.0 collective-permute-start.4
  8.7 2.5 %collective-permute-start.3 = (bf16[2,256,256]{2,1,0:T(8,128)(2,1)S(1)}, bf16[2,256,256]{2,1,0:T(8,128)(2,1)S(1)}, u32[]{:S(2)}, u32[]{:S(2)}) collective-permute-start(bf16[2,256,256]{2,1,0:T(8,128)(2,1)S(1)} %get-tuple-element.35), channel_id=1, source_target_pairs={{0,24},{4,28},{8,16},{12,20},{16,8},{20,12},{24,0},{28,4},{1,25},{... | collective-permute-start | bytes 786440 | tf_op jit(solution)/shard_map/ppermute | solution.py:173
  11.3 0.5 collective-permute-start.2
  11.8 0.5 collective-permute-start.1
  12.3 3.6 %collective-permute-done.5.three_ref = bf16[2,256,256]{2,1,0:T(8,128)(2,1)S(1)} collective-permute-done((bf16[2,256,256]{2,1,0:T(8,128)(2,1)S(1)}, bf16[2,256,256]{2,1,0:T(8,128)(2,1)S(1)}, u32[]{:S(2)}, u32[]{:S(2)}) %collective-permute-start.5) | collective-permute-done | bytes 262176 | tf_op jit(solution)/shard_map/ppermute | solution.py:177
  15.9 5.8 %collective-permute-start.6 = (bf16[2,256,256]{2,1,0:T(8,128)(2,1)S(1)}, bf16[2,256,256]{2,1,0:T(8,128)(2,1)S(1)}, u32[]{:S(2)}, u32[]{:S(2)}) collective-permute-start(bf16[2,256,256]{2,1,0:T(8,128)(2,1)S(1)} %passed.2), channel_id=1, source_target_pairs={{2,3},{1,0},{0,2},{3,1},{6,7},{5,4},{4,6},{7,5},{10,11},{9,8},{8,1... | collective-permute-start | bytes 786440 | tf_op jit(solution)/shard_map/ppermute | solution.py:177
  21.7 0.0 collective-permute-done.3
  21.7 1.6 %collective-permute-done.2 = bf16[2,256,256]{2,1,0:T(8,128)(2,1)S(1)} collective-permute-done((bf16[2,256,256]{2,1,0:T(8,128)(2,1)S(1)}, bf16[2,256,256]{2,1,0:T(8,128)(2,1)S(1)}, u32[]{:S(2)}, u32[]{:S(2)}) %collective-permute-start.2) | collective-permute-done | bytes 262176 | tf_op jit(solution)/shard_map/ppermute | solution.py:173
  23.4 0.1 collective-permute-done.1
  23.5 0.0 collective-permute-done.4.one_ref
  23.5 3.3 %collective-permute-done.6.two_ref = bf16[2,256,256]{2,1,0:T(8,128)(2,1)S(1)} collective-permute-done((bf16[2,256,256]{2,1,0:T(8,128)(2,1)S(1)}, bf16[2,256,256]{2,1,0:T(8,128)(2,1)S(1)}, u32[]{:S(2)}, u32[]{:S(2)}) %collective-permute-start.6) | collective-permute-done | bytes 262176 | tf_op jit(solution)/shard_map/ppermute | solution.py:177
  26.9 1.6 %collective-permute-start.10 = (bf16[2,256,256]{2,1,0:T(8,128)(2,1)S(1)}, bf16[2,256,256]{2,1,0:T(8,128)(2,1)S(1)}, u32[]{:S(2)}, u32[]{:S(2)}) collective-permute-start(bf16[2,256,256]{2,1,0:T(8,128)(2,1)S(1)} %get-tuple-element.31), channel_id=1, source_target_pairs={{0,8},{4,12},{8,0},{12,4},{16,24},{20,28},{24,16},{28,20},{1,9},{5... | collective-permute-start | bytes 786440 | tf_op jit(solution)/shard_map/ppermute | solution.py:173
  28.4 2.2 %collective-permute-start.8 = (bf16[6,256,256]{2,1,0:T(8,128)(2,1)S(1)}, bf16[6,256,256]{2,1,0:T(8,128)(2,1)S(1)}, u32[]{:S(2)}, u32[]{:S(2)}) collective-permute-start(bf16[6,256,256]{2,1,0:T(8,128)(2,1)S(1)} %constant_dynamic-update-slice_fusion.own_ref), channel_id=1, source_target_pairs={{0,3},{3,0},{1,2},{2,1},{4,7},{7,4},{5,6},{6,5},{8,11},{11,8},{9,1... | collective-permute-start | bytes 2359304 | tf_op jit(solution)/shard_map/ppermute | solution.py:177
  30.6 1.7 %collective-permute-start.7 = (bf16[6,256,256]{2,1,0:T(8,128)(2,1)S(1)}, bf16[6,256,256]{2,1,0:T(8,128)(2,1)S(1)}, u32[]{:S(2)}, u32[]{:S(2)}) collective-permute-start(bf16[6,256,256]{2,1,0:T(8,128)(2,1)S(1)} %constant_dynamic-update-slice_fusion.own_ref), channel_id=1, source_target_pairs={{0,1},{1,0},{2,3},{3,2},{4,5},{5,4},{6,7},{7,6},{8,9},{9,8},{10,11... | collective-permute-start | bytes 2359304 | tf_op jit(solution)/shard_map/ppermute | solution.py:177
  32.4 1.5 %collective-permute-done.10 = bf16[2,256,256]{2,1,0:T(8,128)(2,1)S(1)} collective-permute-done((bf16[2,256,256]{2,1,0:T(8,128)(2,1)S(1)}, bf16[2,256,256]{2,1,0:T(8,128)(2,1)S(1)}, u32[]{:S(2)}, u32[]{:S(2)}) %collective-permute-start.10) | collective-permute-done | bytes 262176 | tf_op jit(solution)/shard_map/ppermute | solution.py:173
  33.9 1.6 %collective-permute-start.11 = (bf16[4,256,256]{2,1,0:T(8,128)(2,1)S(1)}, bf16[4,256,256]{2,1,0:T(8,128)(2,1)S(1)}, u32[]{:S(2)}, u32[]{:S(2)}) collective-permute-start(bf16[4,256,256]{2,1,0:T(8,128)(2,1)S(1)} %pad_maximum_fusion.1), channel_id=1, source_target_pairs={{0,16},{4,20},{8,24},{12,28},{16,0},{20,4},{24,8},{28,12},{1,17},{... | collective-permute-start | bytes 1572872 | tf_op jit(solution)/shard_map/ppermute | solution.py:173
  35.5 15.3 %collective-permute-done.8.three_ref = bf16[6,256,256]{2,1,0:T(8,128)(2,1)S(1)} collective-permute-done((bf16[6,256,256]{2,1,0:T(8,128)(2,1)S(1)}, bf16[6,256,256]{2,1,0:T(8,128)(2,1)S(1)}, u32[]{:S(2)}, u32[]{:S(2)}) %collective-permute-start.8) | collective-permute-done | bytes 786464 | tf_op jit(solution)/shard_map/ppermute | solution.py:177
  50.7 0.1 passed.3
  50.8 0.0 collective-permute-done.11
  50.8 14.2 %collective-permute-done.7.one_ref = bf16[6,256,256]{2,1,0:T(8,128)(2,1)S(1)} collective-permute-done((bf16[6,256,256]{2,1,0:T(8,128)(2,1)S(1)}, bf16[6,256,256]{2,1,0:T(8,128)(2,1)S(1)}, u32[]{:S(2)}, u32[]{:S(2)}) %collective-permute-start.7) | collective-permute-done | bytes 786464 | tf_op jit(solution)/shard_map/ppermute | solution.py:177
  65.0 0.1 pad_maximum_fusion
  65.1 0.1 collective-permute-start.12
  65.2 1.3 %collective-permute-start.14 = (bf16[3,256,256]{2,1,0:T(8,128)(2,1)S(1)}, bf16[3,256,256]{2,1,0:T(8,128)(2,1)S(1)}, u32[]{:S(2)}, u32[]{:S(2)}) collective-permute-start(bf16[3,256,256]{2,1,0:T(8,128)(2,1)S(1)} %get-tuple-element.32), channel_id=1, source_target_pairs={{2,3},{1,0},{0,2},{3,1},{6,7},{5,4},{4,6},{7,5},{10,11},{9,8},{8,1... | collective-permute-start | bytes 1179656 | tf_op jit(solution)/shard_map/ppermute | solution.py:177
  66.5 0.9 %collective-permute-start.13 = (bf16[2,256,256]{2,1,0:T(8,128)(2,1)S(1)}, bf16[2,256,256]{2,1,0:T(8,128)(2,1)S(1)}, u32[]{:S(2)}, u32[]{:S(2)}) collective-permute-start(bf16[2,256,256]{2,1,0:T(8,128)(2,1)S(1)} %get-tuple-element.33), channel_id=1, source_target_pairs={{2,3},{1,0},{0,2},{3,1},{6,7},{5,4},{4,6},{7,5},{10,11},{9,8},{8,1... | collective-permute-start | bytes 786440 | tf_op jit(solution)/shard_map/ppermute | solution.py:177
  67.5 1.1 %collective-permute-start.9 = (bf16[1,256,256]{2,1,0:T(8,128)(2,1)S(1)}, bf16[1,256,256]{2,1,0:T(8,128)(2,1)S(1)}, u32[]{:S(2)}, u32[]{:S(2)}) collective-permute-start(bf16[1,256,256]{2,1,0:T(8,128)(2,1)S(1)} %get-tuple-element.29), channel_id=1, source_target_pairs={{2,3},{1,0},{0,2},{3,1},{6,7},{5,4},{4,6},{7,5},{10,11},{9,8},{8,1... | collective-permute-start | bytes 393224 | tf_op jit(solution)/shard_map/ppermute | solution.py:177
  68.5 0.0 collective-permute-done.12.other_ref
  68.5 0.2 order_b.1.b_ref
  68.8 2.1 %chunk_product.4.rest_0_ = bf16[2048,1024]{1,0:T(8,128)(2,1)} custom-call(bf16[2,256,256]{2,1,0:T(8,128)(2,1)S(1)} %slice_dynamic-update-slice_fusion.own_ref, bf16[2,256,256]{2,1,0:T(8,128)(2,1)S(1)} %collective-permute-done.4.one_ref, bf16[2,256,256]{2,1,0:T(8,128)(2,1)S(1)} %collective-permute-done.6.two_ref, ...), custom_call_target="tpu_custom_call" | custom-call | flops 1073741824 | bytes 4194304 | tf_op jit(solution)/shard_map/chunk_product/pallas_call | solution.py:152
  70.8 6.3 %collective-permute-done.14.two_ref = bf16[3,256,256]{2,1,0:T(8,128)(2,1)S(1)} collective-permute-done((bf16[3,256,256]{2,1,0:T(8,128)(2,1)S(1)}, bf16[3,256,256]{2,1,0:T(8,128)(2,1)S(1)}, u32[]{:S(2)}, u32[]{:S(2)}) %collective-permute-start.14) | collective-permute-done | bytes 393248 | tf_op jit(solution)/shard_map/ppermute | solution.py:177
  77.2 2.6 %chunk_product.5.rest_0_ = bf16[2048,1024]{1,0:T(8,128)(2,1)} custom-call(bf16[6,256,256]{2,1,0:T(8,128)(2,1)S(1)} %constant_dynamic-update-slice_fusion.own_ref, bf16[6,256,256]{2,1,0:T(8,128)(2,1)S(1)} %collective-permute-done.7.one_ref, bf16[3,256,256]{2,1,0:T(8,128)(2,1)S(1)} %collective-permute-done.14.two_ref, ...), custom_call_target="tpu_custom_call", output_to_operand_aliasing={{}: (5, {})} | custom-call | flops 1610612736 | bytes 4194304 | tf_op jit(solution)/shard_map/chunk_product/pallas_call | solution.py:152
  79.8 3.0 %collective-permute-done.13.two_ref = bf16[2,256,256]{2,1,0:T(8,128)(2,1)S(1)} collective-permute-done((bf16[2,256,256]{2,1,0:T(8,128)(2,1)S(1)}, bf16[2,256,256]{2,1,0:T(8,128)(2,1)S(1)}, u32[]{:S(2)}, u32[]{:S(2)}) %collective-permute-start.13) | collective-permute-done | bytes 262176 | tf_op jit(solution)/shard_map/ppermute | solution.py:177
  82.8 2.1 %chunk_product.6.rest_0_ = bf16[2048,1024]{1,0:T(8,128)(2,1)} custom-call(bf16[6,256,256]{2,1,0:T(8,128)(2,1)S(1)} %constant_dynamic-update-slice_fusion.own_ref, bf16[6,256,256]{2,1,0:T(8,128)(2,1)S(1)} %collective-permute-done.7.one_ref, bf16[2,256,256]{2,1,0:T(8,128)(2,1)S(1)} %collective-permute-done.13.two_ref, ...), custom_call_target="tpu_custom_call", output_to_operand_aliasing={{}: (5, {})} | custom-call | flops 1073741824 | bytes 4194304 | tf_op jit(solution)/shard_map/chunk_product/pallas_call | solution.py:152
  84.9 0.3 collective-permute-done.9.two_ref
  85.1 1.5 %chunk_product.7 = bf16[2048,1024]{1,0:T(8,128)(2,1)} custom-call(bf16[6,256,256]{2,1,0:T(8,128)(2,1)S(1)} %constant_dynamic-update-slice_fusion.own_ref, bf16[6,256,256]{2,1,0:T(8,128)(2,1)S(1)} %collective-permute-done.7.one_ref, bf16[1,256,256]{2,1,0:T(8,128)(2,1)S(1)} %collective-permute-done.9.two_ref, ...), custom_call_target="tpu_custom_call", output_to_operand_aliasing={{}: (5, {})} | custom-call | flops 536870912 | bytes 4194304 | tf_op jit(solution)/shard_map/chunk_product/pallas_call | solution.py:152
  (7 shorter events, 0.2 us)
Async XLA Ops:
  1.6 2.1 %collective-permute-start = (bf16[4,256,256]{2,1,0:T(8,128)(2,1)S(1)}, bf16[4,256,256]{2,1,0:T(8,128)(2,1)S(1)}, u32[]{:S(2)}, u32[]{:S(2)}) collective-permute-start(bf16[4,256,256]{2,1,0:T(8,128)(2,1)S(1)} %get-tuple-element.21), channel_id=1, source_target_pairs={{0,4},{4,0},{8,12},{12,8},{16,20},{20,16},{24,28},{28,24},{1,5},{5... | collective-permute-start | bytes 1572872 | tf_op jit(solution)/shard_map/ppermute | solution.py:173
  3.7 12.2 %collective-permute-start.5 = (bf16[2,256,256]{2,1,0:T(8,128)(2,1)S(1)}, bf16[2,256,256]{2,1,0:T(8,128)(2,1)S(1)}, u32[]{:S(2)}, u32[]{:S(2)}) collective-permute-start(bf16[2,256,256]{2,1,0:T(8,128)(2,1)S(1)} %slice_dynamic-update-slice_fusion.own_ref), channel_id=1, source_target_pairs={{0,3},{3,0},{1,2},{2,1},{4,7},{7,4},{5,6},{6,5},{8,11},{11,8},{9,1... | collective-permute-start | bytes 786440 | tf_op jit(solution)/shard_map/ppermute | solution.py:177
  8.7 14.8 %collective-permute-start.4 = (bf16[2,256,256]{2,1,0:T(8,128)(2,1)S(1)}, bf16[2,256,256]{2,1,0:T(8,128)(2,1)S(1)}, u32[]{:S(2)}, u32[]{:S(2)}) collective-permute-start(bf16[2,256,256]{2,1,0:T(8,128)(2,1)S(1)} %slice_dynamic-update-slice_fusion.own_ref), channel_id=1, source_target_pairs={{0,1},{1,0},{2,3},{3,2},{4,5},{5,4},{6,7},{7,6},{8,9},{9,8},{10,11... | collective-permute-start | bytes 786440 | tf_op jit(solution)/shard_map/ppermute | solution.py:177
  8.7 13.0 %collective-permute-start.3 = (bf16[2,256,256]{2,1,0:T(8,128)(2,1)S(1)}, bf16[2,256,256]{2,1,0:T(8,128)(2,1)S(1)}, u32[]{:S(2)}, u32[]{:S(2)}) collective-permute-start(bf16[2,256,256]{2,1,0:T(8,128)(2,1)S(1)} %get-tuple-element.35), channel_id=1, source_target_pairs={{0,24},{4,28},{8,16},{12,20},{16,8},{20,12},{24,0},{28,4},{1,25},{... | collective-permute-start | bytes 786440 | tf_op jit(solution)/shard_map/ppermute | solution.py:173
  11.3 12.1 %collective-permute-start.2 = (bf16[2,256,256]{2,1,0:T(8,128)(2,1)S(1)}, bf16[2,256,256]{2,1,0:T(8,128)(2,1)S(1)}, u32[]{:S(2)}, u32[]{:S(2)}) collective-permute-start(bf16[2,256,256]{2,1,0:T(8,128)(2,1)S(1)} %get-tuple-element.36), channel_id=1, source_target_pairs={{0,16},{4,20},{8,24},{12,28},{16,0},{20,4},{24,8},{28,12},{1,17},{... | collective-permute-start | bytes 786440 | tf_op jit(solution)/shard_map/ppermute | solution.py:173
  11.8 11.7 %collective-permute-start.1 = (bf16[2,256,256]{2,1,0:T(8,128)(2,1)S(1)}, bf16[2,256,256]{2,1,0:T(8,128)(2,1)S(1)}, u32[]{:S(2)}, u32[]{:S(2)}) collective-permute-start(bf16[2,256,256]{2,1,0:T(8,128)(2,1)S(1)} %get-tuple-element.37), channel_id=1, source_target_pairs={{0,8},{4,12},{8,0},{12,4},{16,24},{20,28},{24,16},{28,20},{1,9},{5... | collective-permute-start | bytes 786440 | tf_op jit(solution)/shard_map/ppermute | solution.py:173
  15.9 10.9 %collective-permute-start.6 = (bf16[2,256,256]{2,1,0:T(8,128)(2,1)S(1)}, bf16[2,256,256]{2,1,0:T(8,128)(2,1)S(1)}, u32[]{:S(2)}, u32[]{:S(2)}) collective-permute-start(bf16[2,256,256]{2,1,0:T(8,128)(2,1)S(1)} %passed.2), channel_id=1, source_target_pairs={{2,3},{1,0},{0,2},{3,1},{6,7},{5,4},{4,6},{7,5},{10,11},{9,8},{8,1... | collective-permute-start | bytes 786440 | tf_op jit(solution)/shard_map/ppermute | solution.py:177
  26.9 7.0 %collective-permute-start.10 = (bf16[2,256,256]{2,1,0:T(8,128)(2,1)S(1)}, bf16[2,256,256]{2,1,0:T(8,128)(2,1)S(1)}, u32[]{:S(2)}, u32[]{:S(2)}) collective-permute-start(bf16[2,256,256]{2,1,0:T(8,128)(2,1)S(1)} %get-tuple-element.31), channel_id=1, source_target_pairs={{0,8},{4,12},{8,0},{12,4},{16,24},{20,28},{24,16},{28,20},{1,9},{5... | collective-permute-start | bytes 786440 | tf_op jit(solution)/shard_map/ppermute | solution.py:173
  28.4 22.3 %collective-permute-start.8 = (bf16[6,256,256]{2,1,0:T(8,128)(2,1)S(1)}, bf16[6,256,256]{2,1,0:T(8,128)(2,1)S(1)}, u32[]{:S(2)}, u32[]{:S(2)}) collective-permute-start(bf16[6,256,256]{2,1,0:T(8,128)(2,1)S(1)} %constant_dynamic-update-slice_fusion.own_ref), channel_id=1, source_target_pairs={{0,3},{3,0},{1,2},{2,1},{4,7},{7,4},{5,6},{6,5},{8,11},{11,8},{9,1... | collective-permute-start | bytes 2359304 | tf_op jit(solution)/shard_map/ppermute | solution.py:177
  30.6 34.4 %collective-permute-start.7 = (bf16[6,256,256]{2,1,0:T(8,128)(2,1)S(1)}, bf16[6,256,256]{2,1,0:T(8,128)(2,1)S(1)}, u32[]{:S(2)}, u32[]{:S(2)}) collective-permute-start(bf16[6,256,256]{2,1,0:T(8,128)(2,1)S(1)} %constant_dynamic-update-slice_fusion.own_ref), channel_id=1, source_target_pairs={{0,1},{1,0},{2,3},{3,2},{4,5},{5,4},{6,7},{7,6},{8,9},{9,8},{10,11... | collective-permute-start | bytes 2359304 | tf_op jit(solution)/shard_map/ppermute | solution.py:177
  33.9 16.9 %collective-permute-start.11 = (bf16[4,256,256]{2,1,0:T(8,128)(2,1)S(1)}, bf16[4,256,256]{2,1,0:T(8,128)(2,1)S(1)}, u32[]{:S(2)}, u32[]{:S(2)}) collective-permute-start(bf16[4,256,256]{2,1,0:T(8,128)(2,1)S(1)} %pad_maximum_fusion.1), channel_id=1, source_target_pairs={{0,16},{4,20},{8,24},{12,28},{16,0},{20,4},{24,8},{28,12},{1,17},{... | collective-permute-start | bytes 1572872 | tf_op jit(solution)/shard_map/ppermute | solution.py:173
  65.1 3.4 %collective-permute-start.12 = (bf16[4,2,256,256]{3,2,1,0:T(8,128)(2,1)S(1)}, bf16[4,2,256,256]{3,2,1,0:T(8,128)(2,1)S(1)}, u32[]{:S(2)}, u32[]{:S(2)}) collective-permute-start(bf16[4,2,256,256]{3,2,1,0:T(8,128)(2,1)S(1)} %bitcast.3), channel_id=1, source_target_pairs={{0,4},{4,0},{8,12},{12,8},{16,20},{20,16},{24,28},{28,24},{1,5},{5... | collective-permute-start | bytes 3145736 | tf_op jit(solution)/shard_map/ppermute | solution.py:173
  65.2 12.0 %collective-permute-start.14 = (bf16[3,256,256]{2,1,0:T(8,128)(2,1)S(1)}, bf16[3,256,256]{2,1,0:T(8,128)(2,1)S(1)}, u32[]{:S(2)}, u32[]{:S(2)}) collective-permute-start(bf16[3,256,256]{2,1,0:T(8,128)(2,1)S(1)} %get-tuple-element.32), channel_id=1, source_target_pairs={{2,3},{1,0},{0,2},{3,1},{6,7},{5,4},{4,6},{7,5},{10,11},{9,8},{8,1... | collective-permute-start | bytes 1179656 | tf_op jit(solution)/shard_map/ppermute | solution.py:177
  66.5 16.3 %collective-permute-start.13 = (bf16[2,256,256]{2,1,0:T(8,128)(2,1)S(1)}, bf16[2,256,256]{2,1,0:T(8,128)(2,1)S(1)}, u32[]{:S(2)}, u32[]{:S(2)}) collective-permute-start(bf16[2,256,256]{2,1,0:T(8,128)(2,1)S(1)} %get-tuple-element.33), channel_id=1, source_target_pairs={{2,3},{1,0},{0,2},{3,1},{6,7},{5,4},{4,6},{7,5},{10,11},{9,8},{8,1... | collective-permute-start | bytes 786440 | tf_op jit(solution)/shard_map/ppermute | solution.py:177
  67.5 17.7 %collective-permute-start.9 = (bf16[1,256,256]{2,1,0:T(8,128)(2,1)S(1)}, bf16[1,256,256]{2,1,0:T(8,128)(2,1)S(1)}, u32[]{:S(2)}, u32[]{:S(2)}) collective-permute-start(bf16[1,256,256]{2,1,0:T(8,128)(2,1)S(1)} %get-tuple-element.29), channel_id=1, source_target_pairs={{2,3},{1,0},{0,2},{3,1},{6,7},{5,4},{4,6},{7,5},{10,11},{9,8},{8,1... | collective-permute-start | bytes 393224 | tf_op jit(solution)/shard_map/ppermute | solution.py:177

commit v5 on v4

--- a/solution.py
+++ b/solution.py
@@ -177,35 +177,33 @@
     return lax.ppermute(value, "col", pairs)
 
 
-def order_b_kernel(mine_ref, other_ref, out_ref):
+def order_b_kernel(*refs):
+    out_ref = refs[-1]
     me = lax.axis_index("row")
-    height, width = mine_ref.shape[2:]
+    blocks, height, width = refs[0].shape
+    blocks = blocks // 2
     cols = out_ref.shape[1]
-    tile = mine_ref.shape[1] * height * width // cols
-    for core in range(2):
-        for chip in range(4):
-            far = (me >> 1) ^ chip
-            top = (2 * chip + core) * tile
-            for ref, same in ((mine_ref, True), (other_ref, False)):
-
-                @pl.when((me & 1 == core) == same)
-                def _():
-                    for j in range(cols // width):
-                        piece, up = divmod(j * tile, height)
-                        out_ref[top : top + tile, j * width : (j + 1) * width] = ref[
-                            far, piece, up : up + tile, :
-                        ]
-
-
-def order_b(mine, other, shape):
+    tile = blocks * height * width // cols
+    for far, ref in enumerate(refs[:-1]):
+        for core in range(2):
+            row = me ^ (2 * far + core)
+            top = pl.multiple_of(row * tile, tile)
+            for j in range(cols // width):
+                piece, up = divmod(j * tile, height)
+                out_ref[pl.ds(top, tile), j * width : (j + 1) * width] = ref[
+                    core * blocks + piece, up : up + tile, :
+                ]
+
+
+def order_b(pairs, shape):
     return pl.pallas_call(
         order_b_kernel,
-        out_shape=jax.ShapeDtypeStruct(shape, mine.dtype),
-        in_specs=[VMEM] * 2,
+        out_shape=jax.ShapeDtypeStruct(shape, pairs[0].dtype),
+        in_specs=[VMEM] * len(pairs),
         out_specs=VMEM,
         compiler_params=pltpu.CompilerParams(vmem_limit_bytes=16 << 20),
         name="order_b",
-    )(mine, other)
+    )(*pairs)
 
 
 PAIRS = {
@@ -264,16 +262,15 @@
     far = [by_row(fill(chunk, came, i), 2 * i) for i, chunk in enumerate((x, y, diagonal), 1)]
     (passed,) = pass_on(near, near_3, [2])
     near_2 = by_col(passed, PAIRS[2])
+    own_b = after(own_b, *far)
     far = jnp.concatenate(after(far, near_1, near_2))
     far_3, far_1 = first_hops(far)
-    own_b = after(own_b, far)
-    pair = jnp.concatenate([own_b, by_row(own_b, 2)])
-    came_b = by_row(pair, 4)
+    pair = jnp.concatenate([own_b, by_row(own_b, 1)])
+    came_b = [by_row(pair, 2 * chip) for chip in range(1, 4)]
     passed = pass_on(far, far_3, LAST)
     last = [by_col(piece, PAIRS[2]) for piece in passed]
-    mine = jnp.concatenate([pair, after(came_b, far_1, *passed)])
-    mine = mine.reshape(4, -1, *mine.shape[1:])
-    b_full = order_b(mine, by_row(mine, 1), (8 * b_panels.shape[0], b_panels.shape[1]))
+    pairs = [pair, *after(came_b, far_1, *passed)]
+    b_full = order_b(pairs, (8 * b_panels.shape[0], b_panels.shape[1]))
     rows = 8 * near.shape[1]
     out = chunk_product(0, 0, [near, near_1, near_2, near_3], b_full, None, rows)
     at = 0

time: 86.8 us -> 84 us (0.968)
  waiting for transfers between devices: 50.7 us -> 33.2 us
  starting transfers between devices: 25.4 us -> 40.2 us
    ppermute x8, waiting for transfers between devices: 46 us -> 29.9 us  [by_col(): return lax.ppermute(value, 'col', pairs)]
    ppermute x8, starting transfers between devices: 18.1 us -> 32.6 us  [by_col(): return lax.ppermute(value, 'col', pairs)]
    ppermute x7 -> x8, waiting for transfers between devices: 4.75 us -> 3.3 us  [by_row(): return lax.ppermute(value, 'row', [(i, i ^ distance) for i in range(8)])]
    ppermute x7 -> x8, starting transfers between devices: 7.29 us -> 7.63 us  [by_row(): return lax.ppermute(value, 'row', [(i, i ^ distance) for i in range(8)])]
  transfers between devices with their start and end apart: 15 -> 16, of which waited for: 11 -> 8; matrix products, arithmetic and copies ran while one was open for 0% -> 0% of each run, Pallas kernels for 8% -> 8%
where the time goes in v5:
time: 84 us; the launch traced here: 83.8 us
  starting transfers between devices  40.2 us (48%)
  waiting for transfers between devices  33.2 us (40%)
  Pallas kernels  10.2 us (12%)
    ppermute x8, starting transfers between devices, by_col(): return lax.ppermute(value, 'col', pairs)  32.6 us
    ppermute x8, waiting for transfers between devices, by_col(): return lax.ppermute(value, 'col', pairs)  29.9 us
    pallas_call x4, Pallas kernels, chunk_product(): pl.pallas_call(functools.partial(dot_kernel, first, at), out_shape=jax.Sh...  8.27 us
    ppermute x8, starting transfers between devices, by_row(): return lax.ppermute(value, 'row', [(i, i ^ distance) for i in range(8)])  7.63 us
    ppermute x8, waiting for transfers between devices, by_row(): return lax.ppermute(value, 'row', [(i, i ^ distance) for i in range(8)])  3.3 us
  transfers between devices with their start and end apart: 16, of which 8 were waited for; matrix products, arithmetic and copies ran while one was open for 0% of the time, Pallas kernels for 8%

profile of v5, /device:TPU:0, one launch (start us, length us, event | category | flops | bytes accessed | tf_op | source)
XLA Modules:
  0.0 83.8 jit_solution(5607906163568391749)
XLA Ops:
  0.0 1.6 %pack.1 = (bf16[2,256,256]{2,1,0:T(8,128)(2,1)S(1)}, bf16[2,256,256]{2,1,0:T(8,128)(2,1)S(1)}, bf16[2,256,256]{2,1,0:T(8,128)(2,1)S(1)}, bf16[2,256,256]{2,1,0:T...) custom-call(s32[1,16]{1,0:T(1,128)} %bitcast.3, s32[2,16]{1,0:T(2,128)} %bitcast.2, ...), custom_call_target="tpu_custom_call" | custom-call | tf_op jit(solution)/shard_map/pack/pallas_call | solution.py:99
  1.6 0.5 collective-permute-start
  2.1 1.5 %collective-permute-done = bf16[4,256,256]{2,1,0:T(8,128)(2,1)S(1)} collective-permute-done((bf16[4,256,256]{2,1,0:T(8,128)(2,1)S(1)}, bf16[4,256,256]{2,1,0:T(8,128)(2,1)S(1)}, u32[]{:S(2)}, u32[]{:S(2)}) %collective-permute-start) | collective-permute-done | bytes 524320 | tf_op jit(solution)/shard_map/ppermute | solution.py:173
  3.7 5.0 %collective-permute-start.5 = (bf16[2,256,256]{2,1,0:T(8,128)(2,1)S(1)}, bf16[2,256,256]{2,1,0:T(8,128)(2,1)S(1)}, u32[]{:S(2)}, u32[]{:S(2)}) collective-permute-start(bf16[2,256,256]{2,1,0:T(8,128)(2,1)S(1)} %slice_dynamic-update-slice_fusion.own_ref), channel_id=1, source_target_pairs={{0,3},{3,0},{1,2},{2,1},{4,7},{7,4},{5,6},{6,5},{8,11},{11,8},{9,1... | collective-permute-start | bytes 786440 | tf_op jit(solution)/shard_map/ppermute | solution.py:177
  8.7 0.0 collective-permute-start.4
  8.7 2.5 %collective-permute-start.3 = (bf16[2,256,256]{2,1,0:T(8,128)(2,1)S(1)}, bf16[2,256,256]{2,1,0:T(8,128)(2,1)S(1)}, u32[]{:S(2)}, u32[]{:S(2)}) collective-permute-start(bf16[2,256,256]{2,1,0:T(8,128)(2,1)S(1)} %get-tuple-element.39), channel_id=1, source_target_pairs={{0,24},{4,28},{8,16},{12,20},{16,8},{20,12},{24,0},{28,4},{1,25},{... | collective-permute-start | bytes 786440 | tf_op jit(solution)/shard_map/ppermute | solution.py:173
  11.3 0.5 collective-permute-start.2
  11.8 0.5 collective-permute-start.1
  12.3 3.6 %collective-permute-done.5.three_ref = bf16[2,256,256]{2,1,0:T(8,128)(2,1)S(1)} collective-permute-done((bf16[2,256,256]{2,1,0:T(8,128)(2,1)S(1)}, bf16[2,256,256]{2,1,0:T(8,128)(2,1)S(1)}, u32[]{:S(2)}, u32[]{:S(2)}) %collective-permute-start.5) | collective-permute-done | bytes 262176 | tf_op jit(solution)/shard_map/ppermute | solution.py:177
  15.9 5.8 %collective-permute-start.6 = (bf16[2,256,256]{2,1,0:T(8,128)(2,1)S(1)}, bf16[2,256,256]{2,1,0:T(8,128)(2,1)S(1)}, u32[]{:S(2)}, u32[]{:S(2)}) collective-permute-start(bf16[2,256,256]{2,1,0:T(8,128)(2,1)S(1)} %passed.2), channel_id=1, source_target_pairs={{2,3},{1,0},{0,2},{3,1},{6,7},{5,4},{4,6},{7,5},{10,11},{9,8},{8,1... | collective-permute-start | bytes 786440 | tf_op jit(solution)/shard_map/ppermute | solution.py:177
  21.7 0.0 collective-permute-done.3
  21.7 1.6 %collective-permute-done.2 = bf16[2,256,256]{2,1,0:T(8,128)(2,1)S(1)} collective-permute-done((bf16[2,256,256]{2,1,0:T(8,128)(2,1)S(1)}, bf16[2,256,256]{2,1,0:T(8,128)(2,1)S(1)}, u32[]{:S(2)}, u32[]{:S(2)}) %collective-permute-start.2) | collective-permute-done | bytes 262176 | tf_op jit(solution)/shard_map/ppermute | solution.py:173
  23.4 0.1 collective-permute-done.1
  23.5 0.0 collective-permute-done.4.one_ref
  23.5 3.3 %collective-permute-done.6.two_ref = bf16[2,256,256]{2,1,0:T(8,128)(2,1)S(1)} collective-permute-done((bf16[2,256,256]{2,1,0:T(8,128)(2,1)S(1)}, bf16[2,256,256]{2,1,0:T(8,128)(2,1)S(1)}, u32[]{:S(2)}, u32[]{:S(2)}) %collective-permute-start.6) | collective-permute-done | bytes 262176 | tf_op jit(solution)/shard_map/ppermute | solution.py:177
  26.9 2.3 %collective-permute-start.8 = (bf16[6,256,256]{2,1,0:T(8,128)(2,1)S(1)}, bf16[6,256,256]{2,1,0:T(8,128)(2,1)S(1)}, u32[]{:S(2)}, u32[]{:S(2)}) collective-permute-start(bf16[6,256,256]{2,1,0:T(8,128)(2,1)S(1)} %constant_dynamic-update-slice_fusion.own_ref), channel_id=1, source_target_pairs={{0,3},{3,0},{1,2},{2,1},{4,7},{7,4},{5,6},{6,5},{8,11},{11,8},{9,1... | collective-permute-start | bytes 2359304 | tf_op jit(solution)/shard_map/ppermute | solution.py:177
  29.1 0.0 collective-permute-start.10
  29.1 1.7 %collective-permute-start.7 = (bf16[6,256,256]{2,1,0:T(8,128)(2,1)S(1)}, bf16[6,256,256]{2,1,0:T(8,128)(2,1)S(1)}, u32[]{:S(2)}, u32[]{:S(2)}) collective-permute-start(bf16[6,256,256]{2,1,0:T(8,128)(2,1)S(1)} %constant_dynamic-update-slice_fusion.own_ref), channel_id=1, source_target_pairs={{0,1},{1,0},{2,3},{3,2},{4,5},{5,4},{6,7},{7,6},{8,9},{9,8},{10,11... | collective-permute-start | bytes 2359304 | tf_op jit(solution)/shard_map/ppermute | solution.py:177
  30.9 0.0 collective-permute-done.10
  30.9 2.5 %collective-permute-start.13 = (bf16[4,256,256]{2,1,0:T(8,128)(2,1)S(1)}, bf16[4,256,256]{2,1,0:T(8,128)(2,1)S(1)}, u32[]{:S(2)}, u32[]{:S(2)}) collective-permute-start(bf16[4,256,256]{2,1,0:T(8,128)(2,1)S(1)} %constant_dynamic-update-slice_fusion.3.refs_0_), channel_id=1, source_target_pairs={{0,24},{4,28},{8,16},{12,20},{16,8},{20,12},{24,0},{28,4},{1,25},{... | collective-permute-start | bytes 1572872 | tf_op jit(solution)/shard_map/ppermute | solution.py:173
  33.4 0.5 collective-permute-start.12
  33.9 0.5 collective-permute-start.11
  34.5 14.8 %collective-permute-done.8.three_ref = bf16[6,256,256]{2,1,0:T(8,128)(2,1)S(1)} collective-permute-done((bf16[6,256,256]{2,1,0:T(8,128)(2,1)S(1)}, bf16[6,256,256]{2,1,0:T(8,128)(2,1)S(1)}, u32[]{:S(2)}, u32[]{:S(2)}) %collective-permute-start.8) | collective-permute-done | bytes 786464 | tf_op jit(solution)/shard_map/ppermute | solution.py:177
  49.2 0.1 passed.3
  49.3 15.8 %collective-permute-start.15 = (bf16[3,256,256]{2,1,0:T(8,128)(2,1)S(1)}, bf16[3,256,256]{2,1,0:T(8,128)(2,1)S(1)}, u32[]{:S(2)}, u32[]{:S(2)}) collective-permute-start(bf16[3,256,256]{2,1,0:T(8,128)(2,1)S(1)} %get-tuple-element.34), channel_id=1, source_target_pairs={{2,3},{1,0},{0,2},{3,1},{6,7},{5,4},{4,6},{7,5},{10,11},{9,8},{8,1... | collective-permute-start | bytes 1179656 | tf_op jit(solution)/shard_map/ppermute | solution.py:177
  65.1 0.0 collective-permute-done.13.refs_3_
  65.1 0.1 collective-permute-start.14
  65.2 0.0 collective-permute-done.12.refs_2_
  65.2 1.8 %collective-permute-start.9 = (bf16[1,256,256]{2,1,0:T(8,128)(2,1)S(1)}, bf16[1,256,256]{2,1,0:T(8,128)(2,1)S(1)}, u32[]{:S(2)}, u32[]{:S(2)}) collective-permute-start(bf16[1,256,256]{2,1,0:T(8,128)(2,1)S(1)} %get-tuple-element.31), channel_id=1, source_target_pairs={{2,3},{1,0},{0,2},{3,1},{6,7},{5,4},{4,6},{7,5},{10,11},{9,8},{8,1... | collective-permute-start | bytes 393224 | tf_op jit(solution)/shard_map/ppermute | solution.py:177
  67.0 0.0 collective-permute-done.11.refs_1_
  67.0 0.0 collective-permute-done.7.one_ref
  67.0 0.2 order_b.1.b_ref
  67.3 2.1 %chunk_product.4.rest_0_ = bf16[2048,1024]{1,0:T(8,128)(2,1)} custom-call(bf16[2,256,256]{2,1,0:T(8,128)(2,1)S(1)} %slice_dynamic-update-slice_fusion.own_ref, bf16[2,256,256]{2,1,0:T(8,128)(2,1)S(1)} %collective-permute-done.4.one_ref, bf16[2,256,256]{2,1,0:T(8,128)(2,1)S(1)} %collective-permute-done.6.two_ref, ...), custom_call_target="tpu_custom_call" | custom-call | flops 1073741824 | bytes 4194304 | tf_op jit(solution)/shard_map/chunk_product/pallas_call | solution.py:152
  69.3 5.3 %collective-permute-done.15.two_ref = bf16[3,256,256]{2,1,0:T(8,128)(2,1)S(1)} collective-permute-done((bf16[3,256,256]{2,1,0:T(8,128)(2,1)S(1)}, bf16[3,256,256]{2,1,0:T(8,128)(2,1)S(1)}, u32[]{:S(2)}, u32[]{:S(2)}) %collective-permute-start.15) | collective-permute-done | bytes 393248 | tf_op jit(solution)/shard_map/ppermute | solution.py:177
  74.6 2.6 %chunk_product.5.rest_0_ = bf16[2048,1024]{1,0:T(8,128)(2,1)} custom-call(bf16[6,256,256]{2,1,0:T(8,128)(2,1)S(1)} %constant_dynamic-update-slice_fusion.own_ref, bf16[6,256,256]{2,1,0:T(8,128)(2,1)S(1)} %collective-permute-done.7.one_ref, bf16[3,256,256]{2,1,0:T(8,128)(2,1)S(1)} %collective-permute-done.15.two_ref, ...), custom_call_target="tpu_custom_call", output_to_operand_aliasing={{}: (5, {})} | custom-call | flops 1610612736 | bytes 4194304 | tf_op jit(solution)/shard_map/chunk_product/pallas_call | solution.py:152
  77.2 3.0 %collective-permute-done.14.two_ref = bf16[2,256,256]{2,1,0:T(8,128)(2,1)S(1)} collective-permute-done((bf16[2,256,256]{2,1,0:T(8,128)(2,1)S(1)}, bf16[2,256,256]{2,1,0:T(8,128)(2,1)S(1)}, u32[]{:S(2)}, u32[]{:S(2)}) %collective-permute-start.14) | collective-permute-done | bytes 262176 | tf_op jit(solution)/shard_map/ppermute | solution.py:177
  80.2 2.1 %chunk_product.6.rest_0_ = bf16[2048,1024]{1,0:T(8,128)(2,1)} custom-call(bf16[6,256,256]{2,1,0:T(8,128)(2,1)S(1)} %constant_dynamic-update-slice_fusion.own_ref, bf16[6,256,256]{2,1,0:T(8,128)(2,1)S(1)} %collective-permute-done.7.one_ref, bf16[2,256,256]{2,1,0:T(8,128)(2,1)S(1)} %collective-permute-done.14.two_ref, ...), custom_call_target="tpu_custom_call", output_to_operand_aliasing={{}: (5, {})} | custom-call | flops 1073741824 | bytes 4194304 | tf_op jit(solution)/shard_map/chunk_product/pallas_call | solution.py:152
  82.3 0.0 collective-permute-done.9.two_ref
  82.3 1.5 %chunk_product.7 = bf16[2048,1024]{1,0:T(8,128)(2,1)} custom-call(bf16[6,256,256]{2,1,0:T(8,128)(2,1)S(1)} %constant_dynamic-update-slice_fusion.own_ref, bf16[6,256,256]{2,1,0:T(8,128)(2,1)S(1)} %collective-permute-done.7.one_ref, bf16[1,256,256]{2,1,0:T(8,128)(2,1)S(1)} %collective-permute-done.9.two_ref, ...), custom_call_target="tpu_custom_call", output_to_operand_aliasing={{}: (5, {})} | custom-call | flops 536870912 | bytes 4194304 | tf_op jit(solution)/shard_map/chunk_product/pallas_call | solution.py:152
  (8 shorter events, 0.1 us)
Async XLA Ops:
  1.6 2.1 %collective-permute-start = (bf16[4,256,256]{2,1,0:T(8,128)(2,1)S(1)}, bf16[4,256,256]{2,1,0:T(8,128)(2,1)S(1)}, u32[]{:S(2)}, u32[]{:S(2)}) collective-permute-start(bf16[4,256,256]{2,1,0:T(8,128)(2,1)S(1)} %get-tuple-element.23), channel_id=1, source_target_pairs={{0,4},{4,0},{8,12},{12,8},{16,20},{20,16},{24,28},{28,24},{1,5},{5... | collective-permute-start | bytes 1572872 | tf_op jit(solution)/shard_map/ppermute | solution.py:173
  3.7 12.2 %collective-permute-start.5 = (bf16[2,256,256]{2,1,0:T(8,128)(2,1)S(1)}, bf16[2,256,256]{2,1,0:T(8,128)(2,1)S(1)}, u32[]{:S(2)}, u32[]{:S(2)}) collective-permute-start(bf16[2,256,256]{2,1,0:T(8,128)(2,1)S(1)} %slice_dynamic-update-slice_fusion.own_ref), channel_id=1, source_target_pairs={{0,3},{3,0},{1,2},{2,1},{4,7},{7,4},{5,6},{6,5},{8,11},{11,8},{9,1... | collective-permute-start | bytes 786440 | tf_op jit(solution)/shard_map/ppermute | solution.py:177
  8.7 14.8 %collective-permute-start.4 = (bf16[2,256,256]{2,1,0:T(8,128)(2,1)S(1)}, bf16[2,256,256]{2,1,0:T(8,128)(2,1)S(1)}, u32[]{:S(2)}, u32[]{:S(2)}) collective-permute-start(bf16[2,256,256]{2,1,0:T(8,128)(2,1)S(1)} %slice_dynamic-update-slice_fusion.own_ref), channel_id=1, source_target_pairs={{0,1},{1,0},{2,3},{3,2},{4,5},{5,4},{6,7},{7,6},{8,9},{9,8},{10,11... | collective-permute-start | bytes 786440 | tf_op jit(solution)/shard_map/ppermute | solution.py:177
  8.7 13.0 %collective-permute-start.3 = (bf16[2,256,256]{2,1,0:T(8,128)(2,1)S(1)}, bf16[2,256,256]{2,1,0:T(8,128)(2,1)S(1)}, u32[]{:S(2)}, u32[]{:S(2)}) collective-permute-start(bf16[2,256,256]{2,1,0:T(8,128)(2,1)S(1)} %get-tuple-element.39), channel_id=1, source_target_pairs={{0,24},{4,28},{8,16},{12,20},{16,8},{20,12},{24,0},{28,4},{1,25},{... | collective-permute-start | bytes 786440 | tf_op jit(solution)/shard_map/ppermute | solution.py:173
  11.3 12.1 %collective-permute-start.2 = (bf16[2,256,256]{2,1,0:T(8,128)(2,1)S(1)}, bf16[2,256,256]{2,1,0:T(8,128)(2,1)S(1)}, u32[]{:S(2)}, u32[]{:S(2)}) collective-permute-start(bf16[2,256,256]{2,1,0:T(8,128)(2,1)S(1)} %get-tuple-element.40), channel_id=1, source_target_pairs={{0,16},{4,20},{8,24},{12,28},{16,0},{20,4},{24,8},{28,12},{1,17},{... | collective-permute-start | bytes 786440 | tf_op jit(solution)/shard_map/ppermute | solution.py:173
  11.8 11.7 %collective-permute-start.1 = (bf16[2,256,256]{2,1,0:T(8,128)(2,1)S(1)}, bf16[2,256,256]{2,1,0:T(8,128)(2,1)S(1)}, u32[]{:S(2)}, u32[]{:S(2)}) collective-permute-start(bf16[2,256,256]{2,1,0:T(8,128)(2,1)S(1)} %get-tuple-element.41), channel_id=1, source_target_pairs={{0,8},{4,12},{8,0},{12,4},{16,24},{20,28},{24,16},{28,20},{1,9},{5... | collective-permute-start | bytes 786440 | tf_op jit(solution)/shard_map/ppermute | solution.py:173
  15.9 10.9 %collective-permute-start.6 = (bf16[2,256,256]{2,1,0:T(8,128)(2,1)S(1)}, bf16[2,256,256]{2,1,0:T(8,128)(2,1)S(1)}, u32[]{:S(2)}, u32[]{:S(2)}) collective-permute-start(bf16[2,256,256]{2,1,0:T(8,128)(2,1)S(1)} %passed.2), channel_id=1, source_target_pairs={{2,3},{1,0},{0,2},{3,1},{6,7},{5,4},{4,6},{7,5},{10,11},{9,8},{8,1... | collective-permute-start | bytes 786440 | tf_op jit(solution)/shard_map/ppermute | solution.py:177
  26.9 22.4 %collective-permute-start.8 = (bf16[6,256,256]{2,1,0:T(8,128)(2,1)S(1)}, bf16[6,256,256]{2,1,0:T(8,128)(2,1)S(1)}, u32[]{:S(2)}, u32[]{:S(2)}) collective-permute-start(bf16[6,256,256]{2,1,0:T(8,128)(2,1)S(1)} %constant_dynamic-update-slice_fusion.own_ref), channel_id=1, source_target_pairs={{0,3},{3,0},{1,2},{2,1},{4,7},{7,4},{5,6},{6,5},{8,11},{11,8},{9,1... | collective-permute-start | bytes 2359304 | tf_op jit(solution)/shard_map/ppermute | solution.py:177
  29.1 1.8 %collective-permute-start.10 = (bf16[2,256,256]{2,1,0:T(8,128)(2,1)S(1)}, bf16[2,256,256]{2,1,0:T(8,128)(2,1)S(1)}, u32[]{:S(2)}, u32[]{:S(2)}) collective-permute-start(bf16[2,256,256]{2,1,0:T(8,128)(2,1)S(1)} %get-tuple-element.33), channel_id=1, source_target_pairs={{0,4},{4,0},{8,12},{12,8},{16,20},{20,16},{24,28},{28,24},{1,5},{5... | collective-permute-start | bytes 786440 | tf_op jit(solution)/shard_map/ppermute | solution.py:173
  29.1 37.9 %collective-permute-start.7 = (bf16[6,256,256]{2,1,0:T(8,128)(2,1)S(1)}, bf16[6,256,256]{2,1,0:T(8,128)(2,1)S(1)}, u32[]{:S(2)}, u32[]{:S(2)}) collective-permute-start(bf16[6,256,256]{2,1,0:T(8,128)(2,1)S(1)} %constant_dynamic-update-slice_fusion.own_ref), channel_id=1, source_target_pairs={{0,1},{1,0},{2,3},{3,2},{4,5},{5,4},{6,7},{7,6},{8,9},{9,8},{10,11... | collective-permute-start | bytes 2359304 | tf_op jit(solution)/shard_map/ppermute | solution.py:177
  30.9 34.2 %collective-permute-start.13 = (bf16[4,256,256]{2,1,0:T(8,128)(2,1)S(1)}, bf16[4,256,256]{2,1,0:T(8,128)(2,1)S(1)}, u32[]{:S(2)}, u32[]{:S(2)}) collective-permute-start(bf16[4,256,256]{2,1,0:T(8,128)(2,1)S(1)} %constant_dynamic-update-slice_fusion.3.refs_0_), channel_id=1, source_target_pairs={{0,24},{4,28},{8,16},{12,20},{16,8},{20,12},{24,0},{28,4},{1,25},{... | collective-permute-start | bytes 1572872 | tf_op jit(solution)/shard_map/ppermute | solution.py:173
  33.4 31.7 %collective-permute-start.12 = (bf16[4,256,256]{2,1,0:T(8,128)(2,1)S(1)}, bf16[4,256,256]{2,1,0:T(8,128)(2,1)S(1)}, u32[]{:S(2)}, u32[]{:S(2)}) collective-permute-start(bf16[4,256,256]{2,1,0:T(8,128)(2,1)S(1)} %constant_dynamic-update-slice_fusion.3.refs_0_), channel_id=1, source_target_pairs={{0,16},{4,20},{8,24},{12,28},{16,0},{20,4},{24,8},{28,12},{1,17},{... | collective-permute-start | bytes 1572872 | tf_op jit(solution)/shard_map/ppermute | solution.py:173
  33.9 33.1 %collective-permute-start.11 = (bf16[4,256,256]{2,1,0:T(8,128)(2,1)S(1)}, bf16[4,256,256]{2,1,0:T(8,128)(2,1)S(1)}, u32[]{:S(2)}, u32[]{:S(2)}) collective-permute-start(bf16[4,256,256]{2,1,0:T(8,128)(2,1)S(1)} %constant_dynamic-update-slice_fusion.3.refs_0_), channel_id=1, source_target_pairs={{0,8},{4,12},{8,0},{12,4},{16,24},{20,28},{24,16},{28,20},{1,9},{5... | collective-permute-start | bytes 1572872 | tf_op jit(solution)/shard_map/ppermute | solution.py:173
  49.3 25.3 %collective-permute-start.15 = (bf16[3,256,256]{2,1,0:T(8,128)(2,1)S(1)}, bf16[3,256,256]{2,1,0:T(8,128)(2,1)S(1)}, u32[]{:S(2)}, u32[]{:S(2)}) collective-permute-start(bf16[3,256,256]{2,1,0:T(8,128)(2,1)S(1)} %get-tuple-element.34), channel_id=1, source_target_pairs={{2,3},{1,0},{0,2},{3,1},{6,7},{5,4},{4,6},{7,5},{10,11},{9,8},{8,1... | collective-permute-start | bytes 1179656 | tf_op jit(solution)/shard_map/ppermute | solution.py:177
  65.1 15.1 %collective-permute-start.14 = (bf16[2,256,256]{2,1,0:T(8,128)(2,1)S(1)}, bf16[2,256,256]{2,1,0:T(8,128)(2,1)S(1)}, u32[]{:S(2)}, u32[]{:S(2)}) collective-permute-start(bf16[2,256,256]{2,1,0:T(8,128)(2,1)S(1)} %get-tuple-element.35), channel_id=1, source_target_pairs={{2,3},{1,0},{0,2},{3,1},{6,7},{5,4},{4,6},{7,5},{10,11},{9,8},{8,1... | collective-permute-start | bytes 786440 | tf_op jit(solution)/shard_map/ppermute | solution.py:177
  65.2 17.1 %collective-permute-start.9 = (bf16[1,256,256]{2,1,0:T(8,128)(2,1)S(1)}, bf16[1,256,256]{2,1,0:T(8,128)(2,1)S(1)}, u32[]{:S(2)}, u32[]{:S(2)}) collective-permute-start(bf16[1,256,256]{2,1,0:T(8,128)(2,1)S(1)} %get-tuple-element.31), channel_id=1, source_target_pairs={{2,3},{1,0},{0,2},{3,1},{6,7},{5,4},{4,6},{7,5},{10,11},{9,8},{8,1... | collective-permute-start | bytes 393224 | tf_op jit(solution)/shard_map/ppermute | solution.py:177

commit v6 on v5

--- a/solution.py
+++ b/solution.py
@@ -120,20 +120,25 @@
     blocks, height, depth = two_ref.shape
     me, col = lax.axis_index("row"), lax.axis_index("col")
     copies = []
+    half = b_ref.shape[1] // 2
     for i in range(blocks):
-        total = None
         terms = (own_ref[at + i], one_ref[at + i], two_ref[i], three_ref[at + i])
-        for far, block in enumerate(terms):
-            rows = pl.ds(pl.multiple_of((col ^ far) * depth, depth), depth)
-            term = jnp.dot(block, b_ref[rows, :], preferred_element_type=jnp.float32)
-            total = term if total is None else total + term
-        done[i] = total.astype(done.dtype)
         start = pl.multiple_of((me ^ (first + i)) * height, height)
-        copy = pltpu.make_async_copy(
-            done.at[i], out_ref.at[pl.ds(start, height), :], sems.at[i]
-        )
-        copy.start()
-        copies.append(copy)
+        for side in range(2):
+            part = slice(side * half, (side + 1) * half)
+            total = None
+            for far, block in enumerate(terms):
+                rows = pl.ds(pl.multiple_of((col ^ far) * depth, depth), depth)
+                term = jnp.dot(block, b_ref[rows, part], preferred_element_type=jnp.float32)
+                total = term if total is None else total + term
+            done[i, :, part] = total.astype(done.dtype)
+            copy = pltpu.make_async_copy(
+                done.at[i, :, part],
+                out_ref.at[pl.ds(start, height), part],
+                sems.at[2 * i + side],
+            )
+            copy.start()
+            copies.append(copy)
     for copy in copies:
         copy.wait()
 
@@ -156,7 +161,7 @@
         out_specs=ANY,
         scratch_shapes=[
             pltpu.VMEM((blocks, height, cols), jnp.bfloat16),
-            pltpu.SemaphoreType.DMA((blocks,)),
+            pltpu.SemaphoreType.DMA((2 * blocks,)),
         ],
         input_output_aliases=aliases,
         compiler_params=pltpu.CompilerParams(vmem_limit_bytes=24 << 20),

time: 84 us -> 83.8 us (level)
  no operation moved by 1% of the time
where the time goes in v6:
time: 83.8 us; the launch traced here: 83.7 us
  starting transfers between devices  40.2 us (48%)
  waiting for transfers between devices  33.3 us (40%)
  Pallas kernels  9.87 us (12%)
    ppermute x8, starting transfers between devices, by_col(): return lax.ppermute(value, 'col', pairs)  32.6 us
    ppermute x8, waiting for transfers between devices, by_col(): return lax.ppermute(value, 'col', pairs)  30 us
    pallas_call x4, Pallas kernels, chunk_product(): pl.pallas_call(functools.partial(dot_kernel, first, at), out_shape=jax.Sh...  7.98 us
    ppermute x8, starting transfers between devices, by_row(): return lax.ppermute(value, 'row', [(i, i ^ distance) for i in range(8)])  7.63 us
    ppermute x8, waiting for transfers between devices, by_row(): return lax.ppermute(value, 'row', [(i, i ^ distance) for i in range(8)])  3.3 us
  transfers between devices with their start and end apart: 16, of which 8 were waited for; matrix products, arithmetic and copies ran while one was open for 0% of the time, Pallas kernels for 8%

profile of v6, /device:TPU:0, one launch (start us, length us, event | category | flops | bytes accessed | tf_op | source)
XLA Modules:
  0.0 83.7 jit_solution(3466430944974858022)
XLA Ops:
  0.0 1.6 %pack.1 = (bf16[2,256,256]{2,1,0:T(8,128)(2,1)S(1)}, bf16[2,256,256]{2,1,0:T(8,128)(2,1)S(1)}, bf16[2,256,256]{2,1,0:T(8,128)(2,1)S(1)}, bf16[2,256,256]{2,1,0:T...) custom-call(s32[1,16]{1,0:T(1,128)} %bitcast.3, s32[2,16]{1,0:T(2,128)} %bitcast.2, ...), custom_call_target="tpu_custom_call" | custom-call | tf_op jit(solution)/shard_map/pack/pallas_call | solution.py:99
  1.6 0.5 collective-permute-start
  2.1 1.5 %collective-permute-done = bf16[4,256,256]{2,1,0:T(8,128)(2,1)S(1)} collective-permute-done((bf16[4,256,256]{2,1,0:T(8,128)(2,1)S(1)}, bf16[4,256,256]{2,1,0:T(8,128)(2,1)S(1)}, u32[]{:S(2)}, u32[]{:S(2)}) %collective-permute-start) | collective-permute-done | bytes 524320 | tf_op jit(solution)/shard_map/ppermute | solution.py:178
  3.7 5.0 %collective-permute-start.5 = (bf16[2,256,256]{2,1,0:T(8,128)(2,1)S(1)}, bf16[2,256,256]{2,1,0:T(8,128)(2,1)S(1)}, u32[]{:S(2)}, u32[]{:S(2)}) collective-permute-start(bf16[2,256,256]{2,1,0:T(8,128)(2,1)S(1)} %slice_dynamic-update-slice_fusion.own_ref), channel_id=1, source_target_pairs={{0,3},{3,0},{1,2},{2,1},{4,7},{7,4},{5,6},{6,5},{8,11},{11,8},{9,1... | collective-permute-start | bytes 786440 | tf_op jit(solution)/shard_map/ppermute | solution.py:182
  8.7 0.0 collective-permute-start.4
  8.7 2.5 %collective-permute-start.3 = (bf16[2,256,256]{2,1,0:T(8,128)(2,1)S(1)}, bf16[2,256,256]{2,1,0:T(8,128)(2,1)S(1)}, u32[]{:S(2)}, u32[]{:S(2)}) collective-permute-start(bf16[2,256,256]{2,1,0:T(8,128)(2,1)S(1)} %get-tuple-element.39), channel_id=1, source_target_pairs={{0,24},{4,28},{8,16},{12,20},{16,8},{20,12},{24,0},{28,4},{1,25},{... | collective-permute-start | bytes 786440 | tf_op jit(solution)/shard_map/ppermute | solution.py:178
  11.3 0.5 collective-permute-start.2
  11.8 0.5 collective-permute-start.1
  12.3 3.6 %collective-permute-done.5.three_ref = bf16[2,256,256]{2,1,0:T(8,128)(2,1)S(1)} collective-permute-done((bf16[2,256,256]{2,1,0:T(8,128)(2,1)S(1)}, bf16[2,256,256]{2,1,0:T(8,128)(2,1)S(1)}, u32[]{:S(2)}, u32[]{:S(2)}) %collective-permute-start.5) | collective-permute-done | bytes 262176 | tf_op jit(solution)/shard_map/ppermute | solution.py:182
  15.9 5.8 %collective-permute-start.6 = (bf16[2,256,256]{2,1,0:T(8,128)(2,1)S(1)}, bf16[2,256,256]{2,1,0:T(8,128)(2,1)S(1)}, u32[]{:S(2)}, u32[]{:S(2)}) collective-permute-start(bf16[2,256,256]{2,1,0:T(8,128)(2,1)S(1)} %passed.2), channel_id=1, source_target_pairs={{2,3},{1,0},{0,2},{3,1},{6,7},{5,4},{4,6},{7,5},{10,11},{9,8},{8,1... | collective-permute-start | bytes 786440 | tf_op jit(solution)/shard_map/ppermute | solution.py:182
  21.7 0.0 collective-permute-done.3
  21.7 1.6 %collective-permute-done.2 = bf16[2,256,256]{2,1,0:T(8,128)(2,1)S(1)} collective-permute-done((bf16[2,256,256]{2,1,0:T(8,128)(2,1)S(1)}, bf16[2,256,256]{2,1,0:T(8,128)(2,1)S(1)}, u32[]{:S(2)}, u32[]{:S(2)}) %collective-permute-start.2) | collective-permute-done | bytes 262176 | tf_op jit(solution)/shard_map/ppermute | solution.py:178
  23.4 0.1 collective-permute-done.1
  23.5 0.0 collective-permute-done.4.one_ref
  23.5 3.3 %collective-permute-done.6.two_ref = bf16[2,256,256]{2,1,0:T(8,128)(2,1)S(1)} collective-permute-done((bf16[2,256,256]{2,1,0:T(8,128)(2,1)S(1)}, bf16[2,256,256]{2,1,0:T(8,128)(2,1)S(1)}, u32[]{:S(2)}, u32[]{:S(2)}) %collective-permute-start.6) | collective-permute-done | bytes 262176 | tf_op jit(solution)/shard_map/ppermute | solution.py:182
  26.9 2.3 %collective-permute-start.8 = (bf16[6,256,256]{2,1,0:T(8,128)(2,1)S(1)}, bf16[6,256,256]{2,1,0:T(8,128)(2,1)S(1)}, u32[]{:S(2)}, u32[]{:S(2)}) collective-permute-start(bf16[6,256,256]{2,1,0:T(8,128)(2,1)S(1)} %constant_dynamic-update-slice_fusion.own_ref), channel_id=1, source_target_pairs={{0,3},{3,0},{1,2},{2,1},{4,7},{7,4},{5,6},{6,5},{8,11},{11,8},{9,1... | collective-permute-start | bytes 2359304 | tf_op jit(solution)/shard_map/ppermute | solution.py:182
  29.1 0.0 collective-permute-start.10
  29.1 1.7 %collective-permute-start.7 = (bf16[6,256,256]{2,1,0:T(8,128)(2,1)S(1)}, bf16[6,256,256]{2,1,0:T(8,128)(2,1)S(1)}, u32[]{:S(2)}, u32[]{:S(2)}) collective-permute-start(bf16[6,256,256]{2,1,0:T(8,128)(2,1)S(1)} %constant_dynamic-update-slice_fusion.own_ref), channel_id=1, source_target_pairs={{0,1},{1,0},{2,3},{3,2},{4,5},{5,4},{6,7},{7,6},{8,9},{9,8},{10,11... | collective-permute-start | bytes 2359304 | tf_op jit(solution)/shard_map/ppermute | solution.py:182
  30.9 0.0 collective-permute-done.10
  30.9 2.5 %collective-permute-start.13 = (bf16[4,256,256]{2,1,0:T(8,128)(2,1)S(1)}, bf16[4,256,256]{2,1,0:T(8,128)(2,1)S(1)}, u32[]{:S(2)}, u32[]{:S(2)}) collective-permute-start(bf16[4,256,256]{2,1,0:T(8,128)(2,1)S(1)} %constant_dynamic-update-slice_fusion.3.refs_0_), channel_id=1, source_target_pairs={{0,24},{4,28},{8,16},{12,20},{16,8},{20,12},{24,0},{28,4},{1,25},{... | collective-permute-start | bytes 1572872 | tf_op jit(solution)/shard_map/ppermute | solution.py:178
  33.4 0.5 collective-permute-start.12
  33.9 0.5 collective-permute-start.11
  34.5 14.8 %collective-permute-done.8.three_ref = bf16[6,256,256]{2,1,0:T(8,128)(2,1)S(1)} collective-permute-done((bf16[6,256,256]{2,1,0:T(8,128)(2,1)S(1)}, bf16[6,256,256]{2,1,0:T(8,128)(2,1)S(1)}, u32[]{:S(2)}, u32[]{:S(2)}) %collective-permute-start.8) | collective-permute-done | bytes 786464 | tf_op jit(solution)/shard_map/ppermute | solution.py:182
  49.2 0.1 passed.3
  49.3 15.8 %collective-permute-start.15 = (bf16[3,256,256]{2,1,0:T(8,128)(2,1)S(1)}, bf16[3,256,256]{2,1,0:T(8,128)(2,1)S(1)}, u32[]{:S(2)}, u32[]{:S(2)}) collective-permute-start(bf16[3,256,256]{2,1,0:T(8,128)(2,1)S(1)} %get-tuple-element.34), channel_id=1, source_target_pairs={{2,3},{1,0},{0,2},{3,1},{6,7},{5,4},{4,6},{7,5},{10,11},{9,8},{8,1... | collective-permute-start | bytes 1179656 | tf_op jit(solution)/shard_map/ppermute | solution.py:182
  65.1 0.0 collective-permute-done.13.refs_3_
  65.1 0.1 collective-permute-start.14
  65.2 0.0 collective-permute-done.12.refs_2_
  65.2 1.8 %collective-permute-start.9 = (bf16[1,256,256]{2,1,0:T(8,128)(2,1)S(1)}, bf16[1,256,256]{2,1,0:T(8,128)(2,1)S(1)}, u32[]{:S(2)}, u32[]{:S(2)}) collective-permute-start(bf16[1,256,256]{2,1,0:T(8,128)(2,1)S(1)} %get-tuple-element.31), channel_id=1, source_target_pairs={{2,3},{1,0},{0,2},{3,1},{6,7},{5,4},{4,6},{7,5},{10,11},{9,8},{8,1... | collective-permute-start | bytes 393224 | tf_op jit(solution)/shard_map/ppermute | solution.py:182
  67.0 0.0 collective-permute-done.11.refs_1_
  67.0 0.0 collective-permute-done.7.one_ref
  67.0 0.2 order_b.1.b_ref
  67.3 2.0 %chunk_product.4.rest_0_ = bf16[2048,1024]{1,0:T(8,128)(2,1)} custom-call(bf16[2,256,256]{2,1,0:T(8,128)(2,1)S(1)} %slice_dynamic-update-slice_fusion.own_ref, bf16[2,256,256]{2,1,0:T(8,128)(2,1)S(1)} %collective-permute-done.4.one_ref, bf16[2,256,256]{2,1,0:T(8,128)(2,1)S(1)} %collective-permute-done.6.two_ref, ...), custom_call_target="tpu_custom_call" | custom-call | flops 1073741824 | bytes 4194304 | tf_op jit(solution)/shard_map/chunk_product/pallas_call | solution.py:157
  69.3 5.3 %collective-permute-done.15.two_ref = bf16[3,256,256]{2,1,0:T(8,128)(2,1)S(1)} collective-permute-done((bf16[3,256,256]{2,1,0:T(8,128)(2,1)S(1)}, bf16[3,256,256]{2,1,0:T(8,128)(2,1)S(1)}, u32[]{:S(2)}, u32[]{:S(2)}) %collective-permute-start.15) | collective-permute-done | bytes 393248 | tf_op jit(solution)/shard_map/ppermute | solution.py:182
  74.6 2.5 %chunk_product.5.rest_0_ = bf16[2048,1024]{1,0:T(8,128)(2,1)} custom-call(bf16[6,256,256]{2,1,0:T(8,128)(2,1)S(1)} %constant_dynamic-update-slice_fusion.own_ref, bf16[6,256,256]{2,1,0:T(8,128)(2,1)S(1)} %collective-permute-done.7.one_ref, bf16[3,256,256]{2,1,0:T(8,128)(2,1)S(1)} %collective-permute-done.15.two_ref, ...), custom_call_target="tpu_custom_call", output_to_operand_aliasing={{}: (5, {})} | custom-call | flops 1610612736 | bytes 4194304 | tf_op jit(solution)/shard_map/chunk_product/pallas_call | solution.py:157
  77.2 3.1 %collective-permute-done.14.two_ref = bf16[2,256,256]{2,1,0:T(8,128)(2,1)S(1)} collective-permute-done((bf16[2,256,256]{2,1,0:T(8,128)(2,1)S(1)}, bf16[2,256,256]{2,1,0:T(8,128)(2,1)S(1)}, u32[]{:S(2)}, u32[]{:S(2)}) %collective-permute-start.14) | collective-permute-done | bytes 262176 | tf_op jit(solution)/shard_map/ppermute | solution.py:182
  80.2 2.0 %chunk_product.6.rest_0_ = bf16[2048,1024]{1,0:T(8,128)(2,1)} custom-call(bf16[6,256,256]{2,1,0:T(8,128)(2,1)S(1)} %constant_dynamic-update-slice_fusion.own_ref, bf16[6,256,256]{2,1,0:T(8,128)(2,1)S(1)} %collective-permute-done.7.one_ref, bf16[2,256,256]{2,1,0:T(8,128)(2,1)S(1)} %collective-permute-done.14.two_ref, ...), custom_call_target="tpu_custom_call", output_to_operand_aliasing={{}: (5, {})} | custom-call | flops 1073741824 | bytes 4194304 | tf_op jit(solution)/shard_map/chunk_product/pallas_call | solution.py:157
  82.2 0.0 collective-permute-done.9.two_ref
  82.2 1.4 %chunk_product.7 = bf16[2048,1024]{1,0:T(8,128)(2,1)} custom-call(bf16[6,256,256]{2,1,0:T(8,128)(2,1)S(1)} %constant_dynamic-update-slice_fusion.own_ref, bf16[6,256,256]{2,1,0:T(8,128)(2,1)S(1)} %collective-permute-done.7.one_ref, bf16[1,256,256]{2,1,0:T(8,128)(2,1)S(1)} %collective-permute-done.9.two_ref, ...), custom_call_target="tpu_custom_call", output_to_operand_aliasing={{}: (5, {})} | custom-call | flops 536870912 | bytes 4194304 | tf_op jit(solution)/shard_map/chunk_product/pallas_call | solution.py:157
  (8 shorter events, 0.1 us)
Async XLA Ops:
  1.6 2.1 %collective-permute-start = (bf16[4,256,256]{2,1,0:T(8,128)(2,1)S(1)}, bf16[4,256,256]{2,1,0:T(8,128)(2,1)S(1)}, u32[]{:S(2)}, u32[]{:S(2)}) collective-permute-start(bf16[4,256,256]{2,1,0:T(8,128)(2,1)S(1)} %get-tuple-element.23), channel_id=1, source_target_pairs={{0,4},{4,0},{8,12},{12,8},{16,20},{20,16},{24,28},{28,24},{1,5},{5... | collective-permute-start | bytes 1572872 | tf_op jit(solution)/shard_map/ppermute | solution.py:178
  3.7 12.2 %collective-permute-start.5 = (bf16[2,256,256]{2,1,0:T(8,128)(2,1)S(1)}, bf16[2,256,256]{2,1,0:T(8,128)(2,1)S(1)}, u32[]{:S(2)}, u32[]{:S(2)}) collective-permute-start(bf16[2,256,256]{2,1,0:T(8,128)(2,1)S(1)} %slice_dynamic-update-slice_fusion.own_ref), channel_id=1, source_target_pairs={{0,3},{3,0},{1,2},{2,1},{4,7},{7,4},{5,6},{6,5},{8,11},{11,8},{9,1... | collective-permute-start | bytes 786440 | tf_op jit(solution)/shard_map/ppermute | solution.py:182
  8.7 14.8 %collective-permute-start.4 = (bf16[2,256,256]{2,1,0:T(8,128)(2,1)S(1)}, bf16[2,256,256]{2,1,0:T(8,128)(2,1)S(1)}, u32[]{:S(2)}, u32[]{:S(2)}) collective-permute-start(bf16[2,256,256]{2,1,0:T(8,128)(2,1)S(1)} %slice_dynamic-update-slice_fusion.own_ref), channel_id=1, source_target_pairs={{0,1},{1,0},{2,3},{3,2},{4,5},{5,4},{6,7},{7,6},{8,9},{9,8},{10,11... | collective-permute-start | bytes 786440 | tf_op jit(solution)/shard_map/ppermute | solution.py:182
  8.7 13.0 %collective-permute-start.3 = (bf16[2,256,256]{2,1,0:T(8,128)(2,1)S(1)}, bf16[2,256,256]{2,1,0:T(8,128)(2,1)S(1)}, u32[]{:S(2)}, u32[]{:S(2)}) collective-permute-start(bf16[2,256,256]{2,1,0:T(8,128)(2,1)S(1)} %get-tuple-element.39), channel_id=1, source_target_pairs={{0,24},{4,28},{8,16},{12,20},{16,8},{20,12},{24,0},{28,4},{1,25},{... | collective-permute-start | bytes 786440 | tf_op jit(solution)/shard_map/ppermute | solution.py:178
  11.3 12.1 %collective-permute-start.2 = (bf16[2,256,256]{2,1,0:T(8,128)(2,1)S(1)}, bf16[2,256,256]{2,1,0:T(8,128)(2,1)S(1)}, u32[]{:S(2)}, u32[]{:S(2)}) collective-permute-start(bf16[2,256,256]{2,1,0:T(8,128)(2,1)S(1)} %get-tuple-element.40), channel_id=1, source_target_pairs={{0,16},{4,20},{8,24},{12,28},{16,0},{20,4},{24,8},{28,12},{1,17},{... | collective-permute-start | bytes 786440 | tf_op jit(solution)/shard_map/ppermute | solution.py:178
  11.8 11.7 %collective-permute-start.1 = (bf16[2,256,256]{2,1,0:T(8,128)(2,1)S(1)}, bf16[2,256,256]{2,1,0:T(8,128)(2,1)S(1)}, u32[]{:S(2)}, u32[]{:S(2)}) collective-permute-start(bf16[2,256,256]{2,1,0:T(8,128)(2,1)S(1)} %get-tuple-element.41), channel_id=1, source_target_pairs={{0,8},{4,12},{8,0},{12,4},{16,24},{20,28},{24,16},{28,20},{1,9},{5... | collective-permute-start | bytes 786440 | tf_op jit(solution)/shard_map/ppermute | solution.py:178
  15.9 10.9 %collective-permute-start.6 = (bf16[2,256,256]{2,1,0:T(8,128)(2,1)S(1)}, bf16[2,256,256]{2,1,0:T(8,128)(2,1)S(1)}, u32[]{:S(2)}, u32[]{:S(2)}) collective-permute-start(bf16[2,256,256]{2,1,0:T(8,128)(2,1)S(1)} %passed.2), channel_id=1, source_target_pairs={{2,3},{1,0},{0,2},{3,1},{6,7},{5,4},{4,6},{7,5},{10,11},{9,8},{8,1... | collective-permute-start | bytes 786440 | tf_op jit(solution)/shard_map/ppermute | solution.py:182
  26.9 22.4 %collective-permute-start.8 = (bf16[6,256,256]{2,1,0:T(8,128)(2,1)S(1)}, bf16[6,256,256]{2,1,0:T(8,128)(2,1)S(1)}, u32[]{:S(2)}, u32[]{:S(2)}) collective-permute-start(bf16[6,256,256]{2,1,0:T(8,128)(2,1)S(1)} %constant_dynamic-update-slice_fusion.own_ref), channel_id=1, source_target_pairs={{0,3},{3,0},{1,2},{2,1},{4,7},{7,4},{5,6},{6,5},{8,11},{11,8},{9,1... | collective-permute-start | bytes 2359304 | tf_op jit(solution)/shard_map/ppermute | solution.py:182
  29.1 1.8 %collective-permute-start.10 = (bf16[2,256,256]{2,1,0:T(8,128)(2,1)S(1)}, bf16[2,256,256]{2,1,0:T(8,128)(2,1)S(1)}, u32[]{:S(2)}, u32[]{:S(2)}) collective-permute-start(bf16[2,256,256]{2,1,0:T(8,128)(2,1)S(1)} %get-tuple-element.33), channel_id=1, source_target_pairs={{0,4},{4,0},{8,12},{12,8},{16,20},{20,16},{24,28},{28,24},{1,5},{5... | collective-permute-start | bytes 786440 | tf_op jit(solution)/shard_map/ppermute | solution.py:178
  29.1 37.9 %collective-permute-start.7 = (bf16[6,256,256]{2,1,0:T(8,128)(2,1)S(1)}, bf16[6,256,256]{2,1,0:T(8,128)(2,1)S(1)}, u32[]{:S(2)}, u32[]{:S(2)}) collective-permute-start(bf16[6,256,256]{2,1,0:T(8,128)(2,1)S(1)} %constant_dynamic-update-slice_fusion.own_ref), channel_id=1, source_target_pairs={{0,1},{1,0},{2,3},{3,2},{4,5},{5,4},{6,7},{7,6},{8,9},{9,8},{10,11... | collective-permute-start | bytes 2359304 | tf_op jit(solution)/shard_map/ppermute | solution.py:182
  30.9 34.2 %collective-permute-start.13 = (bf16[4,256,256]{2,1,0:T(8,128)(2,1)S(1)}, bf16[4,256,256]{2,1,0:T(8,128)(2,1)S(1)}, u32[]{:S(2)}, u32[]{:S(2)}) collective-permute-start(bf16[4,256,256]{2,1,0:T(8,128)(2,1)S(1)} %constant_dynamic-update-slice_fusion.3.refs_0_), channel_id=1, source_target_pairs={{0,24},{4,28},{8,16},{12,20},{16,8},{20,12},{24,0},{28,4},{1,25},{... | collective-permute-start | bytes 1572872 | tf_op jit(solution)/shard_map/ppermute | solution.py:178
  33.4 31.7 %collective-permute-start.12 = (bf16[4,256,256]{2,1,0:T(8,128)(2,1)S(1)}, bf16[4,256,256]{2,1,0:T(8,128)(2,1)S(1)}, u32[]{:S(2)}, u32[]{:S(2)}) collective-permute-start(bf16[4,256,256]{2,1,0:T(8,128)(2,1)S(1)} %constant_dynamic-update-slice_fusion.3.refs_0_), channel_id=1, source_target_pairs={{0,16},{4,20},{8,24},{12,28},{16,0},{20,4},{24,8},{28,12},{1,17},{... | collective-permute-start | bytes 1572872 | tf_op jit(solution)/shard_map/ppermute | solution.py:178
  33.9 33.1 %collective-permute-start.11 = (bf16[4,256,256]{2,1,0:T(8,128)(2,1)S(1)}, bf16[4,256,256]{2,1,0:T(8,128)(2,1)S(1)}, u32[]{:S(2)}, u32[]{:S(2)}) collective-permute-start(bf16[4,256,256]{2,1,0:T(8,128)(2,1)S(1)} %constant_dynamic-update-slice_fusion.3.refs_0_), channel_id=1, source_target_pairs={{0,8},{4,12},{8,0},{12,4},{16,24},{20,28},{24,16},{28,20},{1,9},{5... | collective-permute-start | bytes 1572872 | tf_op jit(solution)/shard_map/ppermute | solution.py:178
  49.3 25.3 %collective-permute-start.15 = (bf16[3,256,256]{2,1,0:T(8,128)(2,1)S(1)}, bf16[3,256,256]{2,1,0:T(8,128)(2,1)S(1)}, u32[]{:S(2)}, u32[]{:S(2)}) collective-permute-start(bf16[3,256,256]{2,1,0:T(8,128)(2,1)S(1)} %get-tuple-element.34), channel_id=1, source_target_pairs={{2,3},{1,0},{0,2},{3,1},{6,7},{5,4},{4,6},{7,5},{10,11},{9,8},{8,1... | collective-permute-start | bytes 1179656 | tf_op jit(solution)/shard_map/ppermute | solution.py:182
  65.1 15.1 %collective-permute-start.14 = (bf16[2,256,256]{2,1,0:T(8,128)(2,1)S(1)}, bf16[2,256,256]{2,1,0:T(8,128)(2,1)S(1)}, u32[]{:S(2)}, u32[]{:S(2)}) collective-permute-start(bf16[2,256,256]{2,1,0:T(8,128)(2,1)S(1)} %get-tuple-element.35), channel_id=1, source_target_pairs={{2,3},{1,0},{0,2},{3,1},{6,7},{5,4},{4,6},{7,5},{10,11},{9,8},{8,1... | collective-permute-start | bytes 786440 | tf_op jit(solution)/shard_map/ppermute | solution.py:182
  65.2 17.0 %collective-permute-start.9 = (bf16[1,256,256]{2,1,0:T(8,128)(2,1)S(1)}, bf16[1,256,256]{2,1,0:T(8,128)(2,1)S(1)}, u32[]{:S(2)}, u32[]{:S(2)}) collective-permute-start(bf16[1,256,256]{2,1,0:T(8,128)(2,1)S(1)} %get-tuple-element.31), channel_id=1, source_target_pairs={{2,3},{1,0},{0,2},{3,1},{6,7},{5,4},{4,6},{7,5},{10,11},{9,8},{8,1... | collective-permute-start | bytes 393224 | tf_op jit(solution)/shard_map/ppermute | solution.py:182
